TPU v7x, 512 devices: a whole 4x8x8 slice. The times are simulated.
512 devices in a mesh: row: 32 (over x, y), col: 16 (over z, core).
Axes of the slice: x: 4, y: 8, z: 8, core: 2. Of those that a mesh axis runs over, the one named last changes fastest.
Arguments:
- right_sides: float32 [15, 512, 4096], P(None, 'row', 'col'), may hold values from -6 to 6
- diag_inverse: bfloat16 [15, 4096, 4096], P(None, 'row', 'col'), may hold values from -2 to 2, as said below
- panels: bfloat16 [14, 3, 4096, 4096], P(None, None, 'col', 'row'), may hold values from -0.046875 to 0.046875
- block_map: int32 [14, 16, 3], replicated, may hold values from 8 to 15, as said below
Outputs:
- solution: float32 [15, 512, 4096], P(None, 'col', 'row')
Inputs may be any that keep to these rules, and one draw needn't show every extreme that they name: `block_map`: entry [s, q, c] is an ancestor of supernode s, or 15, which marks an empty slot; the ancestors named in one [s, q] are distinct. Each diag_inverse[n] is lower triangular: entries whose column index exceeds the row index are zero.
All inputs are finite; a program needn't handle non-finite values.
Results may differ from a plain program's by a relative error of at most 0.028.
Values may be sent and summed in bfloat16 or wider, within the bound.
No kernel may reach another device: no remote copies, remote signals or barrier semaphores. Data moves between devices by JAX's collectives and lax.ppermute only.
A program may use at most 64 MiB of HBM per device.

v0:
```python
import jax
import jax.numpy as jnp
from jax import lax
from jax.sharding import PartitionSpec as P

LEV = 4
S = 15


def per_device(right_sides, diag_inverse, panels, block_map):
    col_index = lax.axis_index("col")
    share_cols = right_sides.shape[2]
    samples = right_sides.shape[1] * lax.axis_size("row")
    first_target = 2 ** (LEV - 1)
    pending = jnp.zeros((samples, S - first_target, share_cols), jnp.float32)
    own_blocks = lax.dynamic_slice_in_dim(block_map, col_index, 1, 1)[:, 0, :]
    results = []
    for level_index in range(LEV - 1, -1, -1):
        first_node = 2**LEV - 2 ** (level_index + 1)
        node_count = 2**level_index
        pending_first = first_node - first_target
        current = right_sides[first_node : first_node + node_count]
        if level_index < LEV - 1:
            summed_update = lax.psum_scatter(
                pending[:, pending_first : pending_first + node_count].astype(jnp.bfloat16),
                "row",
                scatter_dimension=0,
                tiled=True,
            ).astype(jnp.float32)
            current = current - jnp.swapaxes(summed_update, 0, 1)
        gathered = lax.all_gather(current.astype(jnp.bfloat16), "row", axis=1, tiled=True)
        inverse = diag_inverse[first_node : first_node + node_count]
        own_rows = lax.psum_scatter(
            jnp.einsum(
                "nck,nik->cni", gathered, inverse, preferred_element_type=jnp.float32
            ).astype(jnp.bfloat16),
            "col",
            scatter_dimension=0,
            tiled=True,
        ).astype(jnp.float32)
        if level_index > 0:
            solved_all = lax.all_gather(own_rows.astype(jnp.bfloat16), "col", axis=0, tiled=True)
        results.append(jnp.swapaxes(own_rows, 0, 1))
        if level_index > 0:
            node_panels = panels[first_node : first_node + node_count]
            node_maps = own_blocks[first_node : first_node + node_count]
            products = jnp.einsum(
                "cnk,nsik->nsci", solved_all, node_panels, preferred_element_type=jnp.float32
            )
            selector = (
                node_maps[:, :, None] == first_target + jnp.arange(S - first_target)[None, None, :]
            ).astype(jnp.float32)
            pending = pending + jnp.einsum(
                "nst,nsci->cti", selector, products, precision=lax.Precision.HIGHEST
            )
    return jnp.concatenate(results, axis=0)


def solution(mesh):
    return jax.shard_map(
        per_device,
        mesh=mesh,
        in_specs=(P(None, "row", "col"), P(None, "row", "col"), P(None, None, "col", "row"), P()),
        out_specs=P(None, "col", "row"),
        check_vma=False,
    )
```

profile of v0, /device:TPU:1, one launch (start us, length us, event | category | flops | bytes accessed | tf_op | source)
XLA Modules:
  0.0 1291.6 jit_solution(15682646200109812419)
XLA Ops:
  6.5 1.6 slice.94
  8.2 84.9 %all-gather.4.cloned.1.call-done = bf16[8,512,256]{2,1,0:T(8,128)(2,1)} async-done(((bf16[8,16,256]{2,1,0:T(8,128)(2,1)}), bf16[8,512,256]{2,1,0:T(8,128)(2,1)}) %all-gather.4.cloned.1.call-update) | async-done | bytes 2097168 | tf_op jit(solution)/shard_map/all_gather | solution.py:31
  93.1 3.6 fusion.14
  96.7 2.6 copy.51
  99.3 60.5 %reduce-scatter.2.cloned.1.call-done = bf16[32,8,128]{2,1,0:T(8,128)(2,1)} async-done(((bf16[512,8,128]{2,1,0:T(8,128)(2,1)}), bf16[32,8,128]{2,1,0:T(8,128)(2,1)}) %reduce-scatter.2.cloned.1.call-update) | async-done | bytes 65552 | tf_op jit(solution)/shard_map/reduce_scatter | solution.py:33
  160.1 45.1 %all-gather.6.cloned.1.call-done = bf16[512,8,128]{2,1,0:T(8,128)(2,1)} async-done(((bf16[32,8,128]{2,1,0:T(8,128)(2,1)}), bf16[512,8,128]{2,1,0:T(8,128)(2,1)}) %all-gather.6.cloned.1.call-update) | async-done | bytes 1048592 | tf_op jit(solution)/shard_map/all_gather | solution.py:42
  205.2 3.0 convolution_bitcast_fusion
  208.3 11.7 fusion
  220.0 1.9 copy-done.2
  222.1 1.3 slice.76
  223.5 1.3 dynamic-slice
  225.4 151.9 %all-reduce.13.cloned.1.call-done = bf16[512,4,256]{2,1,0:T(4,128)(2,1)} async-done(((bf16[512,4,256]{2,1,0:T(4,128)(2,1)}), bf16[512,4,256]{2,1,0:T(4,128)(2,1)}) %all-reduce.13.cloned.1.call-update) | async-done | bytes 1048592
  377.3 1.4 fusion.28
  378.8 81.2 %all-gather.8.cloned.1.call-done = bf16[4,512,256]{2,0,1:T(4,128)(2,1)} async-done(((bf16[4,16,256]{2,0,1:T(4,128)(2,1)}), bf16[4,512,256]{2,0,1:T(4,128)(2,1)}) %all-gather.8.cloned.1.call-update) | async-done | bytes 1048592 | tf_op jit(solution)/shard_map/all_gather | solution.py:31
  460.0 1.7 fusion.15
  461.7 1.2 copy.56
  463.0 1.3 dynamic-slice.2
  465.1 116.2 %all-reduce.15.cloned.1.call-done = bf16[512,4,128]{2,1,0:T(4,128)(2,1)} async-done(((bf16[512,4,128]{2,1,0:T(4,128)(2,1)}), bf16[512,4,128]{2,1,0:T(4,128)(2,1)}) %all-reduce.15.cloned.1.call-update) | async-done | bytes 524304
  582.1 17.0 %all_gather.24 = bf16[512,4,128]{2,1,0:T(4,128)(2,1)S(1)} all-gather(bf16[32,4,128]{2,1,0:T(4,128)(2,1)S(1)} %constant_dynamic-slice_fusion.2), channel_id=1, replica_groups=mesh['row'=32,'col'=16] {'col'}, dimensions={0}, use_global_device_ids=true | all-gather | bytes 557056 | tf_op jit(solution)/shard_map/all_gather | solution.py:42
  601.3 9.1 bitcast_add_fusion.1
  610.4 1.9 copy-done.1
  612.6 1.4 slice.77
  614.0 152.9 %all-reduce.17.cloned.1.call-done = bf16[512,2,256]{2,1,0:T(2,128)(2,1)} async-done(((bf16[512,2,256]{2,1,0:T(2,128)(2,1)}), bf16[512,2,256]{2,1,0:T(2,128)(2,1)}) %all-reduce.17.cloned.1.call-update) | async-done | bytes 524304
  767.7 36.0 %all_gather.25 = bf16[2,512,256]{2,0,1:T(2,128)(2,1)S(1)} all-gather(bf16[2,16,256]{2,0,1:T(2,128)(2,1)S(1)} %fusion.31), channel_id=1, replica_groups=mesh['row'=32,'col'=16] {'row'}, dimensions={1}, use_global_device_ids=true | all-gather | bytes 540672 | tf_op jit(solution)/shard_map/all_gather | solution.py:31
  803.7 1.2 fusion.16
  806.1 129.3 %all-reduce.19.cloned.1.call-done = bf16[512,2,128]{2,1,0:T(2,128)(2,1)} async-done(((bf16[512,2,128]{2,1,0:T(2,128)(2,1)}), bf16[512,2,128]{2,1,0:T(2,128)(2,1)}) %all-reduce.19.cloned.1.call-update) | async-done | bytes 262160
  936.1 15.9 %all_gather.26 = bf16[512,2,128]{2,1,0:T(2,128)(2,1)S(1)} all-gather(bf16[32,2,128]{2,1,0:T(2,128)(2,1)S(1)} %constant_dynamic-slice_fusion.1), channel_id=1, replica_groups=mesh['row'=32,'col'=16] {'col'}, dimensions={0}, use_global_device_ids=true | all-gather | bytes 278528 | tf_op jit(solution)/shard_map/all_gather | solution.py:42
  952.6 7.9 fusion.10
  960.6 1.3 slice.78
  962.8 152.5 %all-reduce.21.cloned.1.call-done = bf16[512,1,256]{2,1,0:T(2,128)(2,1)} async-done(((bf16[512,1,256]{2,1,0:T(2,128)(2,1)}), bf16[512,1,256]{2,1,0:T(2,128)(2,1)}) %all-reduce.21.cloned.1.call-update) | async-done | bytes 262160
  1116.1 35.2 %all_gather.27 = bf16[1,512,256]{2,1,0:T(8,128)(2,1)S(1)} all-gather(bf16[1,16,256]{2,1,0:T(8,128)(2,1)S(1)} %copy.68), channel_id=1, replica_groups=mesh['row'=32,'col'=16] {'row'}, dimensions={1}, use_global_device_ids=true | all-gather | bytes 270336 | tf_op jit(solution)/shard_map/all_gather | solution.py:31
  1154.1 129.2 %all-reduce.23.cloned.1.call-done = bf16[512,1,128]{2,1,0:T(2,128)(2,1)} async-done(((bf16[512,1,128]{2,1,0:T(2,128)(2,1)}), bf16[512,1,128]{2,1,0:T(2,128)(2,1)}) %all-reduce.23.cloned.1.call-update) | async-done | bytes 131088
  (62 shorter events, 13.3 us)
Async XLA Ops:
  6.5 153.3 %copy-start = (s32[14,16,3]{1,0,2:T(8,128)S(1)}, s32[14,16,3]{1,0,2:T(8,128)}, u32[]{:S(2)}) copy-start(s32[14,16,3]{1,0,2:T(8,128)} %param.7) | copy-start | bytes 8068
  6.5 86.6 %all-gather.4.cloned.1.call-start = ((), (), s32[]{:S(2)}) async-start(), calls=%async_computation.1 | async-start | bytes 2162688 | tf_op jit(solution)/shard_map/all_gather | solution.py:31
  8.1 151.7 %reduce-scatter.2.cloned.1.call-start = ((), (), s32[]{:S(2)}) async-start(), calls=%async_computation.2 | async-start | bytes 1114112 | tf_op jit(solution)/shard_map/reduce_scatter | solution.py:33
  96.7 108.6 %copy-start.4 = (bf16[14,3,256,128]{3,2,1,0:T(8,128)(2,1)S(1)}, bf16[14,3,256,128]{3,2,1,0:T(8,128)(2,1)}, u32[]{:S(2)}) copy-start(bf16[14,3,256,128]{3,2,1,0:T(8,128)(2,1)} %param.6) | copy-start | bytes 8257540
  99.3 106.0 %all-gather.6.cloned.1.call-start = ((), (), s32[]{:S(2)}) async-start(), calls=%async_computation.3 | async-start | bytes 1114112 | tf_op jit(solution)/shard_map/all_gather | solution.py:42
  159.8 217.5 %all-reduce.13.cloned.1.call-start = ((), (), s32[]{:S(2)}) async-start(), calls=%async_computation.5 | async-start | bytes 2097152
  219.9 2.0 copy-start.2
  221.9 155.4 %slice-start = ((f32[15,16,256]{2,1,0:T(8,128)}), f32[4,16,256]{2,1,0:T(8,128)S(1)}, s32[]{:S(2)}) async-start(f32[15,16,256]{2,1,0:T(8,128)} %param.4), calls=%async_computation.11 | async-start | bytes 131072 | tf_op jit(solution)/shard_map/slice | solution.py:22
  223.5 236.6 %all-gather.8.cloned.1.call-start = ((), (), s32[]{:S(2)}) async-start(), calls=%async_computation.4 | async-start | bytes 1081344 | tf_op jit(solution)/shard_map/all_gather | solution.py:31
  378.8 202.6 %all-reduce.15.cloned.1.call-start = ((), (), s32[]{:S(2)}) async-start(), calls=%async_computation.6 | async-start | bytes 1048576
  463.0 303.9 %all-reduce.17.cloned.1.call-start = ((), (), s32[]{:S(2)}) async-start(), calls=%async_computation.7 | async-start | bytes 1048576
  599.1 2.2 copy-start.3
  610.4 2.0 copy-start.1
  612.4 154.6 %slice-start.1 = ((f32[15,16,256]{2,1,0:T(8,128)}), f32[2,16,256]{2,1,0:T(8,128)S(1)}, s32[]{:S(2)}) async-start(f32[15,16,256]{2,1,0:T(8,128)} %param.4), calls=%async_computation.12 | async-start | bytes 65536 | tf_op jit(solution)/shard_map/slice | solution.py:22
  614.0 321.4 %all-reduce.19.cloned.1.call-start = ((), (), s32[]{:S(2)}) async-start(), calls=%async_computation.8 | async-start | bytes 524288
  805.9 309.5 %all-reduce.21.cloned.1.call-start = ((), (), s32[]{:S(2)}) async-start(), calls=%async_computation.9 | async-start | bytes 1048576
  952.6 9.4 copy-start.5
  952.6 162.7 %slice-start.2 = ((f32[15,16,256]{2,1,0:T(8,128)}), f32[1,16,256]{2,1,0:T(8,128)S(1)}, s32[]{:S(2)}) async-start(f32[15,16,256]{2,1,0:T(8,128)} %param.4), calls=%async_computation.13 | async-start | bytes 32768 | tf_op jit(solution)/shard_map/slice | solution.py:22
  961.9 321.3 %all-reduce.23.cloned.1.call-start = ((), (), s32[]{:S(2)}) async-start(), calls=%async_computation.10 | async-start | bytes 524288
Sparse Core Ops, SparseCore 0:
  10.4 82.6 all-gather.3
  99.4 60.3 reduce-scatter.1
  162.1 43.0 all-gather.5
  223.6 153.6 all-reduce.12
  380.8 79.1 all-gather.7
  463.1 118.2 all-reduce.14
  614.1 152.7 all-reduce.16
  806.0 129.3 all-reduce.18
  962.1 153.2 all-reduce.20
  1153.4 129.7 all-reduce.22
where the time goes:
time: 1290 us
  waiting for transfers between devices  1100 us (85%)
  blocking collectives  104 us (8%)
  matrix products  40.8 us (3%)
  local copies, waits for them, and re-layouts  23.2 us (2%)
  between operations  15 us (1%)
    unnamed x16, waiting for transfers between devices  832 us
    all_gather x2, waiting for transfers between devices, per_device(): lax.all_gather(current.astype(jnp.bfloat16), 'row', axis=1, tiled=True)  166 us
    all_gather x2, blocking collectives, per_device(): lax.all_gather(current.astype(jnp.bfloat16), 'row', axis=1, tiled=True)  71.2 us
    reduce_scatter x1, waiting for transfers between devices, per_device(): lax.psum_scatter(jnp.einsum('nck,nik->cni', gathered, inverse, preferred_...  60.5 us
    all_gather x1, waiting for transfers between devices, per_device(): lax.all_gather(own_rows.astype(jnp.bfloat16), 'col', axis=0, tiled=True)  45.1 us
    all_gather x2, blocking collectives, per_device(): lax.all_gather(own_rows.astype(jnp.bfloat16), 'col', axis=0, tiled=True)  32.9 us
    dot_general x3, matrix products, per_device(): jnp.einsum('nst,nsci->cti', selector, products, precision=lax.Precision.H...  28.7 us
  transfers between devices with their start and end apart: 10, of which 10 were waited for; matrix products, arithmetic and copies ran while one was open for 0% of the time, Pallas kernels for 0%

commit v1 on v0

v1 whole, which is shorter than its diff:
```python
import jax
import jax.numpy as jnp
from jax import lax
from jax.experimental import pallas as pl
from jax.experimental.pallas import tpu as pltpu
from jax.sharding import Mesh
from jax.sharding import PartitionSpec as P

ROW = ("x", "y")
COL = ("z", "core")
ALL = ("x", "y", "z", "core")
NR = 32
NC = 16
VMEM_LIMIT = 56 * 1024 * 1024
F32 = jnp.float32
BF16 = jnp.bfloat16


def params(n=1):
    return pltpu.CompilerParams(
        vmem_limit_bytes=VMEM_LIMIT, dimension_semantics=("arbitrary",) * n
    )


def dot_t(a, b):
    return lax.dot_general(a, b, (((1,), (1,)), ((), ())), preferred_element_type=F32)


def slot_of(meta, source, target):
    base = 4 + (source * NC + meta[0]) * 3
    second = jnp.where(meta[base + 1] == target, 1, 0)
    slot = jnp.where(meta[base + 2] == target, 2, second)
    return slot, meta[base + slot] == target


def upper_pair(b):
    is_low = b < 8
    source = jnp.where(is_low, 8 + b // 2, 4 + b)
    target = jnp.where(is_low & (b % 2 == 0), 12 + b // 4, 14)
    return source, target


def select_upper(meta, panels):
    def kernel(meta_ref, p_ref, o_ref):
        _, found = slot_of(meta_ref, *upper_pair(pl.program_id(0)))
        o_ref[...] = jnp.where(found, p_ref[0], jnp.zeros_like(p_ref[0]))

    def index(b, meta_ref):
        source, target = upper_pair(b)
        slot, _ = slot_of(meta_ref, source, target)
        return source, slot, 0, 0

    return pl.pallas_call(
        kernel,
        grid_spec=pltpu.PrefetchScalarGridSpec(
            num_scalar_prefetch=1,
            grid=(10,),
            in_specs=[pl.BlockSpec((1, 1, 256, 128), index)],
            out_specs=pl.BlockSpec((1, 256, 128), lambda b, m: (b, 0, 0)),
        ),
        out_shape=jax.ShapeDtypeStruct((10, 256, 128), BF16),
        compiler_params=params(),
        name="select_upper",
    )(meta, panels)


def solve_leaves(spread, inverse):
    def kernel(b_ref, d_ref, x_ref, h_ref):
        acc = jnp.zeros((32, 128), F32)
        for c in range(NC):
            left = b_ref[2 * c : 2 * c + 2, 0].reshape(32, 256)
            acc = acc + dot_t(left, d_ref[c, 0])
        x_ref[0] = acc
        h_ref[0] = acc.astype(BF16)

    return pl.pallas_call(
        kernel,
        grid=(8,),
        in_specs=[
            pl.BlockSpec((32, 1, 16, 256), lambda n: (0, n, 0, 0)),
            pl.BlockSpec((16, 1, 128, 256), lambda n: (0, n, 0, 0)),
        ],
        out_specs=[
            pl.BlockSpec((1, 32, 128), lambda n: (n, 0, 0)),
            pl.BlockSpec((1, 32, 128), lambda n: (n, 0, 0)),
        ],
        out_shape=[
            jax.ShapeDtypeStruct((8, 32, 128), F32),
            jax.ShapeDtypeStruct((8, 32, 128), BF16),
        ],
        compiler_params=params(),
        name="solve_leaves",
    )(spread, inverse)


def update_from_leaves(meta, own, other, panels):
    def kernel(meta_ref, a_ref, b_ref, p_ref, o_ref):
        core = meta_ref[1]
        for t in range(7):
            target = 8 + t
            if t < 4:
                sources = range(2 * t, 2 * t + 2)
            elif t < 6:
                sources = range(4 * (t - 4), 4 * (t - 4) + 4)
            else:
                sources = range(8)
            blocks = []
            for s in sources:
                slot, found = slot_of(meta_ref, s, target)
                block = p_ref[s, slot]
                blocks.append(jnp.where(found, block, jnp.zeros_like(block)))
            for parity, x_ref in ((core, a_ref), (1 - core, b_ref)):
                acc = jnp.zeros((256, 256), F32)
                for s, block in zip(sources, blocks, strict=True):
                    acc = acc + dot_t(x_ref[:, s].reshape(256, 128), block)
                o_ref[:, pl.ds(parity, 1), :, t] = acc.astype(BF16).reshape(8, 1, 2, 16, 256)

    return pl.pallas_call(
        kernel,
        grid_spec=pltpu.PrefetchScalarGridSpec(
            num_scalar_prefetch=1,
            grid=(1,),
            in_specs=[
                pl.BlockSpec((8, 8, 32, 128), lambda i, m: (0, 0, 0, 0)),
                pl.BlockSpec((8, 8, 32, 128), lambda i, m: (0, 0, 0, 0)),
                pl.BlockSpec((8, 3, 256, 128), lambda i, m: (0, 0, 0, 0)),
            ],
            out_specs=pl.BlockSpec((8, 2, 2, 7, 16, 256), lambda i, m: (0, 0, 0, 0, 0, 0)),
        ),
        out_shape=jax.ShapeDtypeStruct((8, 2, 2, 7, 16, 256), BF16),
        compiler_params=params(),
        name="update_from_leaves",
    )(meta, own, other, panels)


def store_pieces(o_ref, residual, d_ref):
    for c in range(NC):
        for half in range(2):
            piece = dot_t(residual, d_ref[2 * c + half, 0])
            o_ref[c, 0, :, 128 * half : 128 * half + 128] = piece.astype(BF16)


def solve_first(parts, right, inverse):
    def kernel(p_ref, b_ref, d_ref, o_ref, rest_ref, scratch):
        n = pl.program_id(0)

        @pl.when(n == 0)
        def _():
            residual = b_ref[...] - jnp.sum(p_ref[...].astype(F32), axis=0)
            scratch[...] = residual[:4].astype(BF16)
            rest_ref[...] = residual[4:]

        store_pieces(o_ref, scratch[n], d_ref)

    return pl.pallas_call(
        kernel,
        grid=(4,),
        in_specs=[
            pl.BlockSpec((32, 7, 16, 256), lambda n: (0, 0, 0, 0)),
            pl.BlockSpec((7, 16, 256), lambda n: (0, 0, 0)),
            pl.BlockSpec((32, 1, 128, 256), lambda n: (0, n, 0, 0)),
        ],
        out_specs=[
            pl.BlockSpec((16, 1, 16, 256), lambda n: (0, n, 0, 0)),
            pl.BlockSpec((3, 16, 256), lambda n: (0, 0, 0)),
        ],
        out_shape=[
            jax.ShapeDtypeStruct((16, 4, 16, 256), BF16),
            jax.ShapeDtypeStruct((3, 16, 256), F32),
        ],
        scratch_shapes=[pltpu.VMEM((4, 16, 256), BF16)],
        compiler_params=params(),
        name="solve_first",
    )(parts, right, inverse)


def solve_next(known, blocks, rest, inverse, nodes, per_source, first_node):
    count, waiting = blocks.shape[1], rest.shape[0]
    after = waiting - nodes
    sources = known.shape[1]

    def kernel(x_ref, l_ref, rest_ref, d_ref, o_ref, *others):
        later_ref = others[0] if after else None
        acc, half = others[-2], others[-1]
        i = pl.program_id(0)

        @pl.when(i == 0)
        def _():
            acc[...] = rest_ref[...]

        @pl.when(i < count)
        def _():
            source = i // per_source
            if per_source == 2:
                target = jnp.where(i % 2 == 0, source // 2, waiting - 1)
            else:
                target = 0
            total = jnp.zeros((16, 256), F32)
            for r in range(NR):
                left = x_ref[r // 2, source, :, 128 * (r % 2) : 128 * (r % 2) + 128]
                total = total + dot_t(left, l_ref[r, 0])
            acc[target] = acc[target] - total

        @pl.when(i == count)
        def _():
            half[...] = acc[:nodes].astype(BF16)
            if after:
                later_ref[...] = acc[nodes:]

        @pl.when(i >= count)
        def _():
            store_pieces(o_ref, half[i - count], d_ref)

    out_specs = [
        pl.BlockSpec((16, 1, 16, 256), lambda i: (0, jnp.maximum(i - count, 0), 0, 0))
    ]
    out_shape = [jax.ShapeDtypeStruct((16, nodes, 16, 256), BF16)]
    if after:
        out_specs.append(pl.BlockSpec((after, 16, 256), lambda i: (0, 0, 0)))
        out_shape.append(jax.ShapeDtypeStruct((after, 16, 256), F32))
    return pl.pallas_call(
        kernel,
        grid=(count + nodes,),
        in_specs=[
            pl.BlockSpec((16, sources, 16, 256), lambda i: (0, 0, 0, 0)),
            pl.BlockSpec((32, 1, 256, 128), lambda i: (0, jnp.minimum(i, count - 1), 0, 0)),
            pl.BlockSpec((waiting, 16, 256), lambda i: (0, 0, 0)),
            pl.BlockSpec(
                (32, 1, 128, 256), lambda i: (0, first_node + jnp.maximum(i - count, 0), 0, 0)
            ),
        ],
        out_specs=out_specs,
        out_shape=out_shape,
        scratch_shapes=[pltpu.VMEM((waiting, 16, 256), F32), pltpu.VMEM((nodes, 16, 256), BF16)],
        compiler_params=params(),
        name="solve_next",
    )(known, blocks, rest, inverse)


def add_pieces(pieces):
    n = pieces.shape[1]

    def kernel(p_ref, x_ref, h_ref):
        total = jnp.sum(p_ref[...].astype(F32), axis=0)
        x_ref[...] = total
        h_ref[...] = total.astype(BF16)

    return pl.pallas_call(
        kernel,
        out_shape=[
            jax.ShapeDtypeStruct((n, 16, 256), F32),
            jax.ShapeDtypeStruct((n, 16, 256), BF16),
        ],
        compiler_params=params(0),
        name="add_pieces",
    )(pieces)


def exchange(values, axes):
    shape = values.shape
    flat = values.reshape(shape[0], -1, shape[-1])
    return lax.all_to_all(flat, axes, 0, 0, tiled=True).reshape(shape)


def spread_over(values, axes, size):
    return exchange(jnp.broadcast_to(values[None], (size,) + values.shape), axes)


def place(values, row):
    odd = row % 2 == 1
    low, high = values[..., :128], values[..., 128:]
    received = []
    for p in range(2):
        pairs = []
        for r in range(NR):
            for c in range(NC):
                pairs.append((r * NC + c, (2 * c + (r + p) % 2) * NC + r // 2))
        take_high = odd if p == 0 else ~odd
        received.append(lax.ppermute(jnp.where(take_high, high, low), ALL, pairs))
    first = jnp.where(odd, received[1], received[0])
    second = jnp.where(odd, received[0], received[1])
    return jnp.concatenate([first, second], axis=1)


def per_device(right_sides, diag_inverse, panels, block_map):
    row = lax.axis_index(ROW)
    col = lax.axis_index(COL)
    core = lax.axis_index("core")
    zero = jnp.zeros((), jnp.int32)
    meta = jnp.concatenate(
        [jnp.stack([col, core, zero, zero]).astype(jnp.int32), block_map.reshape(-1)]
    )

    leaf_inverse = lax.all_gather(diag_inverse[:8], COL, axis=0)
    upper = select_upper(meta, panels)
    inverse_two = lax.all_gather(diag_inverse[8:], ROW, axis=0)
    blocks_two = lax.all_gather(upper[:8], ROW, axis=0)
    blocks_one = lax.all_gather(upper[8:], ROW, axis=0)

    pairs = [
        (r * NC + c, (2 * c + r % 2) * NC + r // 2) for r in range(NR) for c in range(NC)
    ]
    moved = lax.ppermute(right_sides[:8].astype(BF16), ALL, pairs)
    spread = spread_over(moved, ROW, NR)
    leaves, leaves_half = solve_leaves(spread, leaf_inverse)
    own = spread_over(leaves_half, "z", 8)
    other = lax.ppermute(own, "core", [(0, 1), (1, 0)])
    parts = update_from_leaves(meta, own, other, panels)
    parts = exchange(parts.reshape(NR, 7, 16, 256), ROW)

    pieces, rest = solve_first(parts, right_sides[8:], inverse_two)
    two, two_half = add_pieces(exchange(pieces, COL))
    known = lax.all_gather(two_half, COL, axis=0)
    pieces, rest = solve_next(known, blocks_two, rest, inverse_two, 2, 2, 4)
    one, one_half = add_pieces(exchange(pieces, COL))
    known = spread_over(one_half, COL, NC)
    early = place(jnp.concatenate([two, one], axis=0), row)
    (pieces,) = solve_next(known, blocks_one, rest, inverse_two, 1, 1, 6)
    root, _ = add_pieces(exchange(pieces, COL))
    return jnp.concatenate([leaves, early, place(root, row)], axis=0)


def solution(mesh):
    split = Mesh(mesh.devices.reshape(4, 8, 8, 2), ALL)
    return jax.shard_map(
        per_device,
        mesh=split,
        in_specs=(P(None, ROW, COL), P(None, ROW, COL), P(None, None, COL, ROW), P()),
        out_specs=P(None, COL, ROW),
        check_vma=False,
    )
```

time: 1290 us -> 550 us (0.43)
  the two profiles are of different devices: /device:TPU:1 before, /device:TPU:76 now
where the time goes in v1:
time: 550 us; the launch traced here: 548 us
  waiting for transfers between devices  306 us (56%)
  blocking collectives  82.6 us (15%)
  starting transfers between devices  76.2 us (14%)
  Pallas kernels  51.8 us (9%)
  local copies, waits for them, and re-layouts  15.7 us (3%)
  between operations  13.4 us (2%)
    all_to_all x4, waiting for transfers between devices, exchange(): return lax.all_to_all(flat, axes, 0, 0, tiled=True).reshape(shape)  108 us
    all_gather x1, waiting for transfers between devices, per_device(): blocks_two = lax.all_gather(upper[:8], ROW, axis=0)  96.4 us
    all_to_all x3, blocking collectives, exchange(): return lax.all_to_all(flat, axes, 0, 0, tiled=True).reshape(shape)  63.5 us
    all_gather x1, waiting for transfers between devices, per_device(): blocks_one = lax.all_gather(upper[8:], ROW, axis=0)  49.8 us
    all_gather x1, waiting for transfers between devices, per_device(): inverse_two = lax.all_gather(diag_inverse[8:], ROW, axis=0)  36 us
    ppermute x4, starting transfers between devices, place(): received.append(lax.ppermute(jnp.where(take_high, high, low), ALL, pairs))  31.2 us
    all_to_all x4, starting transfers between devices, exchange(): return lax.all_to_all(flat, axes, 0, 0, tiled=True).reshape(shape)  29.5 us
    all_gather x1, blocking collectives, per_device(): known = lax.all_gather(two_half, COL, axis=0)  19.1 us
  transfers between devices with their start and end apart: 14, of which 8 were waited for; matrix products, arithmetic and copies ran while one was open for 2% of the time, Pallas kernels for 9%

profile of v1, /device:TPU:76, one launch (start us, length us, event | category | flops | bytes accessed | tf_op | source)
XLA Modules:
  0.0 547.6 jit_solution(3776372092795914777)
XLA Ops:
  6.5 1.9 slice.32
  8.5 1.8 slice.34
  11.5 6.4 %select_upper.1 = bf16[10,256,128]{2,1,0:T(8,128)(2,1)} custom-call(s32[676]{0:T(1024)} %pad_add_fusion.meta_ref, bf16[14,3,256,128]{3,2,1,0:T(8,128)(2,1)} %p_ref.3), custom_call_target="tpu_custom_call" | custom-call | tf_op jit(solution)/shard_map/select_upper/pallas_call | solution.py:53
  17.9 1.9 slice.42
  19.9 13.4 %collective-permute-start = (bf16[8,16,256]{2,1,0:T(8,128)(2,1)S(1)}, bf16[8,16,256]{2,1,0:T(8,128)(2,1)S(1)}, u32[]{:S(2)}, u32[]{:S(2)}) collective-permute-start(bf16[8,16,256]{2,1,0:T(8,128)(2,1)S(1)} %slice.55), channel_id=1, source_target_pairs={{0,0},{1,32},{2,64},{3,96},{4,128},{5,160},{6,192},{7,224},{8,256}... | collective-permute-start | bytes 196616 | tf_op jit(solution)/shard_map/ppermute | solution.py:303
  33.3 3.3 collective-permute-done
  38.3 10.1 %all-to-all-start = ((bf16[32,128,256]{2,1,0:T(8,128)(2,1)}), bf16[32,128,256]{2,1,0:T(8,128)(2,1)S(1)}, u32[]{:S(2)}, u32[]{:S(2)}) async-start(bf16[32,128,256]{2,1,0:T(8,128)(2,1)} %broadcast_in_dim.25), calls=%async_computation | async-start | bytes 4194304 | tf_op jit(solution)/shard_map/all_to_all | solution.py:262
  50.0 46.0 %all-to-all-done = bf16[32,128,256]{2,1,0:T(8,128)(2,1)S(1)} async-done(((bf16[32,128,256]{2,1,0:T(8,128)(2,1)}), bf16[32,128,256]{2,1,0:T(8,128)(2,1)S(1)}, u32[]{:S(2)}, u32[]{:S(2)}) %all-to-all-start) | async-done | bytes 2097184 | tf_op jit(solution)/shard_map/all_to_all | solution.py:262
  97.4 8.6 %solve_leaves.1 = (f32[8,32,128]{2,1,0:T(8,128)}, bf16[8,32,128]{2,1,0:T(8,128)(2,1)}) custom-call(bf16[32,8,16,256]{3,2,1,0:T(8,128)(2,1)} %bitcast.26, bf16[16,8,128,256]{3,2,1,0:T(8,128)(2,1)} %bitcast.25), custom_call_target="tpu_custom_call" | custom-call | tf_op jit(solution)/shard_map/solve_leaves/pallas_call | solution.py:76
  107.0 23.7 %all_to_all.35 = bf16[8,256,128]{2,1,0:T(8,128)(2,1)S(1)} all-to-all(bf16[8,256,128]{2,1,0:T(8,128)(2,1)S(1)} %broadcast_in_dim.27), channel_id=1, replica_groups=mesh['x'=4,'y'=8,'z'=8,'core'=2] {'z'}, dimensions={0} | all-to-all | bytes 1048576 | tf_op jit(solution)/shard_map/all_to_all | solution.py:262
  130.7 1.9 collective-permute-start.1
  132.6 1.9 collective-permute-done.1.b_ref
  135.3 6.0 %update_from_leaves.1 = bf16[8,2,2,7,16,256]{5,4,3,2,1,0:T(8,128)(2,1)} custom-call(s32[676]{0:T(1024)} %pad_add_fusion.meta_ref, bf16[8,8,32,128]{3,2,1,0:T(8,128)(2,1)} %bitcast.32, bf16[8,8,32,128]{3,2,1,0:T(8,128)(2,1)} %copy-done.4, bf16[14,3,256,128]{3,2,1,0:T(8,128)(2,1)} %p_ref.3), custom_call_target="tpu_custom_call" | custom-call | tf_op jit(solution)/shard_map/update_from_leaves/pallas_call | solution.py:118
  141.3 6.6 %all-to-all-start.2 = ((bf16[32,112,256]{2,1,0:T(8,128)(2,1)}), bf16[32,112,256]{2,1,0:T(8,128)(2,1)S(1)}, u32[]{:S(2)}, u32[]{:S(2)}) async-start(bf16[32,112,256]{2,1,0:T(8,128)(2,1)} %bitcast.28), calls=%async_computation.2 | async-start | bytes 3670016 | tf_op jit(solution)/shard_map/all_to_all | solution.py:262
  148.6 62.5 %all-to-all-done.2 = bf16[32,112,256]{2,1,0:T(8,128)(2,1)S(1)} async-done(((bf16[32,112,256]{2,1,0:T(8,128)(2,1)}), bf16[32,112,256]{2,1,0:T(8,128)(2,1)S(1)}, u32[]{:S(2)}, u32[]{:S(2)}) %all-to-all-start.2) | async-done | bytes 1835040 | tf_op jit(solution)/shard_map/all_to_all | solution.py:262
  211.1 36.0 %all-gather.12.cloned.1.call-done = bf16[224,128,256]{2,1,0:T(8,128)(2,1)} async-done(((bf16[7,128,256]{2,1,0:T(8,128)(2,1)}), bf16[224,128,256]{2,1,0:T(8,128)(2,1)}) %all-gather.12.cloned.1.call-update) | async-done | bytes 14680080 | tf_op jit(solution)/shard_map/all_gather | solution.py:296
  247.0 6.9 %solve_first.1 = (bf16[16,4,16,256]{3,2,1,0:T(8,128)(2,1)}, f32[3,16,256]{2,1,0:T(8,128)}) custom-call(bf16[32,7,16,256]{3,2,1,0:T(8,128)(2,1)} %bitcast.27, f32[7,16,256]{2,1,0:T(8,128)} %slice.33.b_ref, bf16[32,7,128,256]{3,2,1,0:T(8,128)(2,1)} %bitcast.21), custom_call_target="tpu_custom_call" | custom-call | tf_op jit(solution)/shard_map/solve_first/pallas_call | solution.py:155
  253.9 22.2 %all_to_all.36 = bf16[16,64,256]{2,1,0:T(8,128)(2,1)} all-to-all(bf16[16,64,256]{2,1,0:T(8,128)(2,1)} %bitcast.37), channel_id=1, replica_groups=mesh['x'=4,'y'=8,'z'=8,'core'=2] {'z','core'}, dimensions={0} | all-to-all | bytes 1048576 | tf_op jit(solution)/shard_map/all_to_all | solution.py:262
  276.1 1.8 add_pieces.3
  277.9 19.1 %all-gather.2 = bf16[64,16,256]{2,1,0:T(8,128)(2,1)} all-gather(bf16[4,16,256]{2,1,0:T(8,128)(2,1)} %get-tuple-element.20), channel_id=4, replica_groups=mesh['x'=4,'y'=8,'z'=8,'core'=2] {'z','core'}, dimensions={0}, use_global_device_ids=true | all-gather | bytes 557056 | tf_op jit(solution)/shard_map/all_gather | solution.py:313
  297.0 96.4 %all-gather.14.cloned.1.call-done = bf16[256,256,128]{2,1,0:T(8,128)(2,1)} async-done(((bf16[8,256,128]{2,1,0:T(8,128)(2,1)}), bf16[256,256,128]{2,1,0:T(8,128)(2,1)}) %all-gather.14.cloned.1.call-update) | async-done | bytes 16777232 | tf_op jit(solution)/shard_map/all_gather | solution.py:297
  393.4 13.9 %solve_next.2 = (bf16[16,2,16,256]{3,2,1,0:T(8,128)(2,1)}, f32[1,16,256]{2,1,0:T(8,128)}) custom-call(bf16[16,4,16,256]{3,2,1,0:T(8,128)(2,1)} %bitcast.30, bf16[32,8,256,128]{3,2,1,0:T(8,128)(2,1)} %bitcast.24, f32[3,16,256]{2,1,0:T(8,128)} %get-tuple-element.21.rest_ref, bf16[32,7,128,256]{3,2,1,0:T(8,128)(2,1)} %bitcast.22), custom_call_target="tpu_custom_call" | custom-call | tf_op jit(solution)/shard_map/solve_next/pallas_call | solution.py:221
  407.3 17.5 %all_to_all.37 = bf16[16,32,256]{2,1,0:T(8,128)(2,1)} all-to-all(bf16[16,32,256]{2,1,0:T(8,128)(2,1)} %bitcast.39), channel_id=1, replica_groups=mesh['x'=4,'y'=8,'z'=8,'core'=2] {'z','core'}, dimensions={0} | all-to-all | bytes 524288 | tf_op jit(solution)/shard_map/all_to_all | solution.py:262
  427.9 5.0 all-to-all-start.5
  432.9 49.8 %all-gather.16.cloned.1.call-done = bf16[64,256,128]{2,1,0:T(8,128)(2,1)} async-done(((bf16[2,256,128]{2,1,0:T(8,128)(2,1)}), bf16[64,256,128]{2,1,0:T(8,128)(2,1)}) %all-gather.16.cloned.1.call-update) | async-done | bytes 4194320 | tf_op jit(solution)/shard_map/all_gather | solution.py:298
  483.4 5.0 solve_next.3
  488.4 7.8 %all-to-all-start.6 = ((bf16[16,16,256]{2,1,0:T(8,128)(2,1)}), bf16[16,16,256]{2,1,0:T(8,128)(2,1)S(1)}, u32[]{:S(2)}, u32[]{:S(2)}) async-start(bf16[16,16,256]{2,1,0:T(8,128)(2,1)} %bitcast.36), calls=%async_computation.6 | async-start | bytes 262144 | tf_op jit(solution)/shard_map/all_to_all | solution.py:262
  496.2 8.7 %collective-permute-start.2 = (f32[6,16,128]{2,1,0:T(8,128)S(1)}, f32[6,16,128]{2,1,0:T(8,128)S(1)}, u32[]{:S(2)}, u32[]{:S(2)}) collective-permute-start(f32[6,16,128]{2,1,0:T(8,128)S(1)} %get-tuple-element.29), channel_id=1, source_target_pairs={{0,16},{1,48},{2,80},{3,112},{4,144},{5,176},{6,208},{7,240},{8,27... | collective-permute-start | bytes 147464 | tf_op jit(solution)/shard_map/ppermute | solution.py:279
  505.0 6.1 %collective-permute-start.3 = (f32[6,16,128]{2,1,0:T(8,128)S(1)}, f32[6,16,128]{2,1,0:T(8,128)S(1)}, u32[]{:S(2)}, u32[]{:S(2)}) collective-permute-start(f32[6,16,128]{2,1,0:T(8,128)S(1)} %get-tuple-element.30), channel_id=1, source_target_pairs={{0,0},{1,32},{2,64},{3,96},{4,128},{5,160},{6,192},{7,224},{8,256}... | collective-permute-start | bytes 147464 | tf_op jit(solution)/shard_map/ppermute | solution.py:279
  513.9 10.6 %collective-permute-start.4 = (f32[1,16,128]{2,1,0:T(8,128)S(1)}, f32[1,16,128]{2,1,0:T(8,128)S(1)}, u32[]{:S(2)}, u32[]{:S(2)}) collective-permute-start(f32[1,16,128]{2,1,0:T(8,128)S(1)} %get-tuple-element.33), channel_id=1, source_target_pairs={{0,16},{1,48},{2,80},{3,112},{4,144},{5,176},{6,208},{7,240},{8,27... | collective-permute-start | bytes 24584 | tf_op jit(solution)/shard_map/ppermute | solution.py:279
  524.6 5.8 %collective-permute-start.5 = (f32[1,16,128]{2,1,0:T(8,128)S(1)}, f32[1,16,128]{2,1,0:T(8,128)S(1)}, u32[]{:S(2)}, u32[]{:S(2)}) collective-permute-start(f32[1,16,128]{2,1,0:T(8,128)S(1)} %get-tuple-element.34), channel_id=1, source_target_pairs={{0,0},{1,32},{2,64},{3,96},{4,128},{5,160},{6,192},{7,224},{8,256}... | collective-permute-start | bytes 24584 | tf_op jit(solution)/shard_map/ppermute | solution.py:279
  530.4 9.9 %collective-permute-done.5 = f32[1,16,128]{2,1,0:T(8,128)S(1)} collective-permute-done((f32[1,16,128]{2,1,0:T(8,128)S(1)}, f32[1,16,128]{2,1,0:T(8,128)S(1)}, u32[]{:S(2)}, u32[]{:S(2)}) %collective-permute-start.5) | collective-permute-done | bytes 8224 | tf_op jit(solution)/shard_map/ppermute | solution.py:279
  (55 shorter events, 15.7 us)
Async XLA Ops:
  6.5 3.9 copy-start.10
  6.5 89.5 %all-gather.10.cloned.1.call-start = ((), (), s32[]{:S(2)}) async-start(), calls=%async_computation.7 | async-start | bytes 8912896 | tf_op jit(solution)/shard_map/all_gather | solution.py:294
  8.5 238.6 %all-gather.12.cloned.1.call-start = ((), (), s32[]{:S(2)}) async-start(), calls=%async_computation.8 | async-start | bytes 15138816 | tf_op jit(solution)/shard_map/all_gather | solution.py:296
  10.4 9.5 %copy-start.6 = (f32[15,16,256]{2,1,0:T(8,128)S(1)}, f32[15,16,256]{2,1,0:T(8,128)}, u32[]{:S(2)}) copy-start(f32[15,16,256]{2,1,0:T(8,128)} %param.4) | copy-start | bytes 737284
  10.4 383.0 %all-gather.14.cloned.1.call-start = ((), (), s32[]{:S(2)}) async-start(), calls=%async_computation.9 | async-start | bytes 17301504 | tf_op jit(solution)/shard_map/all_gather | solution.py:297
  19.9 16.8 %collective-permute-start = (bf16[8,16,256]{2,1,0:T(8,128)(2,1)S(1)}, bf16[8,16,256]{2,1,0:T(8,128)(2,1)S(1)}, u32[]{:S(2)}, u32[]{:S(2)}) collective-permute-start(bf16[8,16,256]{2,1,0:T(8,128)(2,1)S(1)} %slice.55), channel_id=1, source_target_pairs={{0,0},{1,32},{2,64},{3,96},{4,128},{5,160},{6,192},{7,224},{8,256}... | collective-permute-start | bytes 196616 | tf_op jit(solution)/shard_map/ppermute | solution.py:303
  38.3 57.8 %all-to-all-start = ((bf16[32,128,256]{2,1,0:T(8,128)(2,1)}), bf16[32,128,256]{2,1,0:T(8,128)(2,1)S(1)}, u32[]{:S(2)}, u32[]{:S(2)}) async-start(bf16[32,128,256]{2,1,0:T(8,128)(2,1)} %broadcast_in_dim.25), calls=%async_computation | async-start | bytes 4194304 | tf_op jit(solution)/shard_map/all_to_all | solution.py:262
  48.4 434.3 %all-gather.16.cloned.1.call-start = ((), (), s32[]{:S(2)}) async-start(), calls=%async_computation.10 | async-start | bytes 4325376 | tf_op jit(solution)/shard_map/all_gather | solution.py:298
  96.0 1.4 copy-start
  130.7 3.8 copy-start.2
  130.7 3.8 collective-permute-start.1
  134.5 0.8 copy-start.4
  141.3 69.8 %all-to-all-start.2 = ((bf16[32,112,256]{2,1,0:T(8,128)(2,1)}), bf16[32,112,256]{2,1,0:T(8,128)(2,1)S(1)}, u32[]{:S(2)}, u32[]{:S(2)}) async-start(bf16[32,112,256]{2,1,0:T(8,128)(2,1)} %bitcast.28), calls=%async_computation.2 | async-start | bytes 3670016 | tf_op jit(solution)/shard_map/all_to_all | solution.py:262
  211.1 36.0 %copy-start.1 = (bf16[32,112,256]{2,1,0:T(8,128)(2,1)}, bf16[32,112,256]{2,1,0:T(8,128)(2,1)S(1)}, u32[]{:S(2)}) copy-start(bf16[32,112,256]{2,1,0:T(8,128)(2,1)S(1)} %all-to-all-done.2) | copy-start | bytes 5505028
  393.4 39.4 %copy-start.8 = (f32[4,16,256]{2,1,0:T(8,128)S(1)}, f32[4,16,256]{2,1,0:T(8,128)}, u32[]{:S(2)}) copy-start(f32[4,16,256]{2,1,0:T(8,128)} %get-tuple-element.19) | copy-start | bytes 196612
  427.9 54.8 %all-to-all-start.5 = ((bf16[16,32,256]{2,1,0:T(8,128)(2,1)}), bf16[16,32,256]{2,1,0:T(8,128)(2,1)S(1)}, u32[]{:S(2)}, u32[]{:S(2)}) async-start(bf16[16,32,256]{2,1,0:T(8,128)(2,1)} %broadcast_in_dim.29), calls=%async_computation.5 | async-start | bytes 524288 | tf_op jit(solution)/shard_map/all_to_all | solution.py:262
  482.7 0.7 copy-start.3
  483.4 12.8 %copy-start.9 = (f32[2,16,256]{2,1,0:T(8,128)S(1)}, f32[2,16,256]{2,1,0:T(8,128)}, u32[]{:S(2)}) copy-start(f32[2,16,256]{2,1,0:T(8,128)} %get-tuple-element.23) | copy-start | bytes 98308
  483.4 57.0 %copy-start.7 = (f32[8,32,128]{2,1,0:T(8,128)S(1)}, f32[8,32,128]{2,1,0:T(8,128)}, u32[]{:S(2)}) copy-start(f32[8,32,128]{2,1,0:T(8,128)} %get-tuple-element.16) | copy-start | bytes 393220
  488.4 22.6 %all-to-all-start.6 = ((bf16[16,16,256]{2,1,0:T(8,128)(2,1)}), bf16[16,16,256]{2,1,0:T(8,128)(2,1)S(1)}, u32[]{:S(2)}, u32[]{:S(2)}) async-start(bf16[16,16,256]{2,1,0:T(8,128)(2,1)} %bitcast.36), calls=%async_computation.6 | async-start | bytes 262144 | tf_op jit(solution)/shard_map/all_to_all | solution.py:262
  496.2 34.2 %collective-permute-start.2 = (f32[6,16,128]{2,1,0:T(8,128)S(1)}, f32[6,16,128]{2,1,0:T(8,128)S(1)}, u32[]{:S(2)}, u32[]{:S(2)}) collective-permute-start(f32[6,16,128]{2,1,0:T(8,128)S(1)} %get-tuple-element.29), channel_id=1, source_target_pairs={{0,16},{1,48},{2,80},{3,112},{4,144},{5,176},{6,208},{7,240},{8,27... | collective-permute-start | bytes 147464 | tf_op jit(solution)/shard_map/ppermute | solution.py:279
  505.0 25.4 %collective-permute-start.3 = (f32[6,16,128]{2,1,0:T(8,128)S(1)}, f32[6,16,128]{2,1,0:T(8,128)S(1)}, u32[]{:S(2)}, u32[]{:S(2)}) collective-permute-start(f32[6,16,128]{2,1,0:T(8,128)S(1)} %get-tuple-element.30), channel_id=1, source_target_pairs={{0,0},{1,32},{2,64},{3,96},{4,128},{5,160},{6,192},{7,224},{8,256}... | collective-permute-start | bytes 147464 | tf_op jit(solution)/shard_map/ppermute | solution.py:279
  511.0 0.7 copy-start.5
  513.9 16.5 %collective-permute-start.4 = (f32[1,16,128]{2,1,0:T(8,128)S(1)}, f32[1,16,128]{2,1,0:T(8,128)S(1)}, u32[]{:S(2)}, u32[]{:S(2)}) collective-permute-start(f32[1,16,128]{2,1,0:T(8,128)S(1)} %get-tuple-element.33), channel_id=1, source_target_pairs={{0,16},{1,48},{2,80},{3,112},{4,144},{5,176},{6,208},{7,240},{8,27... | collective-permute-start | bytes 24584 | tf_op jit(solution)/shard_map/ppermute | solution.py:279
  524.6 15.8 %collective-permute-start.5 = (f32[1,16,128]{2,1,0:T(8,128)S(1)}, f32[1,16,128]{2,1,0:T(8,128)S(1)}, u32[]{:S(2)}, u32[]{:S(2)}) collective-permute-start(f32[1,16,128]{2,1,0:T(8,128)S(1)} %get-tuple-element.34), channel_id=1, source_target_pairs={{0,0},{1,32},{2,64},{3,96},{4,128},{5,160},{6,192},{7,224},{8,256}... | collective-permute-start | bytes 24584 | tf_op jit(solution)/shard_map/ppermute | solution.py:279
Sparse Core Ops, SparseCore 0:
  9.5 62.1 all-gather.9
  74.9 172.1 all-gather.11
  250.2 143.1 all-gather.13
  396.4 86.1 all-gather.15

commit v2 on v1

v2 whole, which is shorter than its diff:
```python
import jax
import jax.numpy as jnp
from jax import lax
from jax.experimental import pallas as pl
from jax.experimental.pallas import tpu as pltpu
from jax.sharding import Mesh
from jax.sharding import PartitionSpec as P

ROW = ("x", "y")
COL = ("z", "core")
ALL = ("x", "y", "z", "core")
NR = 32
NC = 16
VMEM_LIMIT = 24 * 1024 * 1024
F32 = jnp.float32
BF16 = jnp.bfloat16


def params(n=1):
    return pltpu.CompilerParams(
        vmem_limit_bytes=VMEM_LIMIT, dimension_semantics=("arbitrary",) * n
    )


def dot_t(a, b):
    return lax.dot_general(a, b, (((1,), (1,)), ((), ())), preferred_element_type=F32)


def slot_of(meta, source, target):
    base = 4 + (source * NC + meta[0]) * 3
    second = jnp.where(meta[base + 1] == target, 1, 0)
    slot = jnp.where(meta[base + 2] == target, 2, second)
    return slot, meta[base + slot] == target


def upper_pair(b):
    is_low = b < 8
    source = jnp.where(is_low, 8 + b // 2, 4 + b)
    target = jnp.where(is_low & (b % 2 == 0), 12 + b // 4, 14)
    return source, target


def select_upper(meta, panels):
    def kernel(meta_ref, p_ref, o_ref):
        _, found = slot_of(meta_ref, *upper_pair(pl.program_id(0)))
        o_ref[...] = jnp.where(found, p_ref[0], jnp.zeros_like(p_ref[0]))

    def index(b, meta_ref):
        source, target = upper_pair(b)
        slot, _ = slot_of(meta_ref, source, target)
        return source, slot, 0, 0

    return pl.pallas_call(
        kernel,
        grid_spec=pltpu.PrefetchScalarGridSpec(
            num_scalar_prefetch=1,
            grid=(10,),
            in_specs=[pl.BlockSpec((1, 1, 256, 128), index)],
            out_specs=pl.BlockSpec((1, 256, 128), lambda b, m: (b, 0, 0)),
        ),
        out_shape=jax.ShapeDtypeStruct((10, 256, 128), BF16),
        compiler_params=params(),
        name="select_upper",
    )(meta, panels)


def solve_leaves(spread, inverse):
    def kernel(b_ref, d_ref, x_ref, h_ref):
        acc = jnp.zeros((32, 128), F32)
        for c in range(NC):
            left = b_ref[2 * c : 2 * c + 2, 0].reshape(32, 256)
            acc = acc + dot_t(left, d_ref[c, 0])
        x_ref[0] = acc
        h_ref[0] = acc.astype(BF16)

    return pl.pallas_call(
        kernel,
        grid=(8,),
        in_specs=[
            pl.BlockSpec((32, 1, 16, 256), lambda n: (0, n, 0, 0)),
            pl.BlockSpec((16, 1, 128, 256), lambda n: (0, n, 0, 0)),
        ],
        out_specs=[
            pl.BlockSpec((1, 32, 128), lambda n: (n, 0, 0)),
            pl.BlockSpec((1, 32, 128), lambda n: (n, 0, 0)),
        ],
        out_shape=[
            jax.ShapeDtypeStruct((8, 32, 128), F32),
            jax.ShapeDtypeStruct((8, 32, 128), BF16),
        ],
        compiler_params=params(),
        name="solve_leaves",
    )(spread, inverse)


def update_from_leaves(meta, own, other, panels):
    def kernel(meta_ref, a_ref, b_ref, p_ref, o_ref):
        core = meta_ref[1]
        for t in range(7):
            target = 8 + t
            if t < 4:
                sources = range(2 * t, 2 * t + 2)
            elif t < 6:
                sources = range(4 * (t - 4), 4 * (t - 4) + 4)
            else:
                sources = range(8)
            blocks = []
            for s in sources:
                slot, found = slot_of(meta_ref, s, target)
                block = p_ref[s, slot]
                blocks.append(jnp.where(found, block, jnp.zeros_like(block)))
            for parity, x_ref in ((core, a_ref), (1 - core, b_ref)):
                acc = jnp.zeros((256, 256), F32)
                for s, block in zip(sources, blocks, strict=True):
                    acc = acc + dot_t(x_ref[:, s].reshape(256, 128), block)
                o_ref[:, pl.ds(parity, 1), :, t] = acc.astype(BF16).reshape(8, 1, 2, 16, 256)

    return pl.pallas_call(
        kernel,
        grid_spec=pltpu.PrefetchScalarGridSpec(
            num_scalar_prefetch=1,
            grid=(1,),
            in_specs=[
                pl.BlockSpec((8, 8, 32, 128), lambda i, m: (0, 0, 0, 0)),
                pl.BlockSpec((8, 8, 32, 128), lambda i, m: (0, 0, 0, 0)),
                pl.BlockSpec((8, 3, 256, 128), lambda i, m: (0, 0, 0, 0)),
            ],
            out_specs=pl.BlockSpec((8, 2, 2, 7, 16, 256), lambda i, m: (0, 0, 0, 0, 0, 0)),
        ),
        out_shape=jax.ShapeDtypeStruct((8, 2, 2, 7, 16, 256), BF16),
        compiler_params=params(),
        name="update_from_leaves",
    )(meta, own, other, panels)


VMEM = pl.BlockSpec(memory_space=pltpu.VMEM)
SMEM = pl.BlockSpec(memory_space=pltpu.SMEM)


def first_residual(meta, parts, right):
    def kernel(meta_ref, p_ref, b_ref, even_ref, odd_ref):
        residual = b_ref[8:] - jnp.sum(p_ref[...].astype(F32), axis=0)
        low, high = residual[..., :128], residual[..., 128:]
        odd = meta_ref[2] == 1
        even_ref[...] = jnp.where(odd, high, low)
        odd_ref[...] = jnp.where(odd, low, high)

    return pl.pallas_call(
        kernel,
        in_specs=[SMEM, VMEM, VMEM],
        out_specs=[VMEM, VMEM],
        out_shape=[jax.ShapeDtypeStruct((7, 16, 128), F32)] * 2,
        compiler_params=params(0),
        name="first_residual",
    )(meta, parts, right)


def join_residual(meta, even, odd_sent):
    def kernel(meta_ref, a_ref, b_ref, o_ref, rest_ref):
        odd = meta_ref[2] == 1
        a, b = a_ref[...], b_ref[...]
        first = jnp.where(odd, b, a)
        second = jnp.where(odd, a, b)
        rest_ref[:, :16] = first[4:]
        rest_ref[:, 16:] = second[4:]
        both = jnp.concatenate([first[:4], second[:4]], axis=1).astype(BF16)
        for r in range(NR):
            o_ref[r] = both

    return pl.pallas_call(
        kernel,
        in_specs=[SMEM, VMEM, VMEM],
        out_specs=[VMEM, VMEM],
        out_shape=[
            jax.ShapeDtypeStruct((NR, 4, 32, 128), BF16),
            jax.ShapeDtypeStruct((3, 32, 128), F32),
        ],
        compiler_params=params(0),
        name="join_residual",
    )(meta, even, odd_sent)


def solve_node(x_ref, d_ref, n, place):
    acc = jnp.zeros((32, 128), F32)
    for c in range(NC):
        left = jnp.concatenate([x_ref[2 * c, n], x_ref[2 * c + 1, n]], axis=1)
        acc = acc + dot_t(left, d_ref[c, place])
    return acc


def solve_level(residual, inverse, place, blocks, block_place, targets):
    nodes = residual.shape[1]

    def kernel(x_ref, d_ref, l_ref, s_ref, o_ref):
        solved = []
        for n in range(nodes):
            x = solve_node(x_ref, d_ref, n, place + n)
            s_ref[n] = x
            solved.append(x.astype(BF16))
        for c in range(NC):
            for t, terms in enumerate(targets):
                acc = jnp.zeros((32, 256), F32)
                for s, b in terms:
                    acc = acc + dot_t(solved[s], l_ref[c, block_place + b])
                out = acc.astype(BF16)
                o_ref[2 * c, t] = out[:, :128]
                o_ref[2 * c + 1, t] = out[:, 128:]

    return pl.pallas_call(
        kernel,
        in_specs=[VMEM, VMEM, VMEM],
        out_specs=[VMEM, VMEM],
        out_shape=[
            jax.ShapeDtypeStruct((nodes, 32, 128), F32),
            jax.ShapeDtypeStruct((NR, len(targets), 32, 128), BF16),
        ],
        compiler_params=params(0),
        name="solve_level",
    )(residual, inverse, blocks)


def solve_root(residual, inverse):
    def kernel(x_ref, d_ref, s_ref):
        s_ref[0] = solve_node(x_ref, d_ref, 0, 6)

    return pl.pallas_call(
        kernel,
        in_specs=[VMEM, VMEM],
        out_specs=VMEM,
        out_shape=jax.ShapeDtypeStruct((1, 32, 128), F32),
        compiler_params=params(0),
        name="solve_root",
    )(residual, inverse)


def next_residual(parts, rest, nodes):
    count = rest.shape[0]
    after = count - nodes

    def kernel(p_ref, rest_ref, o_ref, *later):
        residual = rest_ref[...] - jnp.sum(p_ref[...].astype(F32), axis=0)
        half = residual[:nodes].astype(BF16)
        for r in range(NR):
            o_ref[r] = half
        if after:
            later[0][...] = residual[nodes:]

    out_shape = [jax.ShapeDtypeStruct((NR, nodes, 32, 128), BF16)]
    if after:
        out_shape.append(jax.ShapeDtypeStruct((after, 32, 128), F32))
    return pl.pallas_call(
        kernel,
        in_specs=[VMEM, VMEM],
        out_specs=[VMEM] * len(out_shape),
        out_shape=out_shape,
        compiler_params=params(0),
        name="next_residual",
    )(parts, rest)


def exchange(values, axes):
    shape = values.shape
    flat = values.reshape(shape[0], -1, shape[-1])
    return lax.all_to_all(flat, axes, 0, 0, tiled=True).reshape(shape)


def spread_over(values, axes, size):
    return exchange(jnp.broadcast_to(values[None], (size,) + values.shape), axes)


def to_owner(values, p):
    pairs = [
        (r * NC + c, (2 * c + (r + p) % 2) * NC + r // 2) for r in range(NR) for c in range(NC)
    ]
    return lax.ppermute(values, ALL, pairs)


def per_device(right_sides, diag_inverse, panels, block_map):
    row = lax.axis_index(ROW)
    col = lax.axis_index(COL)
    core = lax.axis_index("core")
    leaf_inverse = lax.all_gather(diag_inverse[:8], COL, axis=0)
    moved = to_owner(right_sides[:8].astype(BF16), 0)
    spread = spread_over(moved, ROW, NR)

    zero = jnp.zeros((), jnp.int32)
    meta = jnp.concatenate(
        [jnp.stack([col, core, row % 2, zero]).astype(jnp.int32), block_map.reshape(-1)]
    )
    meta, _ = lax.optimization_barrier((meta, moved))
    blocks = lax.all_gather(select_upper(meta, panels), COL, axis=0)
    inverse = lax.all_gather(diag_inverse[8:], COL, axis=0)

    leaves, leaves_half = solve_leaves(spread, leaf_inverse)
    own = spread_over(leaves_half, "z", 8)
    other = lax.ppermute(own, "core", [(0, 1), (1, 0)])
    parts = update_from_leaves(meta, own, other, panels)
    parts = exchange(parts.reshape(NR, 7, 16, 256), ROW)
    even, odd = first_residual(meta, parts, right_sides)
    residual, rest = join_residual(meta, to_owner(even, 0), to_owner(odd, 1))

    residual = exchange(residual, ROW)
    targets = [[(0, 0), (1, 2)], [(2, 4), (3, 6)], [(0, 1), (1, 3), (2, 5), (3, 7)]]
    two, parts = solve_level(residual, inverse, 0, blocks, 0, targets)
    residual, rest = next_residual(exchange(parts, ROW), rest, 2)
    residual = exchange(residual, ROW)
    one, parts = solve_level(residual, inverse, 4, blocks, 8, [[(0, 0), (1, 1)]])
    (residual,) = next_residual(exchange(parts, ROW), rest, 1)
    root = solve_root(exchange(residual, ROW), inverse)
    return jnp.concatenate([leaves, two, one, root], axis=0)


def solution(mesh):
    split = Mesh(mesh.devices.reshape(4, 8, 8, 2), ALL)
    return jax.shard_map(
        per_device,
        mesh=split,
        in_specs=(P(None, ROW, COL), P(None, ROW, COL), P(None, None, COL, ROW), P()),
        out_specs=P(None, COL, ROW),
        check_vma=False,
    )
```

time: 550 us -> 349 us (0.63)
  the two profiles are of different devices: /device:TPU:76 before, /device:TPU:72 now
where the time goes in v2:
time: 349 us; the launch traced here: 348 us
  blocking collectives  228 us (65%)
  waiting for transfers between devices  41.5 us (12%)
  starting transfers between devices  27.7 us (8%)
  Pallas kernels  19.5 us (6%)
  local copies, waits for them, and re-layouts  16.9 us (5%)
  between operations  13.3 us (4%)
    all_to_all x7, blocking collectives, exchange(): return lax.all_to_all(flat, axes, 0, 0, tiled=True).reshape(shape)  228 us
    all_to_all x1, waiting for transfers between devices, exchange(): return lax.all_to_all(flat, axes, 0, 0, tiled=True).reshape(shape)  29.6 us
    ppermute x3, starting transfers between devices, to_owner(): return lax.ppermute(values, ALL, pairs)  15 us
    unnamed x19, local copies, waits for them, and re-layouts  12.4 us
    all_to_all x1, starting transfers between devices, exchange(): return lax.all_to_all(flat, axes, 0, 0, tiled=True).reshape(shape)  10.7 us
    ppermute x3, waiting for transfers between devices, to_owner(): return lax.ppermute(values, ALL, pairs)  9.95 us
  transfers between devices with their start and end apart: 8, of which 5 were waited for; matrix products, arithmetic and copies ran while one was open for 1% of the time, Pallas kernels for 4%

profile of v2, /device:TPU:72, one launch (start us, length us, event | category | flops | bytes accessed | tf_op | source)
XLA Modules:
  0.0 348.0 jit_solution(7379364661200998142)
XLA Ops:
  6.5 2.0 slice.11
  8.7 1.8 slice.12
  10.6 5.9 %collective-permute-start = (bf16[8,16,256]{2,1,0:T(8,128)(2,1)S(1)}, bf16[8,16,256]{2,1,0:T(8,128)(2,1)S(1)}, u32[]{:S(2)}, u32[]{:S(2)}) collective-permute-start(bf16[8,16,256]{2,1,0:T(8,128)(2,1)S(1)} %slice.15), channel_id=1, source_target_pairs={{0,0},{1,32},{2,64},{3,96},{4,128},{5,160},{6,192},{7,224},{8,256}... | collective-permute-start | bytes 196616 | tf_op jit(solution)/shard_map/ppermute | solution.py:275
  17.0 5.6 %collective-permute-done = bf16[8,16,256]{2,1,0:T(8,128)(2,1)S(1)} collective-permute-done((bf16[8,16,256]{2,1,0:T(8,128)(2,1)S(1)}, bf16[8,16,256]{2,1,0:T(8,128)(2,1)S(1)}, u32[]{:S(2)}, u32[]{:S(2)}) %collective-permute-start) | collective-permute-done | bytes 65568 | tf_op jit(solution)/shard_map/ppermute | solution.py:275
  22.6 3.8 %select_upper.1 = bf16[10,256,128]{2,1,0:T(8,128)(2,1)} custom-call(s32[676]{0:T(1024)S(1)} %concatenate.6.meta_ref, bf16[14,3,256,128]{3,2,1,0:T(8,128)(2,1)S(1)} %copy-done.4), custom_call_target="tpu_custom_call" | custom-call | tf_op jit(solution)/shard_map/select_upper/pallas_call | solution.py:53
  26.7 63.5 %all_to_all.40 = bf16[32,128,256]{2,1,0:T(8,128)(2,1)} all-to-all(bf16[32,128,256]{2,1,0:T(8,128)(2,1)S(1)} %broadcast_in_dim.17), channel_id=1, replica_groups=mesh['x'=4,'y'=8,'z'=8,'core'=2] {'x','y'}, dimensions={0} | all-to-all | bytes 4194304 | tf_op jit(solution)/shard_map/all_to_all | solution.py:264
  90.2 3.5 %copy-done.5 = bf16[128,128,256]{2,1,0:T(8,128)(2,1)S(1)} copy-done((bf16[128,128,256]{2,1,0:T(8,128)(2,1)S(1)}, bf16[128,128,256]{2,1,0:T(8,128)(2,1)}, u32[]{:S(2)}) %copy-start.5) | copy-done | bytes 8388632
  93.8 1.6 copy-done.6
  95.4 4.3 %solve_leaves.1 = (f32[8,32,128]{2,1,0:T(8,128)S(1)}, bf16[8,32,128]{2,1,0:T(8,128)(2,1)S(1)}) custom-call(bf16[32,8,16,256]{3,2,1,0:T(8,128)(2,1)S(1)} %bitcast.28, bf16[16,8,128,256]{3,2,1,0:T(8,128)(2,1)S(1)} %bitcast.27), custom_call_target="tpu_custom_call" | custom-call | tf_op jit(solution)/shard_map/solve_leaves/pallas_call | solution.py:76
  99.8 31.0 %all_to_all.41 = bf16[8,256,128]{2,1,0:T(8,128)(2,1)S(1)} all-to-all(bf16[8,256,128]{2,1,0:T(8,128)(2,1)S(1)} %broadcast_in_dim.19), channel_id=1, replica_groups=mesh['x'=4,'y'=8,'z'=8,'core'=2] {'z'}, dimensions={0} | all-to-all | bytes 1048576 | tf_op jit(solution)/shard_map/all_to_all | solution.py:264
  130.7 1.9 collective-permute-start.1
  132.7 1.9 collective-permute-done.1.b_ref
  134.5 2.4 update_from_leaves.1
  136.9 50.9 %all_to_all.42 = bf16[32,112,256]{2,1,0:T(8,128)(2,1)S(1)} all-to-all(bf16[32,112,256]{2,1,0:T(8,128)(2,1)S(1)} %bitcast.30), channel_id=1, replica_groups=mesh['x'=4,'y'=8,'z'=8,'core'=2] {'x','y'}, dimensions={0} | all-to-all | bytes 3670016 | tf_op jit(solution)/shard_map/all_to_all | solution.py:264
  187.9 0.8 first_residual.1
  188.7 3.2 collective-permute-start.2
  191.9 5.9 %collective-permute-start.3 = (f32[7,16,128]{2,1,0:T(8,128)S(1)}, f32[7,16,128]{2,1,0:T(8,128)S(1)}, u32[]{:S(2)}, u32[]{:S(2)}) collective-permute-start(f32[7,16,128]{2,1,0:T(8,128)S(1)} %get-tuple-element.22), channel_id=1, source_target_pairs={{0,16},{1,48},{2,80},{3,112},{4,144},{5,176},{6,208},{7,240},{8,27... | collective-permute-start | bytes 172040 | tf_op jit(solution)/shard_map/ppermute | solution.py:275
  197.8 2.3 collective-permute-done.2.a_ref
  200.2 2.0 collective-permute-done.3.b_ref
  202.2 1.7 join_residual.1
  203.9 10.7 %all-to-all-start.3 = ((bf16[32,128,128]{2,1,0:T(8,128)(2,1)}), bf16[32,128,128]{2,1,0:T(8,128)(2,1)S(1)}, u32[]{:S(2)}, u32[]{:S(2)}) async-start(bf16[32,128,128]{2,1,0:T(8,128)(2,1)} %bitcast.10), calls=%async_computation.3 | async-start | bytes 2097152 | tf_op jit(solution)/shard_map/all_to_all | solution.py:264
  214.6 29.6 %all-to-all-done.3 = bf16[32,128,128]{2,1,0:T(8,128)(2,1)S(1)} async-done(((bf16[32,128,128]{2,1,0:T(8,128)(2,1)}), bf16[32,128,128]{2,1,0:T(8,128)(2,1)S(1)}, u32[]{:S(2)}, u32[]{:S(2)}) %all-to-all-start.3) | async-done | bytes 1048608 | tf_op jit(solution)/shard_map/all_to_all | solution.py:264
  244.2 3.1 copy-done
  247.2 4.0 %copy-done.2 = bf16[160,256,128]{2,1,0:T(8,128)(2,1)S(1)} copy-done((bf16[160,256,128]{2,1,0:T(8,128)(2,1)S(1)}, bf16[160,256,128]{2,1,0:T(8,128)(2,1)}, u32[]{:S(2)}) %copy-start.2) | copy-done | bytes 10485784
  251.2 4.3 %solve_level.2 = (f32[4,32,128]{2,1,0:T(8,128)S(1)}, bf16[32,3,32,128]{3,2,1,0:T(8,128)(2,1)S(1)}) custom-call(bf16[32,4,32,128]{3,2,1,0:T(8,128)(2,1)S(1)} %bitcast.31, bf16[16,7,128,256]{3,2,1,0:T(8,128)(2,1)S(1)} %bitcast.22, bf16[16,10,256,128]{3,2,1,0:T(8,128)(2,1)S(1)} %bitcast.25), custom_call_target="tpu_custom_call" | custom-call | tf_op jit(solution)/shard_map/solve_level/pallas_call | solution.py:209
  255.5 28.9 %all_to_all.43 = bf16[32,96,128]{2,1,0:T(8,128)(2,1)S(1)} all-to-all(bf16[32,96,128]{2,1,0:T(8,128)(2,1)S(1)} %bitcast.39), channel_id=1, replica_groups=mesh['x'=4,'y'=8,'z'=8,'core'=2] {'x','y'}, dimensions={0} | all-to-all | bytes 1572864 | tf_op jit(solution)/shard_map/all_to_all | solution.py:264
  284.6 22.1 %all_to_all.44 = bf16[32,64,128]{2,1,0:T(8,128)(2,1)S(1)} all-to-all(bf16[32,64,128]{2,1,0:T(8,128)(2,1)S(1)} %bitcast.40), channel_id=1, replica_groups=mesh['x'=4,'y'=8,'z'=8,'core'=2] {'x','y'}, dimensions={0} | all-to-all | bytes 1048576 | tf_op jit(solution)/shard_map/all_to_all | solution.py:264
  306.7 1.5 solve_level.3
  308.2 16.4 %all_to_all.45 = bf16[32,32,128]{2,1,0:T(8,128)(2,1)S(1)} all-to-all(bf16[32,32,128]{2,1,0:T(8,128)(2,1)S(1)} %bitcast.41), channel_id=1, replica_groups=mesh['x'=4,'y'=8,'z'=8,'core'=2] {'x','y'}, dimensions={0} | all-to-all | bytes 524288 | tf_op jit(solution)/shard_map/all_to_all | solution.py:264
  324.7 15.6 %all_to_all.46 = bf16[32,32,128]{2,1,0:T(8,128)(2,1)S(1)} all-to-all(bf16[32,32,128]{2,1,0:T(8,128)(2,1)S(1)} %bitcast.37), channel_id=1, replica_groups=mesh['x'=4,'y'=8,'z'=8,'core'=2] {'x','y'}, dimensions={0} | all-to-all | bytes 524288 | tf_op jit(solution)/shard_map/all_to_all | solution.py:264
  340.3 0.4 solve_root.1
  340.8 0.7 pad_maximum_fusion
  (31 shorter events, 1.2 us)
Async XLA Ops:
  6.5 4.0 %copy-start.7 = (f32[15,16,256]{2,1,0:T(8,128)S(1)}, f32[15,16,256]{2,1,0:T(8,128)}, u32[]{:S(2)}) copy-start(f32[15,16,256]{2,1,0:T(8,128)} %b_ref.1) | copy-start | bytes 737284
  6.5 10.0 %copy-start.8 = (s32[14,16,3]{1,0,2:T(8,128)S(1)}, s32[14,16,3]{1,0,2:T(8,128)}, u32[]{:S(2)}) copy-start(s32[14,16,3]{1,0,2:T(8,128)} %param.7) | copy-start | bytes 8068
  6.5 16.1 %copy-start.4 = (bf16[14,3,256,128]{3,2,1,0:T(8,128)(2,1)S(1)}, bf16[14,3,256,128]{3,2,1,0:T(8,128)(2,1)}, u32[]{:S(2)}) copy-start(bf16[14,3,256,128]{3,2,1,0:T(8,128)(2,1)} %p_ref.3) | copy-start | bytes 8257540
  6.5 83.7 %all-gather.7.cloned.1.call-start = ((), (), s32[]{:S(2)}) async-start(), calls=%async_computation.8 | async-start | bytes 8912896 | tf_op jit(solution)/shard_map/all_gather | solution.py:282
  8.6 205.9 %all-gather.9.cloned.1.call-start = ((), (), s32[]{:S(2)}) async-start(), calls=%async_computation.9 | async-start | bytes 7798784 | tf_op jit(solution)/shard_map/all_gather | solution.py:292
  10.5 204.0 %all-gather.11.cloned.1.call-start = ((), (), s32[]{:S(2)}) async-start(), calls=%async_computation.10 | async-start | bytes 11141120 | tf_op jit(solution)/shard_map/all_gather | solution.py:291
  10.6 12.0 %collective-permute-start = (bf16[8,16,256]{2,1,0:T(8,128)(2,1)S(1)}, bf16[8,16,256]{2,1,0:T(8,128)(2,1)S(1)}, u32[]{:S(2)}, u32[]{:S(2)}) collective-permute-start(bf16[8,16,256]{2,1,0:T(8,128)(2,1)S(1)} %slice.15), channel_id=1, source_target_pairs={{0,0},{1,32},{2,64},{3,96},{4,128},{5,160},{6,192},{7,224},{8,256}... | collective-permute-start | bytes 196616 | tf_op jit(solution)/shard_map/ppermute | solution.py:275
  90.2 3.5 %copy-start.5 = (bf16[128,128,256]{2,1,0:T(8,128)(2,1)S(1)}, bf16[128,128,256]{2,1,0:T(8,128)(2,1)}, u32[]{:S(2)}) copy-start(bf16[128,128,256]{2,1,0:T(8,128)(2,1)} %all-gather.7.cloned.1.call-done) | copy-start | bytes 25165828
  93.8 1.6 copy-start.6
  130.7 3.8 %collective-permute-start.1 = (bf16[8,8,32,128]{3,2,1,0:T(8,128)(2,1)S(1)}, bf16[8,8,32,128]{3,2,1,0:T(8,128)(2,1)S(1)}, u32[]{:S(2)}, u32[]{:S(2)}) collective-permute-start(bf16[8,8,32,128]{3,2,1,0:T(8,128)(2,1)S(1)} %bitcast.33), channel_id=1, source_target_pairs={{0,1},{1,0},{2,3},{3,2},{4,5},{5,4},{6,7},{7,6},{8,9},{9,8},{10,11... | collective-permute-start | bytes 1572872 | tf_op jit(solution)/shard_map/ppermute | solution.py:296
  188.7 11.4 %collective-permute-start.2 = (f32[7,16,128]{2,1,0:T(8,128)S(1)}, f32[7,16,128]{2,1,0:T(8,128)S(1)}, u32[]{:S(2)}, u32[]{:S(2)}) collective-permute-start(f32[7,16,128]{2,1,0:T(8,128)S(1)} %get-tuple-element.21), channel_id=1, source_target_pairs={{0,0},{1,32},{2,64},{3,96},{4,128},{5,160},{6,192},{7,224},{8,256}... | collective-permute-start | bytes 172040 | tf_op jit(solution)/shard_map/ppermute | solution.py:275
  191.9 10.3 %collective-permute-start.3 = (f32[7,16,128]{2,1,0:T(8,128)S(1)}, f32[7,16,128]{2,1,0:T(8,128)S(1)}, u32[]{:S(2)}, u32[]{:S(2)}) collective-permute-start(f32[7,16,128]{2,1,0:T(8,128)S(1)} %get-tuple-element.22), channel_id=1, source_target_pairs={{0,16},{1,48},{2,80},{3,112},{4,144},{5,176},{6,208},{7,240},{8,27... | collective-permute-start | bytes 172040 | tf_op jit(solution)/shard_map/ppermute | solution.py:275
  203.9 40.3 %all-to-all-start.3 = ((bf16[32,128,128]{2,1,0:T(8,128)(2,1)}), bf16[32,128,128]{2,1,0:T(8,128)(2,1)S(1)}, u32[]{:S(2)}, u32[]{:S(2)}) async-start(bf16[32,128,128]{2,1,0:T(8,128)(2,1)} %bitcast.10), calls=%async_computation.3 | async-start | bytes 2097152 | tf_op jit(solution)/shard_map/all_to_all | solution.py:264
  244.2 3.1 copy-start
  247.2 4.0 %copy-start.2 = (bf16[160,256,128]{2,1,0:T(8,128)(2,1)S(1)}, bf16[160,256,128]{2,1,0:T(8,128)(2,1)}, u32[]{:S(2)}) copy-start(bf16[160,256,128]{2,1,0:T(8,128)(2,1)} %all-gather.11.cloned.1.call-done) | copy-start | bytes 31457284
  251.2 55.5 %copy-start.1 = (bf16[112,128,256]{2,1,0:T(8,128)(2,1)S(1)}, bf16[112,128,256]{2,1,0:T(8,128)(2,1)}, u32[]{:S(2)}) copy-start(bf16[112,128,256]{2,1,0:T(8,128)(2,1)} %all-gather.9.cloned.1.call-done) | copy-start | bytes 22020100
  251.2 55.5 %copy-start.3 = (bf16[160,256,128]{2,1,0:T(8,128)(2,1)S(1)}, bf16[160,256,128]{2,1,0:T(8,128)(2,1)}, u32[]{:S(2)}) copy-start(bf16[160,256,128]{2,1,0:T(8,128)(2,1)} %all-gather.11.cloned.1.call-done) | copy-start | bytes 31457284
Sparse Core Ops, SparseCore 0:
  9.5 60.7 all-gather.6
  72.4 64.2 all-gather.8
  138.9 73.9 all-gather.10

commit v3 on v2

v3 whole, which is shorter than its diff:
```python
import jax
import jax.numpy as jnp
from jax import lax
from jax.experimental import pallas as pl
from jax.experimental.pallas import tpu as pltpu
from jax.sharding import Mesh
from jax.sharding import PartitionSpec as P

ROW = ("x", "y")
COL = ("z", "core")
ALL = ("x", "y", "z", "core")
NR = 32
NC = 16
VMEM_LIMIT = 24 * 1024 * 1024
F32 = jnp.float32
BF16 = jnp.bfloat16
VMEM = pl.BlockSpec(memory_space=pltpu.VMEM)
SMEM = pl.BlockSpec(memory_space=pltpu.SMEM)
HBM = pl.BlockSpec(memory_space=pltpu.HBM)


def params(n=1):
    return pltpu.CompilerParams(
        vmem_limit_bytes=VMEM_LIMIT, dimension_semantics=("arbitrary",) * n
    )


def dot_t(a, b):
    return lax.dot_general(a, b, (((1,), (1,)), ((), ())), preferred_element_type=F32)


def slot_of(meta, source, target):
    base = 4 + (source * NC + meta[0]) * 3
    second = jnp.where(meta[base + 1] == target, 1, 0)
    slot = jnp.where(meta[base + 2] == target, 2, second)
    return slot, meta[base + slot] == target


def gathered_block(b):
    is_low = b < 8
    source = jnp.where(is_low, 8 + b // 2, 4 + b)
    target = jnp.where(is_low & (b % 2 == 0), 12 + b // 4, 14)
    return source, target


def stack_upper(meta, inverse, panels, first_node, nodes, first_block, blocks):
    def kernel(meta_ref, d_ref, p_ref, o_ref):
        i = pl.program_id(0)

        @pl.when(i < nodes)
        def _():
            o_ref[...] = d_ref[...]

        @pl.when(i >= nodes)
        def _():
            _, found = slot_of(meta_ref, *gathered_block(first_block + i - nodes))
            block = p_ref[0, 0]
            block = jnp.where(found, block, jnp.zeros_like(block))
            o_ref[0, :, :128] = block[:128]
            o_ref[0, :, 128:] = block[128:]

    def index(i, meta_ref):
        source, target = gathered_block(first_block + jnp.maximum(i - nodes, 0))
        slot, _ = slot_of(meta_ref, source, target)
        return source, slot, 0, 0

    return pl.pallas_call(
        kernel,
        grid_spec=pltpu.PrefetchScalarGridSpec(
            num_scalar_prefetch=1,
            grid=(nodes + blocks,),
            in_specs=[
                pl.BlockSpec(
                    (1, 128, 256), lambda i, m: (first_node + jnp.minimum(i, nodes - 1), 0, 0)
                ),
                pl.BlockSpec((1, 1, 256, 128), index),
            ],
            out_specs=pl.BlockSpec((1, 128, 256), lambda i, m: (i, 0, 0)),
        ),
        out_shape=jax.ShapeDtypeStruct((nodes + blocks, 128, 256), BF16),
        compiler_params=params(),
        name="stack_upper",
    )(meta, inverse, panels)


def solve_leaves(spread, inverse):
    def kernel(b_ref, d_hbm, x_ref, h_ref, d_ref, sem):
        copies = [
            pltpu.make_async_copy(d_hbm.at[:, n], d_ref.at[:, n], sem.at[n]) for n in range(8)
        ]
        for copy in copies:
            copy.start()
        for n in range(8):
            copies[n].wait()
            acc = jnp.zeros((32, 128), F32)
            for c in range(NC):
                left = b_ref[2 * c : 2 * c + 2, n].reshape(32, 256)
                acc = acc + dot_t(left, d_ref[c, n])
            x_ref[n] = acc
            half = acc.astype(BF16)
            for z in range(8):
                h_ref[z, n] = half

    return pl.pallas_call(
        kernel,
        in_specs=[VMEM, HBM],
        out_specs=[VMEM, VMEM],
        out_shape=[
            jax.ShapeDtypeStruct((8, 32, 128), F32),
            jax.ShapeDtypeStruct((8, 8, 32, 128), BF16),
        ],
        scratch_shapes=[
            pltpu.VMEM((NC, 8, 128, 256), BF16),
            pltpu.SemaphoreType.DMA((8,)),
        ],
        compiler_params=params(0),
        name="solve_leaves",
    )(spread, inverse)


def update_from_leaves(meta, own, other, panels, right):
    def kernel(meta_ref, a_ref, b_ref, p_ref, r_ref, o_ref):
        core, row = meta_ref[1], meta_ref[2]
        for t in range(7):
            target = 8 + t
            if t < 4:
                sources = range(2 * t, 2 * t + 2)
            elif t < 6:
                sources = range(4 * (t - 4), 4 * (t - 4) + 4)
            else:
                sources = range(8)
            blocks = []
            for s in sources:
                slot, found = slot_of(meta_ref, s, target)
                block = p_ref[s, slot]
                blocks.append(jnp.where(found, block, jnp.zeros_like(block)))
            for parity, x_ref in ((core, a_ref), (1 - core, b_ref)):
                acc = jnp.zeros((256, 256), F32)
                for s, block in zip(sources, blocks, strict=True):
                    acc = acc + dot_t(x_ref[:, s].reshape(256, 128), block)
                for half in range(2):
                    value = acc[:, 128 * half : 128 * half + 128].astype(BF16)
                    o_ref[:, pl.ds(parity, 1), half, t] = value.reshape(8, 1, 32, 128)
        z, parity = row // 4, (row // 2) % 2
        start = pl.multiple_of(16 * (row % 2), 16)
        for half in range(2):
            for t in range(7):
                part = o_ref[z, parity, half, t, pl.ds(start, 16), :].astype(F32)
                part = part - r_ref[8 + t, :, 128 * half : 128 * half + 128]
                o_ref[z, parity, half, t, pl.ds(start, 16), :] = part.astype(BF16)

    return pl.pallas_call(
        kernel,
        grid=(1,),
        in_specs=[
            SMEM,
            VMEM,
            VMEM,
            pl.BlockSpec((8, 3, 256, 128), lambda i: (0, 0, 0, 0)),
            VMEM,
        ],
        out_specs=VMEM,
        out_shape=jax.ShapeDtypeStruct((8, 2, 2, 7, 32, 128), BF16),
        compiler_params=params(),
        name="update_from_leaves",
    )(meta, own, other, panels, right)


def first_residual(parts):
    def kernel(p_ref, o_ref):
        o_ref[...] = (-jnp.sum(p_ref[...].astype(F32), axis=0)).astype(BF16)

    return pl.pallas_call(
        kernel,
        in_specs=[VMEM],
        out_specs=VMEM,
        out_shape=jax.ShapeDtypeStruct((7, 32, 128), BF16),
        compiler_params=params(0),
        name="first_residual",
    )(parts)


def solve_node(x_ref, d_ref, n, place):
    acc = jnp.zeros((32, 128), F32)
    for c in range(NC):
        left = jnp.concatenate([x_ref[2 * c, n], x_ref[2 * c + 1, n]], axis=1)
        acc = acc + dot_t(left, d_ref[c, place])
    return acc


def update_above(solved, w_ref, c, nodes, targets, o_ref):
    for t, terms in enumerate(targets):
        for half in range(2):
            acc = jnp.zeros((32, 128), F32)
            for s, b in terms:
                block = w_ref[c, nodes + b, :, 128 * half : 128 * half + 128]
                acc = acc + dot_t(solved[s], block)
            o_ref[2 * c + half, t] = acc.astype(BF16)


def solve_level(residual, weights, nodes, targets, stream):
    groups = 4

    def body(x_ref, w_ref, s_ref, o_ref, wait):
        solved = []
        for n in range(nodes):
            wait(n)
            x = solve_node(x_ref, w_ref, n, n)
            s_ref[n] = x
            solved.append(x.astype(BF16))
        for g in range(groups):
            wait(nodes + g)
            for c in range(g * NC // groups, (g + 1) * NC // groups):
                update_above(solved, w_ref, c, nodes, targets, o_ref)

    def direct(x_ref, w_ref, s_ref, o_ref):
        body(x_ref, w_ref, s_ref, o_ref, lambda i: None)

    def streamed(x_ref, w_hbm, s_ref, o_ref, w_ref, sem):
        pieces = [(slice(None), n) for n in range(nodes)]
        for g in range(groups):
            pieces.append((pl.ds(g * NC // groups, NC // groups), slice(nodes, None)))
        copies = [
            pltpu.make_async_copy(w_hbm.at[piece], w_ref.at[piece], sem.at[i])
            for i, piece in enumerate(pieces)
        ]
        for copy in copies:
            copy.start()
        body(x_ref, w_ref, s_ref, o_ref, lambda i: copies[i].wait())

    scratch = [
        pltpu.VMEM(weights.shape, BF16),
        pltpu.SemaphoreType.DMA((nodes + groups,)),
    ]
    return pl.pallas_call(
        streamed if stream else direct,
        in_specs=[VMEM, HBM if stream else VMEM],
        out_specs=[VMEM, VMEM],
        out_shape=[
            jax.ShapeDtypeStruct((nodes, 32, 128), F32),
            jax.ShapeDtypeStruct((NR, len(targets), 32, 128), BF16),
        ],
        scratch_shapes=scratch if stream else [],
        compiler_params=params(0),
        name="solve_level",
    )(residual, weights)


def solve_root(residual, inverse):
    def kernel(x_ref, d_ref, s_ref):
        s_ref[0] = solve_node(x_ref, d_ref, 0, 2)

    return pl.pallas_call(
        kernel,
        in_specs=[VMEM, VMEM],
        out_specs=VMEM,
        out_shape=jax.ShapeDtypeStruct((1, 32, 128), F32),
        compiler_params=params(0),
        name="solve_root",
    )(residual, inverse)


def next_residual(parts, rest, nodes):
    count = rest.shape[0]
    after = count - nodes

    def kernel(p_ref, rest_ref, o_ref, *later):
        residual = rest_ref[...].astype(F32) - jnp.sum(p_ref[...].astype(F32), axis=0)
        half = residual[:nodes].astype(BF16)
        for r in range(NR):
            o_ref[r] = half
        if after:
            later[0][...] = residual[nodes:]

    out_shape = [jax.ShapeDtypeStruct((NR, nodes, 32, 128), BF16)]
    if after:
        out_shape.append(jax.ShapeDtypeStruct((after, 32, 128), F32))
    return pl.pallas_call(
        kernel,
        in_specs=[VMEM, VMEM],
        out_specs=[VMEM] * len(out_shape),
        out_shape=out_shape,
        compiler_params=params(0),
        name="next_residual",
    )(parts, rest)


def exchange(values, axes):
    shape = values.shape
    flat = values.reshape(shape[0], -1, shape[-1])
    return lax.all_to_all(flat, axes, 0, 0, tiled=True).reshape(shape)


def spread_over(values, axes, size):
    return exchange(jnp.broadcast_to(values[None], (size,) + values.shape), axes)


def to_owner(values):
    pairs = [
        (r * NC + c, (2 * c + r % 2) * NC + r // 2) for r in range(NR) for c in range(NC)
    ]
    return lax.ppermute(values, ALL, pairs)


def per_device(right_sides, diag_inverse, panels, block_map):
    row = lax.axis_index(ROW)
    col = lax.axis_index(COL)
    core = lax.axis_index("core")
    leaf_inverse = lax.all_gather(diag_inverse[:8], COL, axis=0)
    moved = to_owner(right_sides[:8].astype(BF16))
    spread = spread_over(moved, ROW, NR)

    zero = jnp.zeros((), jnp.int32)
    meta = jnp.concatenate(
        [jnp.stack([col, core, row, zero]).astype(jnp.int32), block_map.reshape(-1)]
    )
    meta, _ = lax.optimization_barrier((meta, moved))
    stack_two = stack_upper(meta, diag_inverse, panels, 8, 4, 0, 8)
    stack_one = stack_upper(meta, diag_inverse, panels, 12, 3, 8, 2)

    leaves, copies = solve_leaves(spread, leaf_inverse)
    own = exchange(copies, "z")
    other = lax.ppermute(own, "core", [(0, 1), (1, 0)])
    stack_two, stack_one, own = lax.optimization_barrier((stack_two, stack_one, own))
    weights_two = lax.all_gather(stack_two, COL, axis=0)
    weights_one = lax.all_gather(stack_one, COL, axis=0)
    parts = update_from_leaves(meta, own, other, panels, right_sides)
    parts = exchange(parts.reshape(NR, 7, 32, 128), ROW)
    residual = to_owner(first_residual(parts))

    targets = [[(0, 0), (1, 2)], [(2, 4), (3, 6)], [(0, 1), (1, 3), (2, 5), (3, 7)]]
    spread = spread_over(residual[:4], ROW, NR)
    two, parts = solve_level(spread, weights_two, 4, targets, True)
    spread, rest = next_residual(exchange(parts, ROW), residual[4:], 2)
    targets = [[(0, 1), (1, 2)]]
    one, parts = solve_level(exchange(spread, ROW), weights_one, 2, targets, False)
    (spread,) = next_residual(exchange(parts, ROW), rest, 1)
    root = solve_root(exchange(spread, ROW), weights_one)
    return jnp.concatenate([leaves, two, one, root], axis=0)


def solution(mesh):
    split = Mesh(mesh.devices.reshape(4, 8, 8, 2), ALL)
    return jax.shard_map(
        per_device,
        mesh=split,
        in_specs=(P(None, ROW, COL), P(None, ROW, COL), P(None, None, COL, ROW), P()),
        out_specs=P(None, COL, ROW),
        check_vma=False,
    )
```

time: 349 us -> 337 us (0.966)
  blocking collectives: 228 us -> 183 us
  waiting for transfers between devices: 41.5 us -> 62.1 us
  Pallas kernels: 19.5 us -> 26.5 us
  local copies, waits for them, and re-layouts: 16.9 us -> 21 us
    all_to_all x7 -> x5, blocking collectives: 228 us -> 183 us  [exchange(): return lax.all_to_all(flat, axes, 0, 0, tiled=True).reshape(shape)]
    all_to_all x1 -> x3, waiting for transfers between devices: 29.6 us -> 45.4 us  [exchange(): return lax.all_to_all(flat, axes, 0, 0, tiled=True).reshape(shape)]
    all_to_all x1 -> x3, starting transfers between devices: 10.7 us -> 18.8 us  [exchange(): return lax.all_to_all(flat, axes, 0, 0, tiled=True).reshape(shape)]
    pallas_call x7, Pallas kernels: 18.9 us -> 25.1 us  [the longest x2 11.2 us: solve_level(): pl.pallas_call(streamed if stream else direct, in_specs=[VMEM, HBM if str...]
    ppermute x3 -> x2, starting transfers between devices: 15 us -> 9.37 us  [to_owner(): return lax.ppermute(values, ALL, pairs)]
    unnamed x19 -> x29, local copies, waits for them, and re-layouts: 12.4 us -> 17.5 us
    ppermute x3 -> x2, waiting for transfers between devices: 9.95 us -> 14.1 us  [to_owner(): return lax.ppermute(values, ALL, pairs)]
  transfers between devices with their start and end apart: 8 -> 9, of which waited for: 5 -> 6; matrix products, arithmetic and copies ran while one was open for 1% -> 1% of each run, Pallas kernels for 4% -> 5%
where the time goes in v3:
time: 337 us; the launch traced here: 336 us
  blocking collectives  183 us (54%)
  waiting for transfers between devices  62.1 us (18%)
  starting transfers between devices  30.2 us (9%)
  Pallas kernels  26.5 us (8%)
  local copies, waits for them, and re-layouts  21 us (6%)
  between operations  13.3 us (4%)
    all_to_all x5, blocking collectives, exchange(): return lax.all_to_all(flat, axes, 0, 0, tiled=True).reshape(shape)  183 us
    all_to_all x3, waiting for transfers between devices, exchange(): return lax.all_to_all(flat, axes, 0, 0, tiled=True).reshape(shape)  45.4 us
    all_to_all x3, starting transfers between devices, exchange(): return lax.all_to_all(flat, axes, 0, 0, tiled=True).reshape(shape)  18.8 us
    unnamed x29, local copies, waits for them, and re-layouts  17.5 us
    ppermute x2, waiting for transfers between devices, to_owner(): return lax.ppermute(values, ALL, pairs)  14.1 us
    pallas_call x2, Pallas kernels, solve_level(): pl.pallas_call(streamed if stream else direct, in_specs=[VMEM, HBM if str...  11.2 us
    ppermute x2, starting transfers between devices, to_owner(): return lax.ppermute(values, ALL, pairs)  9.37 us
  transfers between devices with their start and end apart: 9, of which 6 were waited for; matrix products, arithmetic and copies ran while one was open for 1% of the time, Pallas kernels for 5%

profile of v3, /device:TPU:72, one launch (start us, length us, event | category | flops | bytes accessed | tf_op | source)
XLA Modules:
  0.0 336.2 jit_solution(17028866068206609635)
XLA Ops:
  6.5 1.9 slice.14
  8.4 0.9 slice.21
  9.4 5.9 %collective-permute-start = (bf16[8,16,256]{2,1,0:T(8,128)(2,1)S(1)}, bf16[8,16,256]{2,1,0:T(8,128)(2,1)S(1)}, u32[]{:S(2)}, u32[]{:S(2)}) collective-permute-start(bf16[8,16,256]{2,1,0:T(8,128)(2,1)S(1)} %slice.21), channel_id=1, source_target_pairs={{0,0},{1,32},{2,64},{3,96},{4,128},{5,160},{6,192},{7,224},{8,256}... | collective-permute-start | bytes 196616 | tf_op jit(solution)/shard_map/ppermute | solution.py:302
  15.3 6.1 %collective-permute-done = bf16[8,16,256]{2,1,0:T(8,128)(2,1)S(1)} collective-permute-done((bf16[8,16,256]{2,1,0:T(8,128)(2,1)S(1)}, bf16[8,16,256]{2,1,0:T(8,128)(2,1)S(1)}, u32[]{:S(2)}, u32[]{:S(2)}) %collective-permute-start) | collective-permute-done | bytes 65568 | tf_op jit(solution)/shard_map/ppermute | solution.py:302
  21.6 63.5 %all_to_all.40 = bf16[32,128,256]{2,1,0:T(8,128)(2,1)} all-to-all(bf16[32,128,256]{2,1,0:T(8,128)(2,1)S(1)} %broadcast_in_dim.17), channel_id=1, replica_groups=mesh['x'=4,'y'=8,'z'=8,'core'=2] {'x','y'}, dimensions={0} | all-to-all | bytes 4194304 | tf_op jit(solution)/shard_map/all_to_all | solution.py:291
  85.1 3.4 %copy-done.4 = bf16[128,128,256]{2,1,0:T(8,128)(2,1)S(1)} copy-done((bf16[128,128,256]{2,1,0:T(8,128)(2,1)S(1)}, bf16[128,128,256]{2,1,0:T(8,128)(2,1)}, u32[]{:S(2)}) %copy-start.4) | copy-done | bytes 8388632
  88.5 1.6 copy-done.5
  90.1 5.9 %solve_leaves.1 = (f32[8,32,128]{2,1,0:T(8,128)S(1)}, bf16[8,8,32,128]{3,2,1,0:T(8,128)(2,1)S(1)}) custom-call(bf16[32,8,16,256]{3,2,1,0:T(8,128)(2,1)S(1)} %bitcast.26, bf16[16,8,128,256]{3,2,1,0:T(8,128)(2,1)S(1)} %bitcast.25), custom_call_target="tpu_custom_call" | custom-call | tf_op jit(solution)/shard_map/solve_leaves/pallas_call | solution.py:104
  97.5 8.7 %all-to-all-start.1 = ((bf16[8,256,128]{2,1,0:T(8,128)(2,1)}), bf16[8,256,128]{2,1,0:T(8,128)(2,1)S(1)}, u32[]{:S(2)}, u32[]{:S(2)}) async-start(bf16[8,256,128]{2,1,0:T(8,128)(2,1)} %bitcast.37), calls=%async_computation.1 | async-start | bytes 1048576 | tf_op jit(solution)/shard_map/all_to_all | solution.py:291
  106.7 1.2 copy-done.6
  107.9 4.5 %stack_upper.2 = bf16[12,128,256]{2,1,0:T(8,128)(2,1)} custom-call(s32[676]{0:T(1024)S(1)} %concatenate.6.meta_ref, bf16[15,128,256]{2,1,0:T(8,128)(2,1)S(1)} %copy-done.6, bf16[14,3,256,128]{3,2,1,0:T(8,128)(2,1)S(1)} %copy-done), custom_call_target="tpu_custom_call" | custom-call | tf_op jit(solution)/shard_map/stack_upper/pallas_call | solution.py:67
  112.4 1.2 copy-done.7
  113.6 0.8 stack_upper.3
  115.2 6.8 %all-to-all-done.1 = bf16[8,256,128]{2,1,0:T(8,128)(2,1)S(1)} async-done(((bf16[8,256,128]{2,1,0:T(8,128)(2,1)}), bf16[8,256,128]{2,1,0:T(8,128)(2,1)S(1)}, u32[]{:S(2)}, u32[]{:S(2)}) %all-to-all-start.1) | async-done | bytes 524320 | tf_op jit(solution)/shard_map/all_to_all | solution.py:291
  122.7 1.9 collective-permute-start.1
  124.6 1.9 collective-permute-done.1.b_ref
  126.5 2.4 update_from_leaves.1
  128.9 51.4 %all_to_all.41 = bf16[32,224,128]{2,1,0:T(8,128)(2,1)S(1)} all-to-all(bf16[32,224,128]{2,1,0:T(8,128)(2,1)S(1)} %bitcast.27), channel_id=1, replica_groups=mesh['x'=4,'y'=8,'z'=8,'core'=2] {'x','y'}, dimensions={0} | all-to-all | bytes 3670016 | tf_op jit(solution)/shard_map/all_to_all | solution.py:291
  180.6 3.4 %collective-permute-start.2 = (bf16[7,32,128]{2,1,0:T(8,128)(2,1)S(1)}, bf16[7,32,128]{2,1,0:T(8,128)(2,1)S(1)}, u32[]{:S(2)}, u32[]{:S(2)}) collective-permute-start(bf16[7,32,128]{2,1,0:T(8,128)(2,1)S(1)} %first_residual.1), channel_id=1, source_target_pairs={{0,0},{1,32},{2,64},{3,96},{4,128},{5,160},{6,192},{7,224},{8,256}... | collective-permute-start | bytes 172040 | tf_op jit(solution)/shard_map/ppermute | solution.py:302
  184.0 8.0 %collective-permute-done.2 = bf16[7,32,128]{2,1,0:T(8,128)(2,1)S(1)} collective-permute-done((bf16[7,32,128]{2,1,0:T(8,128)(2,1)S(1)}, bf16[7,32,128]{2,1,0:T(8,128)(2,1)S(1)}, u32[]{:S(2)}, u32[]{:S(2)}) %collective-permute-start.2) | collective-permute-done | bytes 57376 | tf_op jit(solution)/shard_map/ppermute | solution.py:302
  192.2 36.7 %all_to_all.42 = bf16[32,128,128]{2,1,0:T(8,128)(2,1)S(1)} all-to-all(bf16[32,128,128]{2,1,0:T(8,128)(2,1)S(1)} %broadcast_in_dim.19), channel_id=1, replica_groups=mesh['x'=4,'y'=8,'z'=8,'core'=2] {'x','y'}, dimensions={0} | all-to-all | bytes 2097152 | tf_op jit(solution)/shard_map/all_to_all | solution.py:291
  228.9 4.8 %copy-done.3 = bf16[192,128,256]{2,1,0:T(8,128)(2,1)S(1)} copy-done((bf16[192,128,256]{2,1,0:T(8,128)(2,1)S(1)}, bf16[192,128,256]{2,1,0:T(8,128)(2,1)}, u32[]{:S(2)}) %copy-start.3) | copy-done | bytes 12582936
  233.7 9.3 %solve_level.2 = (f32[4,32,128]{2,1,0:T(8,128)S(1)}, bf16[32,3,32,128]{3,2,1,0:T(8,128)(2,1)}) custom-call(bf16[32,4,32,128]{3,2,1,0:T(8,128)(2,1)S(1)} %bitcast.29, bf16[16,12,128,256]{3,2,1,0:T(8,128)(2,1)S(1)} %bitcast.24), custom_call_target="tpu_custom_call" | custom-call | tf_op jit(solution)/shard_map/solve_level/pallas_call | solution.py:235
  243.0 5.1 %all-to-all-start.4 = ((bf16[32,96,128]{2,1,0:T(8,128)(2,1)}), bf16[32,96,128]{2,1,0:T(8,128)(2,1)S(1)}, u32[]{:S(2)}, u32[]{:S(2)}) async-start(bf16[32,96,128]{2,1,0:T(8,128)(2,1)} %bitcast.13), calls=%async_computation.4 | async-start | bytes 1572864 | tf_op jit(solution)/shard_map/all_to_all | solution.py:291
  248.2 22.1 %all-to-all-done.4 = bf16[32,96,128]{2,1,0:T(8,128)(2,1)S(1)} async-done(((bf16[32,96,128]{2,1,0:T(8,128)(2,1)}), bf16[32,96,128]{2,1,0:T(8,128)(2,1)S(1)}, u32[]{:S(2)}, u32[]{:S(2)}) %all-to-all-start.4) | async-done | bytes 786464 | tf_op jit(solution)/shard_map/all_to_all | solution.py:291
  270.2 0.9 next_residual.2
  271.1 4.9 %all-to-all-start.5 = ((bf16[32,64,128]{2,1,0:T(8,128)(2,1)}), bf16[32,64,128]{2,1,0:T(8,128)(2,1)S(1)}, u32[]{:S(2)}, u32[]{:S(2)}) async-start(bf16[32,64,128]{2,1,0:T(8,128)(2,1)} %bitcast.15), calls=%async_computation.5 | async-start | bytes 1048576 | tf_op jit(solution)/shard_map/all_to_all | solution.py:291
  276.1 16.6 %all-to-all-done.5 = bf16[32,64,128]{2,1,0:T(8,128)(2,1)S(1)} async-done(((bf16[32,64,128]{2,1,0:T(8,128)(2,1)}), bf16[32,64,128]{2,1,0:T(8,128)(2,1)S(1)}, u32[]{:S(2)}, u32[]{:S(2)}) %all-to-all-start.5) | async-done | bytes 524320 | tf_op jit(solution)/shard_map/all_to_all | solution.py:291
  292.7 2.5 copy-done.1
  295.1 1.9 solve_level.3
  297.1 15.6 %all_to_all.43 = bf16[32,32,128]{2,1,0:T(8,128)(2,1)S(1)} all-to-all(bf16[32,32,128]{2,1,0:T(8,128)(2,1)S(1)} %bitcast.38), channel_id=1, replica_groups=mesh['x'=4,'y'=8,'z'=8,'core'=2] {'x','y'}, dimensions={0} | all-to-all | bytes 524288 | tf_op jit(solution)/shard_map/all_to_all | solution.py:291
  312.7 15.4 %all_to_all.44 = bf16[32,32,128]{2,1,0:T(8,128)(2,1)S(1)} all-to-all(bf16[32,32,128]{2,1,0:T(8,128)(2,1)S(1)} %bitcast.35), channel_id=1, replica_groups=mesh['x'=4,'y'=8,'z'=8,'core'=2] {'x','y'}, dimensions={0} | all-to-all | bytes 524288 | tf_op jit(solution)/shard_map/all_to_all | solution.py:291
  (42 shorter events, 5.8 us)
Async XLA Ops:
  6.5 78.6 %all-gather.7.cloned.1.call-start = ((), (), s32[]{:S(2)}) async-start(), calls=%async_computation.8 | async-start | bytes 8912896 | tf_op jit(solution)/shard_map/all_gather | solution.py:309
  9.4 12.0 %collective-permute-start = (bf16[8,16,256]{2,1,0:T(8,128)(2,1)S(1)}, bf16[8,16,256]{2,1,0:T(8,128)(2,1)S(1)}, u32[]{:S(2)}, u32[]{:S(2)}) collective-permute-start(bf16[8,16,256]{2,1,0:T(8,128)(2,1)S(1)} %slice.21), channel_id=1, source_target_pairs={{0,0},{1,32},{2,64},{3,96},{4,128},{5,160},{6,192},{7,224},{8,256}... | collective-permute-start | bytes 196616 | tf_op jit(solution)/shard_map/ppermute | solution.py:302
  85.1 3.4 %copy-start.4 = (bf16[128,128,256]{2,1,0:T(8,128)(2,1)S(1)}, bf16[128,128,256]{2,1,0:T(8,128)(2,1)}, u32[]{:S(2)}) copy-start(bf16[128,128,256]{2,1,0:T(8,128)(2,1)} %all-gather.7.cloned.1.call-done) | copy-start | bytes 25165828
  88.5 1.6 copy-start.5
  90.1 16.1 %copy-start.13 = (s32[14,16,3]{1,0,2:T(8,128)S(1)}, s32[14,16,3]{1,0,2:T(8,128)}, u32[]{:S(2)}) copy-start(s32[14,16,3]{1,0,2:T(8,128)} %param.7) | copy-start | bytes 8068
  90.1 16.6 %copy-start = (bf16[14,3,256,128]{3,2,1,0:T(8,128)(2,1)S(1)}, bf16[14,3,256,128]{3,2,1,0:T(8,128)(2,1)}, u32[]{:S(2)}) copy-start(bf16[14,3,256,128]{3,2,1,0:T(8,128)(2,1)} %p_ref.5) | copy-start | bytes 8257540
  96.0 0.8 copy-start.9
  96.8 0.7 copy-start.11
  97.5 24.5 %all-to-all-start.1 = ((bf16[8,256,128]{2,1,0:T(8,128)(2,1)}), bf16[8,256,128]{2,1,0:T(8,128)(2,1)S(1)}, u32[]{:S(2)}, u32[]{:S(2)}) async-start(bf16[8,256,128]{2,1,0:T(8,128)(2,1)} %bitcast.37), calls=%async_computation.1 | async-start | bytes 1048576 | tf_op jit(solution)/shard_map/all_to_all | solution.py:291
  106.2 122.7 %all-gather.9.cloned.1.call-start = ((), (), s32[]{:S(2)}) async-start(), calls=%async_computation.9 | async-start | bytes 13369344 | tf_op jit(solution)/shard_map/all_gather | solution.py:325
  106.7 1.2 copy-start.6
  107.9 18.6 %copy-start.10 = (f32[15,16,256]{2,1,0:T(8,128)S(1)}, f32[15,16,256]{2,1,0:T(8,128)}, u32[]{:S(2)}) copy-start(f32[15,16,256]{2,1,0:T(8,128)} %r_ref.1) | copy-start | bytes 737284
  112.4 1.2 copy-start.7
  114.4 0.7 copy-start.8
  122.0 154.1 %all-gather.11.cloned.1.call-start = ((), (), s32[]{:S(2)}) async-start(), calls=%async_computation.10 | async-start | bytes 5570560 | tf_op jit(solution)/shard_map/all_gather | solution.py:326
  122.7 3.8 %collective-permute-start.1 = (bf16[8,8,32,128]{3,2,1,0:T(8,128)(2,1)S(1)}, bf16[8,8,32,128]{3,2,1,0:T(8,128)(2,1)S(1)}, u32[]{:S(2)}, u32[]{:S(2)}) collective-permute-start(bf16[8,8,32,128]{3,2,1,0:T(8,128)(2,1)S(1)} %bitcast.31), channel_id=1, source_target_pairs={{0,1},{1,0},{2,3},{3,2},{4,5},{5,4},{6,7},{7,6},{8,9},{9,8},{10,11... | collective-permute-start | bytes 1572872 | tf_op jit(solution)/shard_map/ppermute | solution.py:323
  180.6 11.4 %collective-permute-start.2 = (bf16[7,32,128]{2,1,0:T(8,128)(2,1)S(1)}, bf16[7,32,128]{2,1,0:T(8,128)(2,1)S(1)}, u32[]{:S(2)}, u32[]{:S(2)}) collective-permute-start(bf16[7,32,128]{2,1,0:T(8,128)(2,1)S(1)} %first_residual.1), channel_id=1, source_target_pairs={{0,0},{1,32},{2,64},{3,96},{4,128},{5,160},{6,192},{7,224},{8,256}... | collective-permute-start | bytes 172040 | tf_op jit(solution)/shard_map/ppermute | solution.py:302
  228.9 4.8 %copy-start.3 = (bf16[192,128,256]{2,1,0:T(8,128)(2,1)S(1)}, bf16[192,128,256]{2,1,0:T(8,128)(2,1)}, u32[]{:S(2)}) copy-start(bf16[192,128,256]{2,1,0:T(8,128)(2,1)} %all-gather.9.cloned.1.call-done) | copy-start | bytes 37748740
  243.0 27.2 %all-to-all-start.4 = ((bf16[32,96,128]{2,1,0:T(8,128)(2,1)}), bf16[32,96,128]{2,1,0:T(8,128)(2,1)S(1)}, u32[]{:S(2)}, u32[]{:S(2)}) async-start(bf16[32,96,128]{2,1,0:T(8,128)(2,1)} %bitcast.13), calls=%async_computation.4 | async-start | bytes 1572864 | tf_op jit(solution)/shard_map/all_to_all | solution.py:291
  271.1 21.5 %all-to-all-start.5 = ((bf16[32,64,128]{2,1,0:T(8,128)(2,1)}), bf16[32,64,128]{2,1,0:T(8,128)(2,1)S(1)}, u32[]{:S(2)}, u32[]{:S(2)}) async-start(bf16[32,64,128]{2,1,0:T(8,128)(2,1)} %bitcast.15), calls=%async_computation.5 | async-start | bytes 1048576 | tf_op jit(solution)/shard_map/all_to_all | solution.py:291
  292.7 2.5 copy-start.1
  295.1 33.0 %copy-start.2 = (bf16[80,128,256]{2,1,0:T(8,128)(2,1)S(1)}, bf16[80,128,256]{2,1,0:T(8,128)(2,1)}, u32[]{:S(2)}) copy-start(bf16[80,128,256]{2,1,0:T(8,128)(2,1)} %all-gather.11.cloned.1.call-done) | copy-start | bytes 15728644
  328.1 0.9 copy-start.12
Sparse Core Ops, SparseCore 0:
  9.5 60.7 all-gather.6
  122.1 72.2 all-gather.8
  196.5 47.6 all-gather.10

commit v4 on v3

--- a/solution.py
+++ b/solution.py
@@ -12,6 +12,7 @@
 NR = 32
 NC = 16
 VMEM_LIMIT = 24 * 1024 * 1024
+STREAM_LIMIT = 56 * 1024 * 1024
 F32 = jnp.float32
 BF16 = jnp.bfloat16
 VMEM = pl.BlockSpec(memory_space=pltpu.VMEM)
@@ -19,9 +20,9 @@
 HBM = pl.BlockSpec(memory_space=pltpu.HBM)
 
 
-def params(n=1):
+def params(n=1, limit=VMEM_LIMIT):
     return pltpu.CompilerParams(
-        vmem_limit_bytes=VMEM_LIMIT, dimension_semantics=("arbitrary",) * n
+        vmem_limit_bytes=limit, dimension_semantics=("arbitrary",) * n
     )
 
 
@@ -113,7 +114,7 @@
             pltpu.VMEM((NC, 8, 128, 256), BF16),
             pltpu.SemaphoreType.DMA((8,)),
         ],
-        compiler_params=params(0),
+        compiler_params=params(0, STREAM_LIMIT),
         name="solve_leaves",
     )(spread, inverse)
 
@@ -198,25 +199,10 @@
             o_ref[2 * c + half, t] = acc.astype(BF16)
 
 
-def solve_level(residual, weights, nodes, targets, stream):
+def solve_level(residual, weights, nodes, targets):
     groups = 4
 
-    def body(x_ref, w_ref, s_ref, o_ref, wait):
-        solved = []
-        for n in range(nodes):
-            wait(n)
-            x = solve_node(x_ref, w_ref, n, n)
-            s_ref[n] = x
-            solved.append(x.astype(BF16))
-        for g in range(groups):
-            wait(nodes + g)
-            for c in range(g * NC // groups, (g + 1) * NC // groups):
-                update_above(solved, w_ref, c, nodes, targets, o_ref)
-
-    def direct(x_ref, w_ref, s_ref, o_ref):
-        body(x_ref, w_ref, s_ref, o_ref, lambda i: None)
-
-    def streamed(x_ref, w_hbm, s_ref, o_ref, w_ref, sem):
+    def kernel(x_ref, w_hbm, s_ref, o_ref, w_ref, sem):
         pieces = [(slice(None), n) for n in range(nodes)]
         for g in range(groups):
             pieces.append((pl.ds(g * NC // groups, NC // groups), slice(nodes, None)))
@@ -226,22 +212,30 @@
         ]
         for copy in copies:
             copy.start()
-        body(x_ref, w_ref, s_ref, o_ref, lambda i: copies[i].wait())
-
-    scratch = [
-        pltpu.VMEM(weights.shape, BF16),
-        pltpu.SemaphoreType.DMA((nodes + groups,)),
-    ]
-    return pl.pallas_call(
-        streamed if stream else direct,
-        in_specs=[VMEM, HBM if stream else VMEM],
+        solved = []
+        for n in range(nodes):
+            copies[n].wait()
+            x = solve_node(x_ref, w_ref, n, n)
+            s_ref[n] = x
+            solved.append(x.astype(BF16))
+        for g in range(groups):
+            copies[nodes + g].wait()
+            for c in range(g * NC // groups, (g + 1) * NC // groups):
+                update_above(solved, w_ref, c, nodes, targets, o_ref)
+
+    return pl.pallas_call(
+        kernel,
+        in_specs=[VMEM, HBM],
         out_specs=[VMEM, VMEM],
         out_shape=[
             jax.ShapeDtypeStruct((nodes, 32, 128), F32),
             jax.ShapeDtypeStruct((NR, len(targets), 32, 128), BF16),
         ],
-        scratch_shapes=scratch if stream else [],
-        compiler_params=params(0),
+        scratch_shapes=[
+            pltpu.VMEM(weights.shape, BF16),
+            pltpu.SemaphoreType.DMA((nodes + groups,)),
+        ],
+        compiler_params=params(0, STREAM_LIMIT),
         name="solve_level",
     )(residual, weights)
 
@@ -308,15 +302,15 @@
     core = lax.axis_index("core")
     leaf_inverse = lax.all_gather(diag_inverse[:8], COL, axis=0)
     moved = to_owner(right_sides[:8].astype(BF16))
-    spread = spread_over(moved, ROW, NR)
 
     zero = jnp.zeros((), jnp.int32)
     meta = jnp.concatenate(
         [jnp.stack([col, core, row, zero]).astype(jnp.int32), block_map.reshape(-1)]
     )
-    meta, _ = lax.optimization_barrier((meta, moved))
     stack_two = stack_upper(meta, diag_inverse, panels, 8, 4, 0, 8)
     stack_one = stack_upper(meta, diag_inverse, panels, 12, 3, 8, 2)
+    moved, stack_two, stack_one = lax.optimization_barrier((moved, stack_two, stack_one))
+    spread = spread_over(moved, ROW, NR)
 
     leaves, copies = solve_leaves(spread, leaf_inverse)
     own = exchange(copies, "z")
@@ -330,10 +324,10 @@
 
     targets = [[(0, 0), (1, 2)], [(2, 4), (3, 6)], [(0, 1), (1, 3), (2, 5), (3, 7)]]
     spread = spread_over(residual[:4], ROW, NR)
-    two, parts = solve_level(spread, weights_two, 4, targets, True)
+    two, parts = solve_level(spread, weights_two, 4, targets)
     spread, rest = next_residual(exchange(parts, ROW), residual[4:], 2)
     targets = [[(0, 1), (1, 2)]]
-    one, parts = solve_level(exchange(spread, ROW), weights_one, 2, targets, False)
+    one, parts = solve_level(exchange(spread, ROW), weights_one, 2, targets)
     (spread,) = next_residual(exchange(parts, ROW), rest, 1)
     root = solve_root(exchange(spread, ROW), weights_one)
     return jnp.concatenate([leaves, two, one, root], axis=0)

time: 337 us -> 338 us (level)
  blocking collectives: 183 us -> 206 us
  waiting for transfers between devices: 62.1 us -> 49.3 us
  local copies, waits for them, and re-layouts: 21 us -> 10.7 us
  Pallas kernels: 26.5 us -> 35.8 us
  starting transfers between devices: 30.2 us -> 21.4 us
    all_to_all x5 -> x6, blocking collectives: 183 us -> 206 us  [exchange(): return lax.all_to_all(flat, axes, 0, 0, tiled=True).reshape(shape)]
    unnamed x29 -> x23, local copies, waits for them, and re-layouts: 17.5 us -> 7.12 us
    all_to_all x3 -> x2, starting transfers between devices: 18.8 us -> 10.1 us  [exchange(): return lax.all_to_all(flat, axes, 0, 0, tiled=True).reshape(shape)]
    all_to_all x3 -> x2, waiting for transfers between devices: 45.4 us -> 38.6 us  [exchange(): return lax.all_to_all(flat, axes, 0, 0, tiled=True).reshape(shape)]
    ppermute x2, waiting for transfers between devices: 14.1 us -> 8 us  [to_owner(): return lax.ppermute(values, ALL, pairs)]
    pallas_call x2, Pallas kernels: 11.2 us -> 17.3 us  [solve_level(): pl.pallas_call(kernel, in_specs=[VMEM, HBM], out_specs=[VMEM, VMEM], out_...]
  transfers between devices with their start and end apart: 9 -> 8, of which waited for: 6 -> 4; matrix products, arithmetic and copies ran while one was open for 1% -> 1% of each run, Pallas kernels for 5% -> 6%
where the time goes in v4:
time: 338 us; the launch traced here: 337 us
  blocking collectives  206 us (61%)
  waiting for transfers between devices  49.3 us (15%)
  Pallas kernels  35.8 us (11%)
  starting transfers between devices  21.4 us (6%)
  between operations  13.3 us (4%)
  local copies, waits for them, and re-layouts  10.7 us (3%)
    all_to_all x6, blocking collectives, exchange(): return lax.all_to_all(flat, axes, 0, 0, tiled=True).reshape(shape)  206 us
    all_to_all x2, waiting for transfers between devices, exchange(): return lax.all_to_all(flat, axes, 0, 0, tiled=True).reshape(shape)  38.6 us
    pallas_call x2, Pallas kernels, solve_level(): pl.pallas_call(kernel, in_specs=[VMEM, HBM], out_specs=[VMEM, VMEM], out_...  17.3 us
    all_to_all x2, starting transfers between devices, exchange(): return lax.all_to_all(flat, axes, 0, 0, tiled=True).reshape(shape)  10.1 us
    ppermute x2, starting transfers between devices, to_owner(): return lax.ppermute(values, ALL, pairs)  9.36 us
    pallas_call x1, Pallas kernels, solve_leaves(): pl.pallas_call(kernel, in_specs=[VMEM, HBM], out_specs=[VMEM, VMEM], out_...  9.09 us
    ppermute x2, waiting for transfers between devices, to_owner(): return lax.ppermute(values, ALL, pairs)  8 us
    unnamed x23, local copies, waits for them, and re-layouts  7.12 us
  transfers between devices with their start and end apart: 8, of which 4 were waited for; matrix products, arithmetic and copies ran while one was open for 1% of the time, Pallas kernels for 6%

profile of v4, /device:TPU:72, one launch (start us, length us, event | category | flops | bytes accessed | tf_op | source)
XLA Modules:
  0.0 336.9 jit_solution(14132506712446458344)
XLA Ops:
  6.5 1.9 slice.14
  8.5 0.9 slice.21
  9.4 5.9 %collective-permute-start = (bf16[8,16,256]{2,1,0:T(8,128)(2,1)S(1)}, bf16[8,16,256]{2,1,0:T(8,128)(2,1)S(1)}, u32[]{:S(2)}, u32[]{:S(2)}) collective-permute-start(bf16[8,16,256]{2,1,0:T(8,128)(2,1)S(1)} %slice.21), channel_id=1, source_target_pairs={{0,0},{1,32},{2,64},{3,96},{4,128},{5,160},{6,192},{7,224},{8,256}... | collective-permute-start | bytes 196616 | tf_op jit(solution)/shard_map/ppermute | solution.py:296
  15.4 0.9 copy.6
  16.6 1.8 copy-done
  18.3 1.2 copy-done.3
  19.5 4.5 %stack_upper.2 = bf16[12,128,256]{2,1,0:T(8,128)(2,1)} custom-call(s32[676]{0:T(1024)S(1)} %concatenate.6.meta_ref, bf16[15,128,256]{2,1,0:T(8,128)(2,1)S(1)} %copy-done.3, bf16[14,3,256,128]{3,2,1,0:T(8,128)(2,1)S(1)} %copy-done), custom_call_target="tpu_custom_call" | custom-call | tf_op jit(solution)/shard_map/stack_upper/pallas_call | solution.py:68
  24.1 1.2 copy-done.4
  25.3 0.8 stack_upper.3
  26.1 0.7 copy-done.5
  27.1 65.4 %all_to_all.40 = bf16[32,128,256]{2,1,0:T(8,128)(2,1)} all-to-all(bf16[32,128,256]{2,1,0:T(8,128)(2,1)S(1)} %broadcast_in_dim.17), channel_id=1, replica_groups=mesh['x'=4,'y'=8,'z'=8,'core'=2] {'x','y'}, dimensions={0} | all-to-all | bytes 4194304 | tf_op jit(solution)/shard_map/all_to_all | solution.py:285
  92.5 9.1 %solve_leaves.1 = (f32[8,32,128]{2,1,0:T(8,128)}, bf16[8,8,32,128]{3,2,1,0:T(8,128)(2,1)}) custom-call(bf16[32,8,16,256]{3,2,1,0:T(8,128)(2,1)} %bitcast.34, bf16[16,8,128,256]{3,2,1,0:T(8,128)(2,1)} %bitcast.33), custom_call_target="tpu_custom_call" | custom-call | tf_op jit(solution)/shard_map/solve_leaves/pallas_call | solution.py:105
  101.6 21.3 %all_to_all.41 = bf16[8,256,128]{2,1,0:T(8,128)(2,1)S(1)} all-to-all(bf16[8,256,128]{2,1,0:T(8,128)(2,1)} %bitcast.38), channel_id=1, replica_groups=mesh['x'=4,'y'=8,'z'=8,'core'=2] {'z'}, dimensions={0} | all-to-all | bytes 1048576 | tf_op jit(solution)/shard_map/all_to_all | solution.py:285
  122.9 0.7 all-gather.11.cloned.1.call-update
  123.6 1.9 collective-permute-start.1
  125.5 1.9 collective-permute-done.1.b_ref
  127.4 2.4 update_from_leaves.1
  129.8 51.2 %all_to_all.42 = bf16[32,224,128]{2,1,0:T(8,128)(2,1)S(1)} all-to-all(bf16[32,224,128]{2,1,0:T(8,128)(2,1)S(1)} %bitcast.24), channel_id=1, replica_groups=mesh['x'=4,'y'=8,'z'=8,'core'=2] {'x','y'}, dimensions={0} | all-to-all | bytes 3670016 | tf_op jit(solution)/shard_map/all_to_all | solution.py:285
  181.3 3.4 %collective-permute-start.2 = (bf16[7,32,128]{2,1,0:T(8,128)(2,1)S(1)}, bf16[7,32,128]{2,1,0:T(8,128)(2,1)S(1)}, u32[]{:S(2)}, u32[]{:S(2)}) collective-permute-start(bf16[7,32,128]{2,1,0:T(8,128)(2,1)S(1)} %first_residual.1), channel_id=1, source_target_pairs={{0,0},{1,32},{2,64},{3,96},{4,128},{5,160},{6,192},{7,224},{8,256}... | collective-permute-start | bytes 172040 | tf_op jit(solution)/shard_map/ppermute | solution.py:296
  184.7 8.0 %collective-permute-done.2 = bf16[7,32,128]{2,1,0:T(8,128)(2,1)S(1)} collective-permute-done((bf16[7,32,128]{2,1,0:T(8,128)(2,1)S(1)}, bf16[7,32,128]{2,1,0:T(8,128)(2,1)S(1)}, u32[]{:S(2)}, u32[]{:S(2)}) %collective-permute-start.2) | collective-permute-done | bytes 57376 | tf_op jit(solution)/shard_map/ppermute | solution.py:296
  193.0 36.8 %all_to_all.43 = bf16[32,128,128]{2,1,0:T(8,128)(2,1)} all-to-all(bf16[32,128,128]{2,1,0:T(8,128)(2,1)S(1)} %broadcast_in_dim.19), channel_id=1, replica_groups=mesh['x'=4,'y'=8,'z'=8,'core'=2] {'x','y'}, dimensions={0} | all-to-all | bytes 2097152 | tf_op jit(solution)/shard_map/all_to_all | solution.py:285
  229.7 10.9 %solve_level.2 = (f32[4,32,128]{2,1,0:T(8,128)}, bf16[32,3,32,128]{3,2,1,0:T(8,128)(2,1)}) custom-call(bf16[32,4,32,128]{3,2,1,0:T(8,128)(2,1)} %bitcast.35, bf16[16,12,128,256]{3,2,1,0:T(8,128)(2,1)} %bitcast.32), custom_call_target="tpu_custom_call" | custom-call | tf_op jit(solution)/shard_map/solve_level/pallas_call | solution.py:226
  240.7 5.1 %all-to-all-start.4 = ((bf16[32,96,128]{2,1,0:T(8,128)(2,1)}), bf16[32,96,128]{2,1,0:T(8,128)(2,1)S(1)}, u32[]{:S(2)}, u32[]{:S(2)}) async-start(bf16[32,96,128]{2,1,0:T(8,128)(2,1)} %bitcast.37), calls=%async_computation.4 | async-start | bytes 1572864 | tf_op jit(solution)/shard_map/all_to_all | solution.py:285
  245.8 22.1 %all-to-all-done.4 = bf16[32,96,128]{2,1,0:T(8,128)(2,1)S(1)} async-done(((bf16[32,96,128]{2,1,0:T(8,128)(2,1)}), bf16[32,96,128]{2,1,0:T(8,128)(2,1)S(1)}, u32[]{:S(2)}, u32[]{:S(2)}) %all-to-all-start.4) | async-done | bytes 786464 | tf_op jit(solution)/shard_map/all_to_all | solution.py:285
  267.9 0.9 next_residual.2
  268.8 4.9 %all-to-all-start.5 = ((bf16[32,64,128]{2,1,0:T(8,128)(2,1)}), bf16[32,64,128]{2,1,0:T(8,128)(2,1)S(1)}, u32[]{:S(2)}, u32[]{:S(2)}) async-start(bf16[32,64,128]{2,1,0:T(8,128)(2,1)} %bitcast.15), calls=%async_computation.5 | async-start | bytes 1048576 | tf_op jit(solution)/shard_map/all_to_all | solution.py:285
  273.8 16.6 %all-to-all-done.5 = bf16[32,64,128]{2,1,0:T(8,128)(2,1)S(1)} async-done(((bf16[32,64,128]{2,1,0:T(8,128)(2,1)}), bf16[32,64,128]{2,1,0:T(8,128)(2,1)S(1)}, u32[]{:S(2)}, u32[]{:S(2)}) %all-to-all-start.5) | async-done | bytes 524320 | tf_op jit(solution)/shard_map/all_to_all | solution.py:285
  290.4 0.8 copy-done.7
  291.2 6.3 %solve_level.3 = (f32[2,32,128]{2,1,0:T(8,128)}, bf16[32,1,32,128]{3,2,1,0:T(8,128)(2,1)}) custom-call(bf16[32,2,32,128]{3,2,1,0:T(8,128)(2,1)} %bitcast.36, bf16[16,5,128,256]{3,2,1,0:T(8,128)(2,1)} %bitcast.22), custom_call_target="tpu_custom_call" | custom-call | tf_op jit(solution)/shard_map/solve_level/pallas_call | solution.py:226
  297.5 15.8 %all_to_all.44 = bf16[32,32,128]{2,1,0:T(8,128)(2,1)S(1)} all-to-all(bf16[32,32,128]{2,1,0:T(8,128)(2,1)} %bitcast.39), channel_id=1, replica_groups=mesh['x'=4,'y'=8,'z'=8,'core'=2] {'x','y'}, dimensions={0} | all-to-all | bytes 524288 | tf_op jit(solution)/shard_map/all_to_all | solution.py:285
  313.4 15.4 %all_to_all.45 = bf16[32,32,128]{2,1,0:T(8,128)(2,1)S(1)} all-to-all(bf16[32,32,128]{2,1,0:T(8,128)(2,1)S(1)} %bitcast.30), channel_id=1, replica_groups=mesh['x'=4,'y'=8,'z'=8,'core'=2] {'x','y'}, dimensions={0} | all-to-all | bytes 524288 | tf_op jit(solution)/shard_map/all_to_all | solution.py:285
  329.7 0.7 pad_maximum_fusion
  (35 shorter events, 2.1 us)
Async XLA Ops:
  6.5 85.9 %all-gather.7.cloned.1.call-start = ((), (), s32[]{:S(2)}) async-start(), calls=%async_computation.8 | async-start | bytes 8912896 | tf_op jit(solution)/shard_map/all_gather | solution.py:303
  8.5 221.3 %all-gather.9.cloned.1.call-start = ((), (), s32[]{:S(2)}) async-start(), calls=%async_computation.9 | async-start | bytes 13369344 | tf_op jit(solution)/shard_map/all_gather | solution.py:319
  9.4 17.4 %collective-permute-start = (bf16[8,16,256]{2,1,0:T(8,128)(2,1)S(1)}, bf16[8,16,256]{2,1,0:T(8,128)(2,1)S(1)}, u32[]{:S(2)}, u32[]{:S(2)}) collective-permute-start(bf16[8,16,256]{2,1,0:T(8,128)(2,1)S(1)} %slice.21), channel_id=1, source_target_pairs={{0,0},{1,32},{2,64},{3,96},{4,128},{5,160},{6,192},{7,224},{8,256}... | collective-permute-start | bytes 196616 | tf_op jit(solution)/shard_map/ppermute | solution.py:296
  16.6 1.8 copy-start
  18.3 1.2 copy-start.3
  19.5 4.5 %copy-start.1 = (bf16[14,3,256,128]{3,2,1,0:T(8,128)(2,1)S(1)}, bf16[14,3,256,128]{3,2,1,0:T(8,128)(2,1)}, u32[]{:S(2)}) copy-start(bf16[14,3,256,128]{3,2,1,0:T(8,128)(2,1)} %p_ref.5) | copy-start | bytes 8257540
  24.1 1.2 copy-start.4
  26.1 0.7 copy-start.5
  92.5 34.9 %copy-start.6 = (f32[15,16,256]{2,1,0:T(8,128)S(1)}, f32[15,16,256]{2,1,0:T(8,128)}, u32[]{:S(2)}) copy-start(f32[15,16,256]{2,1,0:T(8,128)} %r_ref.1) | copy-start | bytes 737284
  122.9 150.9 %all-gather.11.cloned.1.call-start = ((), (), s32[]{:S(2)}) async-start(), calls=%async_computation.10 | async-start | bytes 5570560 | tf_op jit(solution)/shard_map/all_gather | solution.py:320
  123.6 3.8 %collective-permute-start.1 = (bf16[8,8,32,128]{3,2,1,0:T(8,128)(2,1)S(1)}, bf16[8,8,32,128]{3,2,1,0:T(8,128)(2,1)S(1)}, u32[]{:S(2)}, u32[]{:S(2)}) collective-permute-start(bf16[8,8,32,128]{3,2,1,0:T(8,128)(2,1)S(1)} %bitcast.27), channel_id=1, source_target_pairs={{0,1},{1,0},{2,3},{3,2},{4,5},{5,4},{6,7},{7,6},{8,9},{9,8},{10,11... | collective-permute-start | bytes 1572872 | tf_op jit(solution)/shard_map/ppermute | solution.py:317
  181.3 11.4 %collective-permute-start.2 = (bf16[7,32,128]{2,1,0:T(8,128)(2,1)S(1)}, bf16[7,32,128]{2,1,0:T(8,128)(2,1)S(1)}, u32[]{:S(2)}, u32[]{:S(2)}) collective-permute-start(bf16[7,32,128]{2,1,0:T(8,128)(2,1)S(1)} %first_residual.1), channel_id=1, source_target_pairs={{0,0},{1,32},{2,64},{3,96},{4,128},{5,160},{6,192},{7,224},{8,256}... | collective-permute-start | bytes 172040 | tf_op jit(solution)/shard_map/ppermute | solution.py:296
  240.7 27.2 %all-to-all-start.4 = ((bf16[32,96,128]{2,1,0:T(8,128)(2,1)}), bf16[32,96,128]{2,1,0:T(8,128)(2,1)S(1)}, u32[]{:S(2)}, u32[]{:S(2)}) async-start(bf16[32,96,128]{2,1,0:T(8,128)(2,1)} %bitcast.37), calls=%async_computation.4 | async-start | bytes 1572864 | tf_op jit(solution)/shard_map/all_to_all | solution.py:285
  268.8 21.5 %all-to-all-start.5 = ((bf16[32,64,128]{2,1,0:T(8,128)(2,1)}), bf16[32,64,128]{2,1,0:T(8,128)(2,1)S(1)}, u32[]{:S(2)}, u32[]{:S(2)}) async-start(bf16[32,64,128]{2,1,0:T(8,128)(2,1)} %bitcast.15), calls=%async_computation.5 | async-start | bytes 1048576 | tf_op jit(solution)/shard_map/all_to_all | solution.py:285
  290.4 0.8 copy-start.7
  291.2 37.6 %copy-start.2 = (bf16[80,128,256]{2,1,0:T(8,128)(2,1)S(1)}, bf16[80,128,256]{2,1,0:T(8,128)(2,1)}, u32[]{:S(2)}) copy-start(bf16[80,128,256]{2,1,0:T(8,128)(2,1)} %all-gather.11.cloned.1.call-done) | copy-start | bytes 15728644
  328.8 0.9 copy-start.8
  328.8 0.9 copy-start.9
  328.8 0.9 copy-start.10
Sparse Core Ops, SparseCore 0:
  9.5 60.7 all-gather.6
  123.0 71.9 all-gather.8
  197.1 47.5 all-gather.10

commit v5 on v4

--- a/solution.py
+++ b/solution.py
@@ -13,6 +13,7 @@
 NC = 16
 VMEM_LIMIT = 24 * 1024 * 1024
 STREAM_LIMIT = 56 * 1024 * 1024
+DEPTH = 3
 F32 = jnp.float32
 BF16 = jnp.bfloat16
 VMEM = pl.BlockSpec(memory_space=pltpu.VMEM)
@@ -89,10 +90,12 @@
         copies = [
             pltpu.make_async_copy(d_hbm.at[:, n], d_ref.at[:, n], sem.at[n]) for n in range(8)
         ]
-        for copy in copies:
+        for copy in copies[:DEPTH]:
             copy.start()
         for n in range(8):
             copies[n].wait()
+            if n + DEPTH < 8:
+                copies[n + DEPTH].start()
             acc = jnp.zeros((32, 128), F32)
             for c in range(NC):
                 left = b_ref[2 * c : 2 * c + 2, n].reshape(32, 256)
@@ -210,16 +213,22 @@
             pltpu.make_async_copy(w_hbm.at[piece], w_ref.at[piece], sem.at[i])
             for i, piece in enumerate(pieces)
         ]
-        for copy in copies:
+        for copy in copies[:DEPTH]:
             copy.start()
+
+        def arrived(i):
+            copies[i].wait()
+            if i + DEPTH < len(copies):
+                copies[i + DEPTH].start()
+
         solved = []
         for n in range(nodes):
-            copies[n].wait()
+            arrived(n)
             x = solve_node(x_ref, w_ref, n, n)
             s_ref[n] = x
             solved.append(x.astype(BF16))
         for g in range(groups):
-            copies[nodes + g].wait()
+            arrived(nodes + g)
             for c in range(g * NC // groups, (g + 1) * NC // groups):
                 update_above(solved, w_ref, c, nodes, targets, o_ref)
 
@@ -300,8 +309,11 @@
     row = lax.axis_index(ROW)
     col = lax.axis_index(COL)
     core = lax.axis_index("core")
+    leaf_right, diag_inverse = lax.optimization_barrier(
+        (right_sides[:8].astype(BF16), diag_inverse)
+    )
+    moved = to_owner(leaf_right)
     leaf_inverse = lax.all_gather(diag_inverse[:8], COL, axis=0)
-    moved = to_owner(right_sides[:8].astype(BF16))
 
     zero = jnp.zeros((), jnp.int32)
     meta = jnp.concatenate(
@@ -309,8 +321,8 @@
     )
     stack_two = stack_upper(meta, diag_inverse, panels, 8, 4, 0, 8)
     stack_one = stack_upper(meta, diag_inverse, panels, 12, 3, 8, 2)
-    moved, stack_two, stack_one = lax.optimization_barrier((moved, stack_two, stack_one))
     spread = spread_over(moved, ROW, NR)
+    spread, stack_two, stack_one = lax.optimization_barrier((spread, stack_two, stack_one))
 
     leaves, copies = solve_leaves(spread, leaf_inverse)
     own = exchange(copies, "z")

time: 338 us -> 336 us (level)
  blocking collectives: 206 us -> 145 us
  waiting for transfers between devices: 49.3 us -> 95.7 us
  starting transfers between devices: 21.4 us -> 35.1 us
    all_to_all x6 -> x5, blocking collectives: 206 us -> 145 us  [exchange(): return lax.all_to_all(flat, axes, 0, 0, tiled=True).reshape(shape)]
    all_to_all x2 -> x3, waiting for transfers between devices: 38.6 us -> 79 us  [exchange(): return lax.all_to_all(flat, axes, 0, 0, tiled=True).reshape(shape)]
    all_to_all x2 -> x3, starting transfers between devices: 10.1 us -> 23.7 us  [exchange(): return lax.all_to_all(flat, axes, 0, 0, tiled=True).reshape(shape)]
    ppermute x2, waiting for transfers between devices: 8 us -> 14.1 us  [to_owner(): return lax.ppermute(values, ALL, pairs)]
  transfers between devices with their start and end apart: 8 -> 9, of which waited for: 4 -> 6; matrix products, arithmetic and copies ran while one was open for 1% -> 1% of each run, Pallas kernels for 6% -> 6%
where the time goes in v5:
time: 336 us
  blocking collectives  145 us (43%)
  waiting for transfers between devices  95.7 us (28%)
  Pallas kernels  35.8 us (11%)
  starting transfers between devices  35.1 us (10%)
  between operations  13.3 us (4%)
  local copies, waits for them, and re-layouts  9.57 us (3%)
    all_to_all x5, blocking collectives, exchange(): return lax.all_to_all(flat, axes, 0, 0, tiled=True).reshape(shape)  145 us
    all_to_all x3, waiting for transfers between devices, exchange(): return lax.all_to_all(flat, axes, 0, 0, tiled=True).reshape(shape)  79 us
    all_to_all x3, starting transfers between devices, exchange(): return lax.all_to_all(flat, axes, 0, 0, tiled=True).reshape(shape)  23.7 us
    pallas_call x2, Pallas kernels, solve_level(): pl.pallas_call(kernel, in_specs=[VMEM, HBM], out_specs=[VMEM, VMEM], out_...  17.3 us
    ppermute x2, waiting for transfers between devices, to_owner(): return lax.ppermute(values, ALL, pairs)  14.1 us
    ppermute x2, starting transfers between devices, to_owner(): return lax.ppermute(values, ALL, pairs)  9.36 us
    pallas_call x1, Pallas kernels, solve_leaves(): pl.pallas_call(kernel, in_specs=[VMEM, HBM], out_specs=[VMEM, VMEM], out_...  9.08 us
  transfers between devices with their start and end apart: 9, of which 6 were waited for; matrix products, arithmetic and copies ran while one was open for 1% of the time, Pallas kernels for 6%

profile of v5, /device:TPU:72, one launch (start us, length us, event | category | flops | bytes accessed | tf_op | source)
XLA Modules:
  0.0 335.5 jit_solution(2868941152409534330)
XLA Ops:
  6.5 0.9 slice.21
  7.5 1.9 slice.14
  9.4 5.9 %collective-permute-start = (bf16[8,16,256]{2,1,0:T(8,128)(2,1)S(1)}, bf16[8,16,256]{2,1,0:T(8,128)(2,1)S(1)}, u32[]{:S(2)}, u32[]{:S(2)}) collective-permute-start(bf16[8,16,256]{2,1,0:T(8,128)(2,1)S(1)} %slice.21), channel_id=1, source_target_pairs={{0,0},{1,32},{2,64},{3,96},{4,128},{5,160},{6,192},{7,224},{8,256}... | collective-permute-start | bytes 196616 | tf_op jit(solution)/shard_map/ppermute | solution.py:305
  15.3 6.1 %collective-permute-done = bf16[8,16,256]{2,1,0:T(8,128)(2,1)S(1)} collective-permute-done((bf16[8,16,256]{2,1,0:T(8,128)(2,1)S(1)}, bf16[8,16,256]{2,1,0:T(8,128)(2,1)S(1)}, u32[]{:S(2)}, u32[]{:S(2)}) %collective-permute-start) | collective-permute-done | bytes 65568 | tf_op jit(solution)/shard_map/ppermute | solution.py:305
  21.4 1.6 broadcast_in_dim.17
  23.0 13.7 %all-to-all-start = ((bf16[32,128,256]{2,1,0:T(8,128)(2,1)}), bf16[32,128,256]{2,1,0:T(8,128)(2,1)}, u32[]{:S(2)}, u32[]{:S(2)}) async-start(bf16[32,128,256]{2,1,0:T(8,128)(2,1)} %broadcast_in_dim.17), calls=%async_computation | async-start | bytes 4194304 | tf_op jit(solution)/shard_map/all_to_all | solution.py:294
  37.2 1.2 copy-done.2
  38.5 4.5 %stack_upper.2 = bf16[12,128,256]{2,1,0:T(8,128)(2,1)} custom-call(s32[676]{0:T(1024)S(1)} %concatenate.6.meta_ref, bf16[15,128,256]{2,1,0:T(8,128)(2,1)S(1)} %copy-done.2, bf16[14,3,256,128]{3,2,1,0:T(8,128)(2,1)S(1)} %copy-done), custom_call_target="tpu_custom_call" | custom-call | tf_op jit(solution)/shard_map/stack_upper/pallas_call | solution.py:69
  43.0 1.2 copy-done.3
  44.2 0.8 stack_upper.3
  45.1 0.7 copy-done.4
  45.8 40.3 %all-to-all-done = bf16[32,128,256]{2,1,0:T(8,128)(2,1)} async-done(((bf16[32,128,256]{2,1,0:T(8,128)(2,1)}), bf16[32,128,256]{2,1,0:T(8,128)(2,1)}, u32[]{:S(2)}, u32[]{:S(2)}) %all-to-all-start) | async-done | bytes 2097184 | tf_op jit(solution)/shard_map/all_to_all | solution.py:294
  86.1 9.1 %solve_leaves.1 = (f32[8,32,128]{2,1,0:T(8,128)}, bf16[8,8,32,128]{3,2,1,0:T(8,128)(2,1)}) custom-call(bf16[32,8,16,256]{3,2,1,0:T(8,128)(2,1)} %bitcast.1.b_ref, bf16[16,8,128,256]{3,2,1,0:T(8,128)(2,1)} %bitcast.33), custom_call_target="tpu_custom_call" | custom-call | tf_op jit(solution)/shard_map/solve_leaves/pallas_call | solution.py:108
  95.2 24.3 %all_to_all.40 = bf16[8,256,128]{2,1,0:T(8,128)(2,1)S(1)} all-to-all(bf16[8,256,128]{2,1,0:T(8,128)(2,1)} %bitcast.37), channel_id=1, replica_groups=mesh['x'=4,'y'=8,'z'=8,'core'=2] {'z'}, dimensions={0} | all-to-all | bytes 1048576 | tf_op jit(solution)/shard_map/all_to_all | solution.py:294
  120.3 1.9 collective-permute-start.1
  122.3 1.9 collective-permute-done.1.b_ref
  124.2 2.4 update_from_leaves.1
  126.6 53.1 %all_to_all.41 = bf16[32,224,128]{2,1,0:T(8,128)(2,1)S(1)} all-to-all(bf16[32,224,128]{2,1,0:T(8,128)(2,1)S(1)} %bitcast.24), channel_id=1, replica_groups=mesh['x'=4,'y'=8,'z'=8,'core'=2] {'x','y'}, dimensions={0} | all-to-all | bytes 3670016 | tf_op jit(solution)/shard_map/all_to_all | solution.py:294
  179.9 3.4 %collective-permute-start.2 = (bf16[7,32,128]{2,1,0:T(8,128)(2,1)S(1)}, bf16[7,32,128]{2,1,0:T(8,128)(2,1)S(1)}, u32[]{:S(2)}, u32[]{:S(2)}) collective-permute-start(bf16[7,32,128]{2,1,0:T(8,128)(2,1)S(1)} %first_residual.1), channel_id=1, source_target_pairs={{0,0},{1,32},{2,64},{3,96},{4,128},{5,160},{6,192},{7,224},{8,256}... | collective-permute-start | bytes 172040 | tf_op jit(solution)/shard_map/ppermute | solution.py:305
  183.4 8.0 %collective-permute-done.2 = bf16[7,32,128]{2,1,0:T(8,128)(2,1)S(1)} collective-permute-done((bf16[7,32,128]{2,1,0:T(8,128)(2,1)S(1)}, bf16[7,32,128]{2,1,0:T(8,128)(2,1)S(1)}, u32[]{:S(2)}, u32[]{:S(2)}) %collective-permute-start.2) | collective-permute-done | bytes 57376 | tf_op jit(solution)/shard_map/ppermute | solution.py:305
  191.6 36.8 %all_to_all.42 = bf16[32,128,128]{2,1,0:T(8,128)(2,1)} all-to-all(bf16[32,128,128]{2,1,0:T(8,128)(2,1)S(1)} %broadcast_in_dim.19), channel_id=1, replica_groups=mesh['x'=4,'y'=8,'z'=8,'core'=2] {'x','y'}, dimensions={0} | all-to-all | bytes 2097152 | tf_op jit(solution)/shard_map/all_to_all | solution.py:294
  228.4 10.9 %solve_level.2 = (f32[4,32,128]{2,1,0:T(8,128)}, bf16[32,3,32,128]{3,2,1,0:T(8,128)(2,1)}) custom-call(bf16[32,4,32,128]{3,2,1,0:T(8,128)(2,1)} %bitcast.34, bf16[16,12,128,256]{3,2,1,0:T(8,128)(2,1)} %bitcast.32), custom_call_target="tpu_custom_call" | custom-call | tf_op jit(solution)/shard_map/solve_level/pallas_call | solution.py:235
  239.3 5.1 %all-to-all-start.4 = ((bf16[32,96,128]{2,1,0:T(8,128)(2,1)}), bf16[32,96,128]{2,1,0:T(8,128)(2,1)S(1)}, u32[]{:S(2)}, u32[]{:S(2)}) async-start(bf16[32,96,128]{2,1,0:T(8,128)(2,1)} %bitcast.36), calls=%async_computation.4 | async-start | bytes 1572864 | tf_op jit(solution)/shard_map/all_to_all | solution.py:294
  244.4 22.1 %all-to-all-done.4 = bf16[32,96,128]{2,1,0:T(8,128)(2,1)S(1)} async-done(((bf16[32,96,128]{2,1,0:T(8,128)(2,1)}), bf16[32,96,128]{2,1,0:T(8,128)(2,1)S(1)}, u32[]{:S(2)}, u32[]{:S(2)}) %all-to-all-start.4) | async-done | bytes 786464 | tf_op jit(solution)/shard_map/all_to_all | solution.py:294
  266.5 0.9 next_residual.2
  267.4 4.9 %all-to-all-start.5 = ((bf16[32,64,128]{2,1,0:T(8,128)(2,1)}), bf16[32,64,128]{2,1,0:T(8,128)(2,1)S(1)}, u32[]{:S(2)}, u32[]{:S(2)}) async-start(bf16[32,64,128]{2,1,0:T(8,128)(2,1)} %bitcast.15), calls=%async_computation.5 | async-start | bytes 1048576 | tf_op jit(solution)/shard_map/all_to_all | solution.py:294
  272.4 16.6 %all-to-all-done.5 = bf16[32,64,128]{2,1,0:T(8,128)(2,1)S(1)} async-done(((bf16[32,64,128]{2,1,0:T(8,128)(2,1)}), bf16[32,64,128]{2,1,0:T(8,128)(2,1)S(1)}, u32[]{:S(2)}, u32[]{:S(2)}) %all-to-all-start.5) | async-done | bytes 524320 | tf_op jit(solution)/shard_map/all_to_all | solution.py:294
  289.0 0.8 copy-done.6
  289.8 6.3 %solve_level.3 = (f32[2,32,128]{2,1,0:T(8,128)}, bf16[32,1,32,128]{3,2,1,0:T(8,128)(2,1)}) custom-call(bf16[32,2,32,128]{3,2,1,0:T(8,128)(2,1)} %bitcast.35, bf16[16,5,128,256]{3,2,1,0:T(8,128)(2,1)} %bitcast.22), custom_call_target="tpu_custom_call" | custom-call | tf_op jit(solution)/shard_map/solve_level/pallas_call | solution.py:235
  296.1 15.8 %all_to_all.43 = bf16[32,32,128]{2,1,0:T(8,128)(2,1)S(1)} all-to-all(bf16[32,32,128]{2,1,0:T(8,128)(2,1)} %bitcast.38), channel_id=1, replica_groups=mesh['x'=4,'y'=8,'z'=8,'core'=2] {'x','y'}, dimensions={0} | all-to-all | bytes 524288 | tf_op jit(solution)/shard_map/all_to_all | solution.py:294
  312.0 15.4 %all_to_all.44 = bf16[32,32,128]{2,1,0:T(8,128)(2,1)S(1)} all-to-all(bf16[32,32,128]{2,1,0:T(8,128)(2,1)S(1)} %bitcast.30), channel_id=1, replica_groups=mesh['x'=4,'y'=8,'z'=8,'core'=2] {'x','y'}, dimensions={0} | all-to-all | bytes 524288 | tf_op jit(solution)/shard_map/all_to_all | solution.py:294
  328.3 0.7 pad_maximum_fusion
  (36 shorter events, 2.7 us)
Async XLA Ops:
  6.5 79.6 %all-gather.7.cloned.1.call-start = ((), (), s32[]{:S(2)}) async-start(), calls=%async_computation.8 | async-start | bytes 8912896 | tf_op jit(solution)/shard_map/all_gather | solution.py:316
  9.4 12.0 %collective-permute-start = (bf16[8,16,256]{2,1,0:T(8,128)(2,1)S(1)}, bf16[8,16,256]{2,1,0:T(8,128)(2,1)S(1)}, u32[]{:S(2)}, u32[]{:S(2)}) collective-permute-start(bf16[8,16,256]{2,1,0:T(8,128)(2,1)S(1)} %slice.21), channel_id=1, source_target_pairs={{0,0},{1,32},{2,64},{3,96},{4,128},{5,160},{6,192},{7,224},{8,256}... | collective-permute-start | bytes 196616 | tf_op jit(solution)/shard_map/ppermute | solution.py:305
  21.4 15.4 %copy-start.10 = (s32[14,16,3]{1,0,2:T(8,128)S(1)}, s32[14,16,3]{1,0,2:T(8,128)}, u32[]{:S(2)}) copy-start(s32[14,16,3]{1,0,2:T(8,128)} %param.7) | copy-start | bytes 8068
  23.0 14.2 %copy-start = (bf16[14,3,256,128]{3,2,1,0:T(8,128)(2,1)S(1)}, bf16[14,3,256,128]{3,2,1,0:T(8,128)(2,1)}, u32[]{:S(2)}) copy-start(bf16[14,3,256,128]{3,2,1,0:T(8,128)(2,1)} %p_ref.5) | copy-start | bytes 8257540
  23.0 63.1 %all-to-all-start = ((bf16[32,128,256]{2,1,0:T(8,128)(2,1)}), bf16[32,128,256]{2,1,0:T(8,128)(2,1)}, u32[]{:S(2)}, u32[]{:S(2)}) async-start(bf16[32,128,256]{2,1,0:T(8,128)(2,1)} %broadcast_in_dim.17), calls=%async_computation | async-start | bytes 4194304 | tf_op jit(solution)/shard_map/all_to_all | solution.py:294
  36.7 191.7 %all-gather.9.cloned.1.call-start = ((), (), s32[]{:S(2)}) async-start(), calls=%async_computation.9 | async-start | bytes 13369344 | tf_op jit(solution)/shard_map/all_gather | solution.py:331
  37.2 1.2 copy-start.2
  43.0 1.2 copy-start.3
  45.1 0.7 copy-start.4
  86.1 38.0 %copy-start.5 = (f32[15,16,256]{2,1,0:T(8,128)S(1)}, f32[15,16,256]{2,1,0:T(8,128)}, u32[]{:S(2)}) copy-start(f32[15,16,256]{2,1,0:T(8,128)} %r_ref.1) | copy-start | bytes 737284
  119.6 152.8 %all-gather.11.cloned.1.call-start = ((), (), s32[]{:S(2)}) async-start(), calls=%async_computation.10 | async-start | bytes 5570560 | tf_op jit(solution)/shard_map/all_gather | solution.py:332
  120.3 3.8 %collective-permute-start.1 = (bf16[8,8,32,128]{3,2,1,0:T(8,128)(2,1)S(1)}, bf16[8,8,32,128]{3,2,1,0:T(8,128)(2,1)S(1)}, u32[]{:S(2)}, u32[]{:S(2)}) collective-permute-start(bf16[8,8,32,128]{3,2,1,0:T(8,128)(2,1)S(1)} %bitcast.27), channel_id=1, source_target_pairs={{0,1},{1,0},{2,3},{3,2},{4,5},{5,4},{6,7},{7,6},{8,9},{9,8},{10,11... | collective-permute-start | bytes 1572872 | tf_op jit(solution)/shard_map/ppermute | solution.py:329
  179.9 11.4 %collective-permute-start.2 = (bf16[7,32,128]{2,1,0:T(8,128)(2,1)S(1)}, bf16[7,32,128]{2,1,0:T(8,128)(2,1)S(1)}, u32[]{:S(2)}, u32[]{:S(2)}) collective-permute-start(bf16[7,32,128]{2,1,0:T(8,128)(2,1)S(1)} %first_residual.1), channel_id=1, source_target_pairs={{0,0},{1,32},{2,64},{3,96},{4,128},{5,160},{6,192},{7,224},{8,256}... | collective-permute-start | bytes 172040 | tf_op jit(solution)/shard_map/ppermute | solution.py:305
  239.3 27.2 %all-to-all-start.4 = ((bf16[32,96,128]{2,1,0:T(8,128)(2,1)}), bf16[32,96,128]{2,1,0:T(8,128)(2,1)S(1)}, u32[]{:S(2)}, u32[]{:S(2)}) async-start(bf16[32,96,128]{2,1,0:T(8,128)(2,1)} %bitcast.36), calls=%async_computation.4 | async-start | bytes 1572864 | tf_op jit(solution)/shard_map/all_to_all | solution.py:294
  267.4 21.5 %all-to-all-start.5 = ((bf16[32,64,128]{2,1,0:T(8,128)(2,1)}), bf16[32,64,128]{2,1,0:T(8,128)(2,1)S(1)}, u32[]{:S(2)}, u32[]{:S(2)}) async-start(bf16[32,64,128]{2,1,0:T(8,128)(2,1)} %bitcast.15), calls=%async_computation.5 | async-start | bytes 1048576 | tf_op jit(solution)/shard_map/all_to_all | solution.py:294
  289.0 0.8 copy-start.6
  289.8 37.6 %copy-start.1 = (bf16[80,128,256]{2,1,0:T(8,128)(2,1)S(1)}, bf16[80,128,256]{2,1,0:T(8,128)(2,1)}, u32[]{:S(2)}) copy-start(bf16[80,128,256]{2,1,0:T(8,128)(2,1)} %all-gather.11.cloned.1.call-done) | copy-start | bytes 15728644
  327.4 0.9 copy-start.7
  327.4 0.9 copy-start.8
  327.4 0.9 copy-start.9
Sparse Core Ops, SparseCore 0:
  9.5 60.7 all-gather.6
  119.7 73.8 all-gather.8
  195.7 47.5 all-gather.10

commit v6 on v4

--- a/solution.py
+++ b/solution.py
@@ -86,19 +86,19 @@
 
 def solve_leaves(spread, inverse):
     def kernel(b_ref, d_hbm, x_ref, h_ref, d_ref, sem):
-        copies = [
-            pltpu.make_async_copy(d_hbm.at[:, n], d_ref.at[:, n], sem.at[n]) for n in range(8)
-        ]
+        copies = [pltpu.make_async_copy(d_hbm.at[c], d_ref.at[c], sem.at[c]) for c in range(NC)]
         for copy in copies:
             copy.start()
+        for c in range(NC):
+            copies[c].wait()
+            for n in range(8):
+                left = b_ref[2 * c : 2 * c + 2, n].reshape(32, 256)
+                value = dot_t(left, d_ref[c, n])
+                if c:
+                    value = value + x_ref[n]
+                x_ref[n] = value
         for n in range(8):
-            copies[n].wait()
-            acc = jnp.zeros((32, 128), F32)
-            for c in range(NC):
-                left = b_ref[2 * c : 2 * c + 2, n].reshape(32, 256)
-                acc = acc + dot_t(left, d_ref[c, n])
-            x_ref[n] = acc
-            half = acc.astype(BF16)
+            half = x_ref[n].astype(BF16)
             for z in range(8):
                 h_ref[z, n] = half
 
@@ -112,7 +112,7 @@
         ],
         scratch_shapes=[
             pltpu.VMEM((NC, 8, 128, 256), BF16),
-            pltpu.SemaphoreType.DMA((8,)),
+            pltpu.SemaphoreType.DMA((NC,)),
         ],
         compiler_params=params(0, STREAM_LIMIT),
         name="solve_leaves",
@@ -200,28 +200,29 @@
 
 
 def solve_level(residual, weights, nodes, targets):
-    groups = 4
+    used = nodes + min(b for terms in targets for _, b in terms)
 
     def kernel(x_ref, w_hbm, s_ref, o_ref, w_ref, sem):
-        pieces = [(slice(None), n) for n in range(nodes)]
-        for g in range(groups):
-            pieces.append((pl.ds(g * NC // groups, NC // groups), slice(nodes, None)))
+        pieces = [(c, slice(0, nodes)) for c in range(NC)]
+        pieces += [(c, slice(used, None)) for c in range(NC)]
         copies = [
             pltpu.make_async_copy(w_hbm.at[piece], w_ref.at[piece], sem.at[i])
             for i, piece in enumerate(pieces)
         ]
         for copy in copies:
             copy.start()
-        solved = []
-        for n in range(nodes):
-            copies[n].wait()
-            x = solve_node(x_ref, w_ref, n, n)
-            s_ref[n] = x
-            solved.append(x.astype(BF16))
-        for g in range(groups):
-            copies[nodes + g].wait()
-            for c in range(g * NC // groups, (g + 1) * NC // groups):
-                update_above(solved, w_ref, c, nodes, targets, o_ref)
+        for c in range(NC):
+            copies[c].wait()
+            for n in range(nodes):
+                left = jnp.concatenate([x_ref[2 * c, n], x_ref[2 * c + 1, n]], axis=1)
+                value = dot_t(left, w_ref[c, n])
+                if c:
+                    value = value + s_ref[n]
+                s_ref[n] = value
+        solved = [s_ref[n].astype(BF16) for n in range(nodes)]
+        for c in range(NC):
+            copies[NC + c].wait()
+            update_above(solved, w_ref, c, nodes, targets, o_ref)
 
     return pl.pallas_call(
         kernel,
@@ -233,7 +234,7 @@
         ],
         scratch_shapes=[
             pltpu.VMEM(weights.shape, BF16),
-            pltpu.SemaphoreType.DMA((nodes + groups,)),
+            pltpu.SemaphoreType.DMA((2 * NC,)),
         ],
         compiler_params=params(0, STREAM_LIMIT),
         name="solve_level",
@@ -300,8 +301,11 @@
     row = lax.axis_index(ROW)
     col = lax.axis_index(COL)
     core = lax.axis_index("core")
+    leaf_right, diag_inverse = lax.optimization_barrier(
+        (right_sides[:8].astype(BF16), diag_inverse)
+    )
+    moved = to_owner(leaf_right)
     leaf_inverse = lax.all_gather(diag_inverse[:8], COL, axis=0)
-    moved = to_owner(right_sides[:8].astype(BF16))
 
     zero = jnp.zeros((), jnp.int32)
     meta = jnp.concatenate(
@@ -309,8 +313,8 @@
     )
     stack_two = stack_upper(meta, diag_inverse, panels, 8, 4, 0, 8)
     stack_one = stack_upper(meta, diag_inverse, panels, 12, 3, 8, 2)
-    moved, stack_two, stack_one = lax.optimization_barrier((moved, stack_two, stack_one))
     spread = spread_over(moved, ROW, NR)
+    spread, stack_two, stack_one = lax.optimization_barrier((spread, stack_two, stack_one))
 
     leaves, copies = solve_leaves(spread, leaf_inverse)
     own = exchange(copies, "z")

time: 338 us -> 335 us (level)
  blocking collectives: 206 us -> 145 us
  waiting for transfers between devices: 49.3 us -> 95.7 us
  starting transfers between devices: 21.4 us -> 35.1 us
    all_to_all x6 -> x5, blocking collectives: 206 us -> 145 us  [exchange(): return lax.all_to_all(flat, axes, 0, 0, tiled=True).reshape(shape)]
    all_to_all x2 -> x3, waiting for transfers between devices: 38.6 us -> 79 us  [exchange(): return lax.all_to_all(flat, axes, 0, 0, tiled=True).reshape(shape)]
    all_to_all x2 -> x3, starting transfers between devices: 10.1 us -> 23.7 us  [exchange(): return lax.all_to_all(flat, axes, 0, 0, tiled=True).reshape(shape)]
    ppermute x2, waiting for transfers between devices: 8 us -> 14.1 us  [to_owner(): return lax.ppermute(values, ALL, pairs)]
  transfers between devices with their start and end apart: 8 -> 9, of which waited for: 4 -> 6; matrix products, arithmetic and copies ran while one was open for 1% -> 1% of each run, Pallas kernels for 6% -> 6%
where the time goes in v6:
time: 335 us; the launch traced here: 334 us
  blocking collectives  145 us (43%)
  waiting for transfers between devices  95.7 us (29%)
  starting transfers between devices  35.1 us (10%)
  Pallas kernels  34.5 us (10%)
  between operations  13.3 us (4%)
  local copies, waits for them, and re-layouts  9.56 us (3%)
    all_to_all x5, blocking collectives, exchange(): return lax.all_to_all(flat, axes, 0, 0, tiled=True).reshape(shape)  145 us
    all_to_all x3, waiting for transfers between devices, exchange(): return lax.all_to_all(flat, axes, 0, 0, tiled=True).reshape(shape)  79 us
    all_to_all x3, starting transfers between devices, exchange(): return lax.all_to_all(flat, axes, 0, 0, tiled=True).reshape(shape)  23.7 us
    pallas_call x2, Pallas kernels, solve_level(): pl.pallas_call(kernel, in_specs=[VMEM, HBM], out_specs=[VMEM, VMEM], out_...  18.4 us
    ppermute x2, waiting for transfers between devices, to_owner(): return lax.ppermute(values, ALL, pairs)  14.1 us
    ppermute x2, starting transfers between devices, to_owner(): return lax.ppermute(values, ALL, pairs)  9.37 us
  transfers between devices with their start and end apart: 9, of which 6 were waited for; matrix products, arithmetic and copies ran while one was open for 1% of the time, Pallas kernels for 6%

profile of v6, /device:TPU:72, one launch (start us, length us, event | category | flops | bytes accessed | tf_op | source)
XLA Modules:
  0.0 334.2 jit_solution(7202485328019056765)
XLA Ops:
  6.5 0.9 slice.21
  7.5 1.9 slice.14
  9.4 5.9 %collective-permute-start = (bf16[8,16,256]{2,1,0:T(8,128)(2,1)S(1)}, bf16[8,16,256]{2,1,0:T(8,128)(2,1)S(1)}, u32[]{:S(2)}, u32[]{:S(2)}) collective-permute-start(bf16[8,16,256]{2,1,0:T(8,128)(2,1)S(1)} %slice.21), channel_id=1, source_target_pairs={{0,0},{1,32},{2,64},{3,96},{4,128},{5,160},{6,192},{7,224},{8,256}... | collective-permute-start | bytes 196616 | tf_op jit(solution)/shard_map/ppermute | solution.py:297
  15.3 6.1 %collective-permute-done = bf16[8,16,256]{2,1,0:T(8,128)(2,1)S(1)} collective-permute-done((bf16[8,16,256]{2,1,0:T(8,128)(2,1)S(1)}, bf16[8,16,256]{2,1,0:T(8,128)(2,1)S(1)}, u32[]{:S(2)}, u32[]{:S(2)}) %collective-permute-start) | collective-permute-done | bytes 65568 | tf_op jit(solution)/shard_map/ppermute | solution.py:297
  21.4 1.6 broadcast_in_dim.17
  23.0 13.7 %all-to-all-start = ((bf16[32,128,256]{2,1,0:T(8,128)(2,1)}), bf16[32,128,256]{2,1,0:T(8,128)(2,1)}, u32[]{:S(2)}, u32[]{:S(2)}) async-start(bf16[32,128,256]{2,1,0:T(8,128)(2,1)} %broadcast_in_dim.17), calls=%async_computation | async-start | bytes 4194304 | tf_op jit(solution)/shard_map/all_to_all | solution.py:286
  37.2 1.2 copy-done.2
  38.5 4.5 %stack_upper.2 = bf16[12,128,256]{2,1,0:T(8,128)(2,1)} custom-call(s32[676]{0:T(1024)S(1)} %concatenate.6.meta_ref, bf16[15,128,256]{2,1,0:T(8,128)(2,1)S(1)} %copy-done.2, bf16[14,3,256,128]{3,2,1,0:T(8,128)(2,1)S(1)} %copy-done), custom_call_target="tpu_custom_call" | custom-call | tf_op jit(solution)/shard_map/stack_upper/pallas_call | solution.py:68
  43.0 1.2 copy-done.3
  44.2 0.8 stack_upper.3
  45.1 0.7 copy-done.4
  45.8 40.3 %all-to-all-done = bf16[32,128,256]{2,1,0:T(8,128)(2,1)} async-done(((bf16[32,128,256]{2,1,0:T(8,128)(2,1)}), bf16[32,128,256]{2,1,0:T(8,128)(2,1)}, u32[]{:S(2)}, u32[]{:S(2)}) %all-to-all-start) | async-done | bytes 2097184 | tf_op jit(solution)/shard_map/all_to_all | solution.py:286
  86.1 6.6 %solve_leaves.1 = (f32[8,32,128]{2,1,0:T(8,128)}, bf16[8,8,32,128]{3,2,1,0:T(8,128)(2,1)}) custom-call(bf16[32,8,16,256]{3,2,1,0:T(8,128)(2,1)} %bitcast.1.b_ref, bf16[16,8,128,256]{3,2,1,0:T(8,128)(2,1)} %bitcast.33), custom_call_target="tpu_custom_call" | custom-call | tf_op jit(solution)/shard_map/solve_leaves/pallas_call | solution.py:105
  92.8 24.3 %all_to_all.40 = bf16[8,256,128]{2,1,0:T(8,128)(2,1)S(1)} all-to-all(bf16[8,256,128]{2,1,0:T(8,128)(2,1)} %bitcast.37), channel_id=1, replica_groups=mesh['x'=4,'y'=8,'z'=8,'core'=2] {'z'}, dimensions={0} | all-to-all | bytes 1048576 | tf_op jit(solution)/shard_map/all_to_all | solution.py:286
  117.9 1.9 collective-permute-start.1
  119.8 1.9 collective-permute-done.1.b_ref
  121.7 2.4 update_from_leaves.1
  124.1 53.1 %all_to_all.41 = bf16[32,224,128]{2,1,0:T(8,128)(2,1)S(1)} all-to-all(bf16[32,224,128]{2,1,0:T(8,128)(2,1)S(1)} %bitcast.24), channel_id=1, replica_groups=mesh['x'=4,'y'=8,'z'=8,'core'=2] {'x','y'}, dimensions={0} | all-to-all | bytes 3670016 | tf_op jit(solution)/shard_map/all_to_all | solution.py:286
  177.4 3.4 %collective-permute-start.2 = (bf16[7,32,128]{2,1,0:T(8,128)(2,1)S(1)}, bf16[7,32,128]{2,1,0:T(8,128)(2,1)S(1)}, u32[]{:S(2)}, u32[]{:S(2)}) collective-permute-start(bf16[7,32,128]{2,1,0:T(8,128)(2,1)S(1)} %first_residual.1), channel_id=1, source_target_pairs={{0,0},{1,32},{2,64},{3,96},{4,128},{5,160},{6,192},{7,224},{8,256}... | collective-permute-start | bytes 172040 | tf_op jit(solution)/shard_map/ppermute | solution.py:297
  180.9 8.0 %collective-permute-done.2 = bf16[7,32,128]{2,1,0:T(8,128)(2,1)S(1)} collective-permute-done((bf16[7,32,128]{2,1,0:T(8,128)(2,1)S(1)}, bf16[7,32,128]{2,1,0:T(8,128)(2,1)S(1)}, u32[]{:S(2)}, u32[]{:S(2)}) %collective-permute-start.2) | collective-permute-done | bytes 57376 | tf_op jit(solution)/shard_map/ppermute | solution.py:297
  189.1 36.8 %all_to_all.42 = bf16[32,128,128]{2,1,0:T(8,128)(2,1)} all-to-all(bf16[32,128,128]{2,1,0:T(8,128)(2,1)S(1)} %broadcast_in_dim.19), channel_id=1, replica_groups=mesh['x'=4,'y'=8,'z'=8,'core'=2] {'x','y'}, dimensions={0} | all-to-all | bytes 2097152 | tf_op jit(solution)/shard_map/all_to_all | solution.py:286
  225.9 11.2 %solve_level.2 = (f32[4,32,128]{2,1,0:T(8,128)}, bf16[32,3,32,128]{3,2,1,0:T(8,128)(2,1)}) custom-call(bf16[32,4,32,128]{3,2,1,0:T(8,128)(2,1)} %bitcast.34, bf16[16,12,128,256]{3,2,1,0:T(8,128)(2,1)} %bitcast.32), custom_call_target="tpu_custom_call" | custom-call | tf_op jit(solution)/shard_map/solve_level/pallas_call | solution.py:227
  237.1 5.1 %all-to-all-start.4 = ((bf16[32,96,128]{2,1,0:T(8,128)(2,1)}), bf16[32,96,128]{2,1,0:T(8,128)(2,1)S(1)}, u32[]{:S(2)}, u32[]{:S(2)}) async-start(bf16[32,96,128]{2,1,0:T(8,128)(2,1)} %bitcast.36), calls=%async_computation.4 | async-start | bytes 1572864 | tf_op jit(solution)/shard_map/all_to_all | solution.py:286
  242.2 22.1 %all-to-all-done.4 = bf16[32,96,128]{2,1,0:T(8,128)(2,1)S(1)} async-done(((bf16[32,96,128]{2,1,0:T(8,128)(2,1)}), bf16[32,96,128]{2,1,0:T(8,128)(2,1)S(1)}, u32[]{:S(2)}, u32[]{:S(2)}) %all-to-all-start.4) | async-done | bytes 786464 | tf_op jit(solution)/shard_map/all_to_all | solution.py:286
  264.3 0.9 next_residual.2
  265.2 4.9 %all-to-all-start.5 = ((bf16[32,64,128]{2,1,0:T(8,128)(2,1)}), bf16[32,64,128]{2,1,0:T(8,128)(2,1)S(1)}, u32[]{:S(2)}, u32[]{:S(2)}) async-start(bf16[32,64,128]{2,1,0:T(8,128)(2,1)} %bitcast.15), calls=%async_computation.5 | async-start | bytes 1048576 | tf_op jit(solution)/shard_map/all_to_all | solution.py:286
  270.2 16.6 %all-to-all-done.5 = bf16[32,64,128]{2,1,0:T(8,128)(2,1)S(1)} async-done(((bf16[32,64,128]{2,1,0:T(8,128)(2,1)}), bf16[32,64,128]{2,1,0:T(8,128)(2,1)S(1)}, u32[]{:S(2)}, u32[]{:S(2)}) %all-to-all-start.5) | async-done | bytes 524320 | tf_op jit(solution)/shard_map/all_to_all | solution.py:286
  286.8 0.8 copy-done.6
  287.6 7.3 %solve_level.3 = (f32[2,32,128]{2,1,0:T(8,128)}, bf16[32,1,32,128]{3,2,1,0:T(8,128)(2,1)}) custom-call(bf16[32,2,32,128]{3,2,1,0:T(8,128)(2,1)} %bitcast.35, bf16[16,5,128,256]{3,2,1,0:T(8,128)(2,1)} %bitcast.22), custom_call_target="tpu_custom_call" | custom-call | tf_op jit(solution)/shard_map/solve_level/pallas_call | solution.py:227
  294.8 15.8 %all_to_all.43 = bf16[32,32,128]{2,1,0:T(8,128)(2,1)S(1)} all-to-all(bf16[32,32,128]{2,1,0:T(8,128)(2,1)} %bitcast.38), channel_id=1, replica_groups=mesh['x'=4,'y'=8,'z'=8,'core'=2] {'x','y'}, dimensions={0} | all-to-all | bytes 524288 | tf_op jit(solution)/shard_map/all_to_all | solution.py:286
  310.7 15.4 %all_to_all.44 = bf16[32,32,128]{2,1,0:T(8,128)(2,1)S(1)} all-to-all(bf16[32,32,128]{2,1,0:T(8,128)(2,1)S(1)} %bitcast.30), channel_id=1, replica_groups=mesh['x'=4,'y'=8,'z'=8,'core'=2] {'x','y'}, dimensions={0} | all-to-all | bytes 524288 | tf_op jit(solution)/shard_map/all_to_all | solution.py:286
  327.0 0.7 pad_maximum_fusion
  (36 shorter events, 2.7 us)
Async XLA Ops:
  6.5 79.6 %all-gather.7.cloned.1.call-start = ((), (), s32[]{:S(2)}) async-start(), calls=%async_computation.8 | async-start | bytes 8912896 | tf_op jit(solution)/shard_map/all_gather | solution.py:308
  9.4 12.0 %collective-permute-start = (bf16[8,16,256]{2,1,0:T(8,128)(2,1)S(1)}, bf16[8,16,256]{2,1,0:T(8,128)(2,1)S(1)}, u32[]{:S(2)}, u32[]{:S(2)}) collective-permute-start(bf16[8,16,256]{2,1,0:T(8,128)(2,1)S(1)} %slice.21), channel_id=1, source_target_pairs={{0,0},{1,32},{2,64},{3,96},{4,128},{5,160},{6,192},{7,224},{8,256}... | collective-permute-start | bytes 196616 | tf_op jit(solution)/shard_map/ppermute | solution.py:297
  21.4 15.4 %copy-start.10 = (s32[14,16,3]{1,0,2:T(8,128)S(1)}, s32[14,16,3]{1,0,2:T(8,128)}, u32[]{:S(2)}) copy-start(s32[14,16,3]{1,0,2:T(8,128)} %param.7) | copy-start | bytes 8068
  23.0 14.2 %copy-start = (bf16[14,3,256,128]{3,2,1,0:T(8,128)(2,1)S(1)}, bf16[14,3,256,128]{3,2,1,0:T(8,128)(2,1)}, u32[]{:S(2)}) copy-start(bf16[14,3,256,128]{3,2,1,0:T(8,128)(2,1)} %p_ref.5) | copy-start | bytes 8257540
  23.0 63.1 %all-to-all-start = ((bf16[32,128,256]{2,1,0:T(8,128)(2,1)}), bf16[32,128,256]{2,1,0:T(8,128)(2,1)}, u32[]{:S(2)}, u32[]{:S(2)}) async-start(bf16[32,128,256]{2,1,0:T(8,128)(2,1)} %broadcast_in_dim.17), calls=%async_computation | async-start | bytes 4194304 | tf_op jit(solution)/shard_map/all_to_all | solution.py:286
  36.7 189.2 %all-gather.9.cloned.1.call-start = ((), (), s32[]{:S(2)}) async-start(), calls=%async_computation.9 | async-start | bytes 13369344 | tf_op jit(solution)/shard_map/all_gather | solution.py:323
  37.2 1.2 copy-start.2
  43.0 1.2 copy-start.3
  45.1 0.7 copy-start.4
  86.1 35.5 %copy-start.5 = (f32[15,16,256]{2,1,0:T(8,128)S(1)}, f32[15,16,256]{2,1,0:T(8,128)}, u32[]{:S(2)}) copy-start(f32[15,16,256]{2,1,0:T(8,128)} %r_ref.1) | copy-start | bytes 737284
  117.1 153.0 %all-gather.11.cloned.1.call-start = ((), (), s32[]{:S(2)}) async-start(), calls=%async_computation.10 | async-start | bytes 5570560 | tf_op jit(solution)/shard_map/all_gather | solution.py:324
  117.9 3.8 %collective-permute-start.1 = (bf16[8,8,32,128]{3,2,1,0:T(8,128)(2,1)S(1)}, bf16[8,8,32,128]{3,2,1,0:T(8,128)(2,1)S(1)}, u32[]{:S(2)}, u32[]{:S(2)}) collective-permute-start(bf16[8,8,32,128]{3,2,1,0:T(8,128)(2,1)S(1)} %bitcast.27), channel_id=1, source_target_pairs={{0,1},{1,0},{2,3},{3,2},{4,5},{5,4},{6,7},{7,6},{8,9},{9,8},{10,11... | collective-permute-start | bytes 1572872 | tf_op jit(solution)/shard_map/ppermute | solution.py:321
  177.4 11.4 %collective-permute-start.2 = (bf16[7,32,128]{2,1,0:T(8,128)(2,1)S(1)}, bf16[7,32,128]{2,1,0:T(8,128)(2,1)S(1)}, u32[]{:S(2)}, u32[]{:S(2)}) collective-permute-start(bf16[7,32,128]{2,1,0:T(8,128)(2,1)S(1)} %first_residual.1), channel_id=1, source_target_pairs={{0,0},{1,32},{2,64},{3,96},{4,128},{5,160},{6,192},{7,224},{8,256}... | collective-permute-start | bytes 172040 | tf_op jit(solution)/shard_map/ppermute | solution.py:297
  237.1 27.2 %all-to-all-start.4 = ((bf16[32,96,128]{2,1,0:T(8,128)(2,1)}), bf16[32,96,128]{2,1,0:T(8,128)(2,1)S(1)}, u32[]{:S(2)}, u32[]{:S(2)}) async-start(bf16[32,96,128]{2,1,0:T(8,128)(2,1)} %bitcast.36), calls=%async_computation.4 | async-start | bytes 1572864 | tf_op jit(solution)/shard_map/all_to_all | solution.py:286
  265.2 21.5 %all-to-all-start.5 = ((bf16[32,64,128]{2,1,0:T(8,128)(2,1)}), bf16[32,64,128]{2,1,0:T(8,128)(2,1)S(1)}, u32[]{:S(2)}, u32[]{:S(2)}) async-start(bf16[32,64,128]{2,1,0:T(8,128)(2,1)} %bitcast.15), calls=%async_computation.5 | async-start | bytes 1048576 | tf_op jit(solution)/shard_map/all_to_all | solution.py:286
  286.8 0.8 copy-start.6
  287.6 38.5 %copy-start.1 = (bf16[80,128,256]{2,1,0:T(8,128)(2,1)S(1)}, bf16[80,128,256]{2,1,0:T(8,128)(2,1)}, u32[]{:S(2)}) copy-start(bf16[80,128,256]{2,1,0:T(8,128)(2,1)} %all-gather.11.cloned.1.call-done) | copy-start | bytes 15728644
  326.1 0.9 copy-start.7
  326.1 0.9 copy-start.8
  326.1 0.9 copy-start.9
Sparse Core Ops, SparseCore 0:
  9.5 60.7 all-gather.6
  117.2 73.9 all-gather.8
  193.4 47.5 all-gather.10

commit v7 on v6

v7 whole, which is shorter than its diff:
```python
import jax
import jax.numpy as jnp
from jax import lax
from jax.experimental import pallas as pl
from jax.experimental.pallas import tpu as pltpu
from jax.sharding import Mesh
from jax.sharding import PartitionSpec as P

ROW = ("x", "y")
COL = ("z", "core")
ALL = ("x", "y", "z", "core")
NR = 32
NC = 16
VMEM_LIMIT = 24 * 1024 * 1024
STREAM_LIMIT = 56 * 1024 * 1024
F32 = jnp.float32
BF16 = jnp.bfloat16
VMEM = pl.BlockSpec(memory_space=pltpu.VMEM)
SMEM = pl.BlockSpec(memory_space=pltpu.SMEM)
HBM = pl.BlockSpec(memory_space=pltpu.HBM)


def params(n=1, limit=VMEM_LIMIT):
    return pltpu.CompilerParams(
        vmem_limit_bytes=limit, dimension_semantics=("arbitrary",) * n
    )


def dot_t(a, b):
    return lax.dot_general(a, b, (((1,), (1,)), ((), ())), preferred_element_type=F32)


def slot_of(meta, source, target):
    base = 4 + (source * NC + meta[0]) * 3
    second = jnp.where(meta[base + 1] == target, 1, 0)
    slot = jnp.where(meta[base + 2] == target, 2, second)
    return slot, meta[base + slot] == target


def selected(meta_ref, p_ref, source, target):
    slot, found = slot_of(meta_ref, source, target)
    block = p_ref[source, slot]
    return jnp.where(found, block, jnp.zeros_like(block))


MIRRORED_UPPER = [(9, 12), (9, 14), (11, 13), (11, 14), (13, 14)]
MIRRORED_LEAF = [(2, 9), (3, 9), (6, 11), (7, 11), (4, 13), (5, 13), (6, 13), (7, 13)]


def mirrored_weights(meta, inverse, panels):
    def kernel(meta_ref, d_ref, p_ref, upper_ref, leaf_ref):
        for i in range(3):
            upper_ref[i] = d_ref[9 + 2 * i]
        for i, (source, target) in enumerate(MIRRORED_UPPER):
            block = selected(meta_ref, p_ref, source, target)
            upper_ref[3 + i, :, :128] = block[:128]
            upper_ref[3 + i, :, 128:] = block[128:]
        for i, (source, target) in enumerate(MIRRORED_LEAF):
            leaf_ref[i] = selected(meta_ref, p_ref, source, target)

    return pl.pallas_call(
        kernel,
        in_specs=[SMEM, VMEM, VMEM],
        out_specs=[VMEM, VMEM],
        out_shape=[
            jax.ShapeDtypeStruct((8, 128, 256), BF16),
            jax.ShapeDtypeStruct((8, 256, 128), BF16),
        ],
        compiler_params=params(0),
        name="mirrored_weights",
    )(meta, inverse, panels)


def stack_weights(meta, inverse, panels, got):
    def kernel(meta_ref, d_ref, p_ref, g_ref, two_ref, one_ref):
        def join(out_ref, place, source, target, index):
            block = selected(meta_ref, p_ref, source, target)
            for half in range(2):
                rows = slice(128 * half, 128 * half + 128)
                out_ref[place + half, :, :128] = block[rows]
                out_ref[place + half, :, 128:] = g_ref[index, :, rows]

        two_ref[0] = d_ref[8]
        two_ref[1] = d_ref[10]
        two_ref[2] = g_ref[0]
        two_ref[3] = g_ref[1]
        join(two_ref, 4, 8, 12, 3)
        join(two_ref, 6, 10, 13, 5)
        join(two_ref, 8, 8, 14, 4)
        join(two_ref, 10, 10, 14, 6)
        one_ref[0] = d_ref[12]
        one_ref[1] = g_ref[2]
        one_ref[2] = d_ref[14]
        join(one_ref, 3, 12, 14, 7)

    return pl.pallas_call(
        kernel,
        in_specs=[SMEM, VMEM, VMEM, VMEM],
        out_specs=[VMEM, VMEM],
        out_shape=[
            jax.ShapeDtypeStruct((12, 128, 256), BF16),
            jax.ShapeDtypeStruct((5, 128, 256), BF16),
        ],
        compiler_params=params(0),
        name="stack_weights",
    )(meta, inverse, panels, got)


def solve_leaves(spread, inverse):
    def kernel(b_ref, d_hbm, x_ref, h_ref, d_ref, sem):
        copies = [pltpu.make_async_copy(d_hbm.at[c], d_ref.at[c], sem.at[c]) for c in range(NC)]
        for copy in copies:
            copy.start()
        for c in range(NC):
            copies[c].wait()
            for n in range(8):
                left = b_ref[2 * c : 2 * c + 2, n].reshape(32, 256)
                value = dot_t(left, d_ref[c, n])
                if c:
                    value = value + x_ref[n]
                x_ref[n] = value
        for n in range(8):
            half = x_ref[n].astype(BF16)
            for z in range(8):
                h_ref[z, n] = half

    return pl.pallas_call(
        kernel,
        in_specs=[VMEM, HBM],
        out_specs=[VMEM, VMEM],
        out_shape=[
            jax.ShapeDtypeStruct((8, 32, 128), F32),
            jax.ShapeDtypeStruct((8, 8, 32, 128), BF16),
        ],
        scratch_shapes=[
            pltpu.VMEM((NC, 8, 128, 256), BF16),
            pltpu.SemaphoreType.DMA((NC,)),
        ],
        compiler_params=params(0, STREAM_LIMIT),
        name="solve_leaves",
    )(spread, inverse)


def update_from_leaves(meta, own, other, panels, leaf_got, right, right_got):
    def kernel(meta_ref, a_ref, b_ref, p_ref, g_ref, r_ref, rg_ref, o_ref):
        core, row = meta_ref[1], meta_ref[2]
        for t in range(7):
            target = 8 + t
            if t < 4:
                sources = range(2 * t, 2 * t + 2)
            elif t < 6:
                sources = range(4 * (t - 4), 4 * (t - 4) + 4)
            else:
                sources = range(8)
            if t in (1, 3, 5):
                blocks = [g_ref[MIRRORED_LEAF.index((s, target))] for s in sources]
            else:
                blocks = [selected(meta_ref, p_ref, s, target) for s in sources]
            for parity, x_ref in ((core, a_ref), (1 - core, b_ref)):
                acc = jnp.zeros((256, 256), F32)
                for s, block in zip(sources, blocks, strict=True):
                    acc = acc + dot_t(x_ref[:, s].reshape(256, 128), block)
                for half in range(2):
                    side = 1 - half if t in (1, 3, 5) else half
                    value = acc[:, 128 * side : 128 * side + 128].astype(BF16)
                    o_ref[:, pl.ds(parity, 1), half, t] = value.reshape(8, 1, 32, 128)
        z, parity = row // 4, (row // 2) % 2
        start = pl.multiple_of(16 * (row % 2), 16)
        for half in range(2):
            for t in range(7):
                part = o_ref[z, parity, half, t, pl.ds(start, 16), :].astype(F32)
                if t in (1, 3, 5):
                    held = rg_ref[t // 2, :, 128 * (1 - half) : 128 * (1 - half) + 128]
                else:
                    held = r_ref[8 + t, :, 128 * half : 128 * half + 128]
                o_ref[z, parity, half, t, pl.ds(start, 16), :] = (part - held).astype(BF16)

    return pl.pallas_call(
        kernel,
        grid=(1,),
        in_specs=[
            SMEM,
            VMEM,
            VMEM,
            pl.BlockSpec((8, 3, 256, 128), lambda i: (0, 0, 0, 0)),
            VMEM,
            VMEM,
            VMEM,
        ],
        out_specs=VMEM,
        out_shape=jax.ShapeDtypeStruct((8, 2, 2, 7, 32, 128), BF16),
        compiler_params=params(),
        name="update_from_leaves",
    )(meta, own, other, panels, leaf_got, right, right_got)


def first_residual(parts):
    def kernel(p_ref, o_ref):
        o_ref[...] = (-jnp.sum(p_ref[...].astype(F32), axis=0)).astype(BF16)

    return pl.pallas_call(
        kernel,
        in_specs=[VMEM],
        out_specs=VMEM,
        out_shape=jax.ShapeDtypeStruct((7, 32, 128), BF16),
        compiler_params=params(0),
        name="first_residual",
    )(parts)


def first_payload(meta, residual):
    def kernel(meta_ref, x_ref, o_ref):
        row = meta_ref[2]
        for r in range(NR):
            for p in range(2):
                o_ref[r, p] = jnp.where(row <= r, x_ref[2 * p], x_ref[2 * p + 1])

    return pl.pallas_call(
        kernel,
        in_specs=[SMEM, VMEM],
        out_specs=VMEM,
        out_shape=jax.ShapeDtypeStruct((NR, 2, 32, 128), BF16),
        compiler_params=params(0),
        name="first_payload",
    )(meta, residual)


def solve_level(meta, spread, local, places, weights, targets):
    pairs = len(places)
    used = min(b for terms, _ in targets for _, b in terms)

    def kernel(meta_ref, x_ref, y_ref, w_hbm, natural_ref, mirrored_ref, o_ref, w_ref, sem):
        row = meta_ref[2]
        pieces = [(c, slice(0, 2 * pairs)) for c in range(NC)]
        pieces += [(c, slice(used, None)) for c in range(NC)]
        copies = [
            pltpu.make_async_copy(w_hbm.at[piece], w_ref.at[piece], sem.at[i])
            for i, piece in enumerate(pieces)
        ]
        for copy in copies:
            copy.start()

        def mirrored_block(b, p):
            return jnp.where(row == b, y_ref[places[p]], x_ref[b, p])

        for c in range(NC):
            copies[c].wait()
            for p in range(pairs):
                left = jnp.concatenate([x_ref[2 * c, p], x_ref[2 * c + 1, p]], axis=1)
                value = dot_t(left, w_ref[c, p])
                left = jnp.concatenate(
                    [mirrored_block(31 - 2 * c, p), mirrored_block(30 - 2 * c, p)], axis=1
                )
                other = dot_t(left, w_ref[c, pairs + p])
                if c:
                    value = value + natural_ref[p]
                    other = other + mirrored_ref[p]
                natural_ref[p] = value
                mirrored_ref[p] = other
        joined = [
            jnp.concatenate([natural_ref[p].astype(BF16), mirrored_ref[p].astype(BF16)], axis=1)
            for p in range(pairs)
        ]
        for c in range(NC):
            copies[NC + c].wait()
            for t, (terms, flipped) in enumerate(targets):
                for half in range(2):
                    total = jnp.zeros((32, 128), F32)
                    for p, b in terms:
                        total = total + dot_t(joined[p], w_ref[c, b + half])
                    r = 2 * c + half
                    o_ref[31 - r if flipped else r, t] = total.astype(BF16)

    return pl.pallas_call(
        kernel,
        in_specs=[SMEM, VMEM, VMEM, HBM],
        out_specs=[VMEM, VMEM, VMEM],
        out_shape=[
            jax.ShapeDtypeStruct((pairs, 32, 128), F32),
            jax.ShapeDtypeStruct((pairs, 32, 128), F32),
            jax.ShapeDtypeStruct((NR, len(targets), 32, 128), BF16),
        ],
        scratch_shapes=[
            pltpu.VMEM(weights.shape, BF16),
            pltpu.SemaphoreType.DMA((2 * NC,)),
        ],
        compiler_params=params(0, STREAM_LIMIT),
        name="solve_level",
    )(meta, spread, local, weights)


def solve_node(x_ref, d_ref, n, place):
    acc = jnp.zeros((32, 128), F32)
    for c in range(NC):
        left = jnp.concatenate([x_ref[2 * c, n], x_ref[2 * c + 1, n]], axis=1)
        acc = acc + dot_t(left, d_ref[c, place])
    return acc


def solve_root(residual, inverse):
    def kernel(x_ref, d_ref, s_ref):
        s_ref[0] = solve_node(x_ref, d_ref, 0, 2)

    return pl.pallas_call(
        kernel,
        in_specs=[VMEM, VMEM],
        out_specs=VMEM,
        out_shape=jax.ShapeDtypeStruct((1, 32, 128), F32),
        compiler_params=params(0),
        name="solve_root",
    )(residual, inverse)


def next_residual(meta, parts, residual):
    def kernel(meta_ref, p_ref, x_ref, o_ref, local_ref, rest_ref):
        row = meta_ref[2]
        total = x_ref[4:].astype(F32) - jnp.sum(p_ref[...].astype(F32), axis=0)
        natural, mirrored = total[0].astype(BF16), total[1].astype(BF16)
        for r in range(NR):
            o_ref[r, 0] = jnp.where(row <= r, natural, mirrored)
        local_ref[0] = mirrored
        rest_ref[0] = total[2]

    return pl.pallas_call(
        kernel,
        in_specs=[SMEM, VMEM, VMEM],
        out_specs=[VMEM, VMEM, VMEM],
        out_shape=[
            jax.ShapeDtypeStruct((NR, 1, 32, 128), BF16),
            jax.ShapeDtypeStruct((1, 32, 128), BF16),
            jax.ShapeDtypeStruct((1, 32, 128), F32),
        ],
        compiler_params=params(0),
        name="next_residual",
    )(meta, parts, residual)


def last_residual(parts, rest):
    def kernel(p_ref, rest_ref, o_ref):
        half = (rest_ref[...] - jnp.sum(p_ref[...].astype(F32), axis=0)).astype(BF16)
        for r in range(NR):
            o_ref[r] = half

    return pl.pallas_call(
        kernel,
        in_specs=[VMEM, VMEM],
        out_specs=VMEM,
        out_shape=jax.ShapeDtypeStruct((NR, 1, 32, 128), BF16),
        compiler_params=params(0),
        name="last_residual",
    )(parts, rest)


def exchange(values, axes):
    shape = values.shape
    flat = values.reshape(shape[0], -1, shape[-1])
    return lax.all_to_all(flat, axes, 0, 0, tiled=True).reshape(shape)


def spread_over(values, axes, size):
    return exchange(jnp.broadcast_to(values[None], (size,) + values.shape), axes)


def to_owner(values):
    pairs = [
        (r * NC + c, (2 * c + r % 2) * NC + r // 2) for r in range(NR) for c in range(NC)
    ]
    return lax.ppermute(values, ALL, pairs)


def to_mirrored_row(values):
    pairs = [(r * NC + c, (31 - r) * NC + c) for r in range(NR) for c in range(NC)]
    return lax.ppermute(values, ALL, pairs)


def to_mirrored_column(values):
    pairs = [(r * NC + c, r * NC + 15 - c) for r in range(NR) for c in range(NC)]
    return lax.ppermute(values, ALL, pairs)


def per_device(right_sides, diag_inverse, panels, block_map):
    row = lax.axis_index(ROW)
    col = lax.axis_index(COL)
    core = lax.axis_index("core")
    leaf_right, diag_inverse = lax.optimization_barrier(
        (right_sides[:8].astype(BF16), diag_inverse)
    )
    moved = to_owner(leaf_right)
    leaf_inverse = lax.all_gather(diag_inverse[:8], COL, axis=0)

    zero = jnp.zeros((), jnp.int32)
    meta = jnp.concatenate(
        [jnp.stack([col, core, row, zero]).astype(jnp.int32), block_map.reshape(-1)]
    )
    upper_sent, leaf_sent = mirrored_weights(meta, diag_inverse, panels)
    leaf_got = to_mirrored_column(leaf_sent)
    right_got = to_mirrored_column(right_sides[9:14:2])
    stack_two, stack_one = stack_weights(
        meta, diag_inverse, panels, to_mirrored_row(upper_sent)
    )
    spread = spread_over(moved, ROW, NR)
    spread, stack_two, stack_one, leaf_got, right_got = lax.optimization_barrier(
        (spread, stack_two, stack_one, leaf_got, right_got)
    )

    leaves, copies = solve_leaves(spread, leaf_inverse)
    own = exchange(copies, "z")
    other = lax.ppermute(own, "core", [(0, 1), (1, 0)])
    stack_two, stack_one, own = lax.optimization_barrier((stack_two, stack_one, own))
    weights_two = lax.all_gather(stack_two, COL, axis=0)
    weights_one = lax.all_gather(stack_one, COL, axis=0)
    parts = update_from_leaves(meta, own, other, panels, leaf_got, right_sides, right_got)
    parts = exchange(parts.reshape(NR, 7, 32, 128), ROW)
    residual = to_owner(first_residual(parts))

    spread = exchange(first_payload(meta, residual), ROW)
    targets = [([(0, 4)], False), ([(1, 6)], True), ([(0, 8), (1, 10)], False)]
    two, two_mirrored, parts = solve_level(meta, spread, residual, [1, 3], weights_two, targets)
    spread, local, rest = next_residual(meta, exchange(parts, ROW), residual)
    spread = exchange(spread, ROW)
    one, one_mirrored, parts = solve_level(
        meta, spread, local, [0], weights_one, [([(0, 3)], False)]
    )
    back = to_mirrored_row(jnp.concatenate([two_mirrored, one_mirrored], axis=0))
    spread = last_residual(exchange(parts, ROW), rest)
    root = solve_root(exchange(spread, ROW), weights_one)
    upper = [two[:1], back[:1], two[1:], back[1:2], one, back[2:], root]
    return jnp.concatenate([leaves, *upper], axis=0)


def solution(mesh):
    split = Mesh(mesh.devices.reshape(4, 8, 8, 2), ALL)
    return jax.shard_map(
        per_device,
        mesh=split,
        in_specs=(P(None, ROW, COL), P(None, ROW, COL), P(None, None, COL, ROW), P()),
        out_specs=P(None, COL, ROW),
        check_vma=False,
    )
```

time: 335 us -> 352 us (1.051)
  the two profiles are of different devices: /device:TPU:72 before, /device:TPU:8 now
where the time goes in v7:
time: 352 us; the launch traced here: 351 us
  blocking collectives  150 us (43%)
  starting transfers between devices  71.2 us (20%)
  waiting for transfers between devices  69.5 us (20%)
  Pallas kernels  29.2 us (8%)
  local copies, waits for them, and re-layouts  16.8 us (5%)
  between operations  13.5 us (4%)
    all_to_all x4, blocking collectives, exchange(): return lax.all_to_all(flat, axes, 0, 0, tiled=True).reshape(shape)  150 us
    ppermute x2, waiting for transfers between devices, to_mirrored_row(): return lax.ppermute(values, ALL, pairs)  45.7 us
    all_to_all x4, starting transfers between devices, exchange(): return lax.all_to_all(flat, axes, 0, 0, tiled=True).reshape(shape)  44.2 us
    all_to_all x4, waiting for transfers between devices, exchange(): return lax.all_to_all(flat, axes, 0, 0, tiled=True).reshape(shape)  21.2 us
    pallas_call x2, Pallas kernels, solve_level(): pl.pallas_call(kernel, in_specs=[SMEM, VMEM, VMEM, HBM], out_specs=[VMEM,...  15.6 us
    ppermute x2, starting transfers between devices, to_mirrored_row(): return lax.ppermute(values, ALL, pairs)  15.3 us
    unnamed x48, local copies, waits for them, and re-layouts  8.57 us
    ppermute x2, starting transfers between devices, to_mirrored_column(): return lax.ppermute(values, ALL, pairs)  8.4 us
  transfers between devices with their start and end apart: 14, of which 5 were waited for; matrix products, arithmetic and copies ran while one was open for 1% of the time, Pallas kernels for 4%

profile of v7, /device:TPU:8, one launch (start us, length us, event | category | flops | bytes accessed | tf_op | source)
XLA Modules:
  0.0 350.8 jit_solution(2148875163737445929)
XLA Ops:
  6.5 0.9 slice.43
  7.5 1.9 slice.27
  10.0 1.6 broadcast_in_dim.9
  11.7 26.2 %all-to-all-start = ((bf16[32,128,256]{2,1,0:T(8,128)(2,1)}), bf16[32,128,256]{2,1,0:T(8,128)(2,1)}, u32[]{:S(2)}, u32[]{:S(2)}) async-start(bf16[32,128,256]{2,1,0:T(8,128)(2,1)} %broadcast_in_dim.9), calls=%async_computation | async-start | bytes 4194304 | tf_op jit(solution)/shard_map/all_to_all | solution.py:357
  38.4 1.2 copy-done.1
  40.5 7.7 %collective-permute-start.1 = (bf16[8,128,256]{2,1,0:T(8,128)(2,1)S(1)}, bf16[8,128,256]{2,1,0:T(8,128)(2,1)S(1)}, u32[]{:S(2)}, u32[]{:S(2)}) collective-permute-start(bf16[8,128,256]{2,1,0:T(8,128)(2,1)S(1)} %get-tuple-element.32), channel_id=1, source_target_pairs={{0,496},{1,497},{2,498},{3,499},{4,500},{5,501},{6,502},{7,503},{8... | collective-permute-start | bytes 1572872 | tf_op jit(solution)/shard_map/ppermute | solution.py:373
  48.1 6.5 %collective-permute-start.2 = (bf16[8,256,128]{2,1,0:T(8,128)(2,1)S(1)}, bf16[8,256,128]{2,1,0:T(8,128)(2,1)S(1)}, u32[]{:S(2)}, u32[]{:S(2)}) collective-permute-start(bf16[8,256,128]{2,1,0:T(8,128)(2,1)S(1)} %get-tuple-element.35), channel_id=1, source_target_pairs={{0,15},{1,14},{2,13},{3,12},{4,11},{5,10},{6,9},{7,8},{8,7},{9,6},... | collective-permute-start | bytes 1572872 | tf_op jit(solution)/shard_map/ppermute | solution.py:378
  54.6 1.9 collective-permute-start.3
  56.6 42.3 %collective-permute-done.1.g_ref = bf16[8,128,256]{2,1,0:T(8,128)(2,1)S(1)} collective-permute-done((bf16[8,128,256]{2,1,0:T(8,128)(2,1)S(1)}, bf16[8,128,256]{2,1,0:T(8,128)(2,1)S(1)}, u32[]{:S(2)}, u32[]{:S(2)}) %collective-permute-start.1) | collective-permute-done | bytes 524320 | tf_op jit(solution)/shard_map/ppermute | solution.py:373
  99.6 0.9 copy-done.2
  101.8 0.8 copy-done.4
  102.6 6.5 %solve_leaves.1 = (f32[8,32,128]{2,1,0:T(8,128)}, bf16[8,8,32,128]{3,2,1,0:T(8,128)(2,1)}) custom-call(bf16[32,8,16,256]{3,2,1,0:T(8,128)(2,1)} %bitcast.1.b_ref, bf16[16,8,128,256]{3,2,1,0:T(8,128)(2,1)} %bitcast.32), custom_call_target="tpu_custom_call" | custom-call | tf_op jit(solution)/shard_map/solve_leaves/pallas_call | solution.py:127
  109.2 26.0 %all_to_all.40 = bf16[8,256,128]{2,1,0:T(8,128)(2,1)S(1)} all-to-all(bf16[8,256,128]{2,1,0:T(8,128)(2,1)} %bitcast.37), channel_id=1, replica_groups=mesh['x'=4,'y'=8,'z'=8,'core'=2] {'z'}, dimensions={0} | all-to-all | bytes 1048576 | tf_op jit(solution)/shard_map/all_to_all | solution.py:357
  136.0 1.9 collective-permute-start.4
  137.9 1.9 collective-permute-done.4.b_ref
  139.8 1.0 copy-done.5
  141.6 2.4 update_from_leaves.1
  144.0 61.3 %all_to_all.41 = bf16[32,224,128]{2,1,0:T(8,128)(2,1)S(1)} all-to-all(bf16[32,224,128]{2,1,0:T(8,128)(2,1)S(1)} %bitcast.22), channel_id=1, replica_groups=mesh['x'=4,'y'=8,'z'=8,'core'=2] {'x','y'}, dimensions={0} | all-to-all | bytes 3670016 | tf_op jit(solution)/shard_map/all_to_all | solution.py:357
  207.0 36.7 %all_to_all.42 = bf16[32,64,128]{2,1,0:T(8,128)(2,1)} all-to-all(bf16[32,64,128]{2,1,0:T(8,128)(2,1)S(1)} %bitcast.25), channel_id=1, replica_groups=mesh['x'=4,'y'=8,'z'=8,'core'=2] {'x','y'}, dimensions={0} | all-to-all | bytes 1048576 | tf_op jit(solution)/shard_map/all_to_all | solution.py:357
  243.6 9.3 %solve_level.2 = (f32[2,32,128]{2,1,0:T(8,128)}, f32[2,32,128]{2,1,0:T(8,128)}, bf16[32,3,32,128]{3,2,1,0:T(8,128)(2,1)}) custom-call(s32[676]{0:T(1024)} %copy-done.9, bf16[32,2,32,128]{3,2,1,0:T(8,128)(2,1)} %bitcast.33, bf16[7,32,128]{2,1,0:T(8,128)(2,1)} %copy-done.6, bf16[16,12,128,256]{3,2,1,0:T(8,128)(2,1)} %bitcast.31), custom_call_target="tpu_custom_call" | custom-call | tf_op jit(solution)/shard_map/solve_level/pallas_call | solution.py:274
  252.9 25.8 %all_to_all.43 = bf16[32,96,128]{2,1,0:T(8,128)(2,1)S(1)} all-to-all(bf16[32,96,128]{2,1,0:T(8,128)(2,1)} %bitcast.36), channel_id=1, replica_groups=mesh['x'=4,'y'=8,'z'=8,'core'=2] {'x','y'}, dimensions={0} | all-to-all | bytes 1572864 | tf_op jit(solution)/shard_map/all_to_all | solution.py:357
  278.8 0.8 copy-done.7
  279.6 1.4 next_residual.1
  281.0 4.9 %all-to-all-start.5 = ((bf16[32,32,128]{2,1,0:T(8,128)(2,1)}), bf16[32,32,128]{2,1,0:T(8,128)(2,1)S(1)}, u32[]{:S(2)}, u32[]{:S(2)}) async-start(bf16[32,32,128]{2,1,0:T(8,128)(2,1)} %bitcast.15), calls=%async_computation.5 | async-start | bytes 524288 | tf_op jit(solution)/shard_map/all_to_all | solution.py:357
  286.0 11.0 %all-to-all-done.5 = bf16[32,32,128]{2,1,0:T(8,128)(2,1)S(1)} async-done(((bf16[32,32,128]{2,1,0:T(8,128)(2,1)}), bf16[32,32,128]{2,1,0:T(8,128)(2,1)S(1)}, u32[]{:S(2)}, u32[]{:S(2)}) %all-to-all-start.5) | async-done | bytes 262176 | tf_op jit(solution)/shard_map/all_to_all | solution.py:357
  297.7 6.3 %solve_level.3 = (f32[1,32,128]{2,1,0:T(8,128)}, f32[1,32,128]{2,1,0:T(8,128)}, bf16[32,1,32,128]{3,2,1,0:T(8,128)(2,1)}) custom-call(s32[676]{0:T(1024)} %copy-done.9, bf16[32,1,32,128]{3,2,1,0:T(8,128)(2,1)} %bitcast.34, bf16[1,32,128]{2,1,0:T(8,128)(2,1)} %copy-done.13, bf16[16,5,128,256]{3,2,1,0:T(8,128)(2,1)} %bitcast.29), custom_call_target="tpu_custom_call" | custom-call | tf_op jit(solution)/shard_map/solve_level/pallas_call | solution.py:274
  304.0 4.4 %all-to-all-start.6 = ((bf16[32,32,128]{2,1,0:T(8,128)(2,1)}), bf16[32,32,128]{2,1,0:T(8,128)(2,1)S(1)}, u32[]{:S(2)}, u32[]{:S(2)}) async-start(bf16[32,32,128]{2,1,0:T(8,128)(2,1)} %bitcast.38), calls=%async_computation.6 | async-start | bytes 524288 | tf_op jit(solution)/shard_map/all_to_all | solution.py:357
  309.2 7.7 %collective-permute-start.6 = (f32[3,32,128]{2,1,0:T(8,128)S(1)}, f32[3,32,128]{2,1,0:T(8,128)S(1)}, u32[]{:S(2)}, u32[]{:S(2)}) collective-permute-start(f32[3,32,128]{2,1,0:T(8,128)S(1)} %pad_maximum_fusion), channel_id=1, source_target_pairs={{0,496},{1,497},{2,498},{3,499},{4,500},{5,501},{6,502},{7,503},{8... | collective-permute-start | bytes 147464 | tf_op jit(solution)/shard_map/ppermute | solution.py:373
  316.9 3.4 collective-permute-done.6
  321.1 8.7 %all-to-all-start.7 = ((bf16[32,32,128]{2,1,0:T(8,128)(2,1)}), bf16[32,32,128]{2,1,0:T(8,128)(2,1)S(1)}, u32[]{:S(2)}, u32[]{:S(2)}) async-start(bf16[32,32,128]{2,1,0:T(8,128)(2,1)} %bitcast.20), calls=%async_computation.7 | async-start | bytes 524288 | tf_op jit(solution)/shard_map/all_to_all | solution.py:357
  330.5 10.2 %all-to-all-done.7 = bf16[32,32,128]{2,1,0:T(8,128)(2,1)S(1)} async-done(((bf16[32,32,128]{2,1,0:T(8,128)(2,1)}), bf16[32,32,128]{2,1,0:T(8,128)(2,1)S(1)}, u32[]{:S(2)}, u32[]{:S(2)}) %all-to-all-start.7) | async-done | bytes 262176 | tf_op jit(solution)/shard_map/all_to_all | solution.py:357
  340.7 3.5 %solve_root.1 = f32[15,32,128]{2,1,0:T(8,128)} fusion(f32[15,32,128]{2,1,0:T(8,128)} %copy-done.16, s32[]{} %constant.31, bf16[32,1,32,128]{3,2,1,0:T(8,128)(2,1)S(1)} %bitcast.35, bf16[16,5,128,256]{3,2,1,0:T(8,128)(2,1)} %bitcast.30), kind=kCustom, calls=%fused_computation.2 | custom fusion | bytes 5525504 | tf_op jit(solution)/shard_map/solve_root/pallas_call | solution.py:304
  (69 shorter events, 10.2 us)
Async XLA Ops:
  6.5 96.1 %all-gather.7.cloned.1.call-start = ((), (), s32[]{:S(2)}) async-start(), calls=%async_computation.8 | async-start | bytes 8912896 | tf_op jit(solution)/shard_map/all_gather | solution.py:389
  9.4 0.7 collective-permute-start
  10.0 27.9 %copy-start.19 = (s32[14,16,3]{1,0,2:T(8,128)S(1)}, s32[14,16,3]{1,0,2:T(8,128)}, u32[]{:S(2)}) copy-start(s32[14,16,3]{1,0,2:T(8,128)} %param.7) | copy-start | bytes 8068
  11.7 26.7 %copy-start = (bf16[14,3,256,128]{3,2,1,0:T(8,128)(2,1)S(1)}, bf16[14,3,256,128]{3,2,1,0:T(8,128)(2,1)}, u32[]{:S(2)}) copy-start(bf16[14,3,256,128]{3,2,1,0:T(8,128)(2,1)} %p_ref.5) | copy-start | bytes 8257540
  11.7 90.9 %all-to-all-start = ((bf16[32,128,256]{2,1,0:T(8,128)(2,1)}), bf16[32,128,256]{2,1,0:T(8,128)(2,1)}, u32[]{:S(2)}, u32[]{:S(2)}) async-start(bf16[32,128,256]{2,1,0:T(8,128)(2,1)} %broadcast_in_dim.9), calls=%async_computation | async-start | bytes 4194304 | tf_op jit(solution)/shard_map/all_to_all | solution.py:357
  37.9 16.7 %copy-start.3 = (f32[15,16,256]{2,1,0:T(8,128)S(1)}, f32[15,16,256]{2,1,0:T(8,128)}, u32[]{:S(2)}) copy-start(f32[15,16,256]{2,1,0:T(8,128)} %r_ref.1) | copy-start | bytes 737284
  37.9 205.7 %all-gather.9.cloned.1.call-start = ((), (), s32[]{:S(2)}) async-start(), calls=%async_computation.9 | async-start | bytes 13369344 | tf_op jit(solution)/shard_map/all_gather | solution.py:410
  38.4 1.2 copy-start.1
  39.6 166.6 %copy-start.9 = (s32[676]{0:T(1024)}, s32[676]{0:T(1024)S(1)}, u32[]{:S(2)}) copy-start(s32[676]{0:T(1024)S(1)} %concatenate.9.meta_ref) | copy-start | bytes 8116
  40.5 58.4 %collective-permute-start.1 = (bf16[8,128,256]{2,1,0:T(8,128)(2,1)S(1)}, bf16[8,128,256]{2,1,0:T(8,128)(2,1)S(1)}, u32[]{:S(2)}, u32[]{:S(2)}) collective-permute-start(bf16[8,128,256]{2,1,0:T(8,128)(2,1)S(1)} %get-tuple-element.32), channel_id=1, source_target_pairs={{0,496},{1,497},{2,498},{3,499},{4,500},{5,501},{6,502},{7,503},{8... | collective-permute-start | bytes 1572872 | tf_op jit(solution)/shard_map/ppermute | solution.py:373
  48.1 53.7 %collective-permute-start.2 = (bf16[8,256,128]{2,1,0:T(8,128)(2,1)S(1)}, bf16[8,256,128]{2,1,0:T(8,128)(2,1)S(1)}, u32[]{:S(2)}, u32[]{:S(2)}) collective-permute-start(bf16[8,256,128]{2,1,0:T(8,128)(2,1)S(1)} %get-tuple-element.35), channel_id=1, source_target_pairs={{0,15},{1,14},{2,13},{3,12},{4,11},{5,10},{6,9},{7,8},{8,7},{9,6},... | collective-permute-start | bytes 1572872 | tf_op jit(solution)/shard_map/ppermute | solution.py:378
  54.6 46.6 %collective-permute-start.3 = (f32[3,16,256]{2,1,0:T(8,128)S(1)}, f32[3,16,256]{2,1,0:T(8,128)S(1)}, u32[]{:S(2)}, u32[]{:S(2)}) collective-permute-start(f32[3,16,256]{2,1,0:T(8,128)S(1)} %slice.26), channel_id=1, source_target_pairs={{0,15},{1,14},{2,13},{3,12},{4,11},{5,10},{6,9},{7,8},{8,7},{9,6},... | collective-permute-start | bytes 147464 | tf_op jit(solution)/shard_map/ppermute | solution.py:378
  99.6 0.9 copy-start.2
  100.5 0.7 copy-start.8
  101.8 0.8 copy-start.4
  135.2 150.7 %all-gather.11.cloned.1.call-start = ((), (), s32[]{:S(2)}) async-start(), calls=%async_computation.10 | async-start | bytes 5570560 | tf_op jit(solution)/shard_map/all_gather | solution.py:411
  136.0 3.8 %collective-permute-start.4 = (bf16[8,8,32,128]{3,2,1,0:T(8,128)(2,1)S(1)}, bf16[8,8,32,128]{3,2,1,0:T(8,128)(2,1)S(1)}, u32[]{:S(2)}, u32[]{:S(2)}) collective-permute-start(bf16[8,8,32,128]{3,2,1,0:T(8,128)(2,1)S(1)} %bitcast.26), channel_id=1, source_target_pairs={{0,1},{1,0},{2,3},{3,2},{4,5},{5,4},{6,7},{7,6},{8,9},{9,8},{10,11... | collective-permute-start | bytes 1572872 | tf_op jit(solution)/shard_map/ppermute | solution.py:408
  139.8 1.0 copy-start.5
  140.8 0.8 copy-start.12
  205.6 0.7 collective-permute-start.5
  206.3 37.3 %copy-start.6 = (bf16[7,32,128]{2,1,0:T(8,128)(2,1)}, bf16[7,32,128]{2,1,0:T(8,128)(2,1)S(1)}, u32[]{:S(2)}) copy-start(bf16[7,32,128]{2,1,0:T(8,128)(2,1)S(1)} %collective-permute-done.5.x_ref.y_ref) | copy-start | bytes 172036
  243.6 35.1 %copy-start.10 = (s32[676]{0:T(1024)S(1)}, s32[676]{0:T(1024)}, u32[]{:S(2)}) copy-start(s32[676]{0:T(1024)} %copy-done.9) | copy-start | bytes 8116
  252.9 33.0 %copy-start.15 = (f32[8,32,128]{2,1,0:T(8,128)S(1)}, f32[8,32,128]{2,1,0:T(8,128)}, u32[]{:S(2)}) copy-start(f32[8,32,128]{2,1,0:T(8,128)} %get-tuple-element.37) | copy-start | bytes 393220
  278.8 0.8 copy-start.7
  281.0 16.0 %copy-start.13 = (bf16[1,32,128]{2,1,0:T(8,128)(2,1)}, bf16[1,32,128]{2,1,0:T(8,128)(2,1)S(1)}, u32[]{:S(2)}) copy-start(bf16[1,32,128]{2,1,0:T(8,128)(2,1)S(1)} %get-tuple-element.49.y_ref) | copy-start | bytes 24580
  281.0 16.0 %all-to-all-start.5 = ((bf16[32,32,128]{2,1,0:T(8,128)(2,1)}), bf16[32,32,128]{2,1,0:T(8,128)(2,1)S(1)}, u32[]{:S(2)}, u32[]{:S(2)}) async-start(bf16[32,32,128]{2,1,0:T(8,128)(2,1)} %bitcast.15), calls=%async_computation.5 | async-start | bytes 524288 | tf_op jit(solution)/shard_map/all_to_all | solution.py:357
  297.7 10.8 %copy-start.17 = (f32[2,32,128]{2,1,0:T(8,128)S(1)}, f32[2,32,128]{2,1,0:T(8,128)}, u32[]{:S(2)}) copy-start(f32[2,32,128]{2,1,0:T(8,128)} %get-tuple-element.46) | copy-start | bytes 98308
  297.7 19.2 %copy-start.18 = (f32[2,32,128]{2,1,0:T(8,128)S(1)}, f32[2,32,128]{2,1,0:T(8,128)}, u32[]{:S(2)}) copy-start(f32[2,32,128]{2,1,0:T(8,128)} %get-tuple-element.45) | copy-start | bytes 98308
  304.0 16.3 %all-to-all-start.6 = ((bf16[32,32,128]{2,1,0:T(8,128)(2,1)}), bf16[32,32,128]{2,1,0:T(8,128)(2,1)S(1)}, u32[]{:S(2)}, u32[]{:S(2)}) async-start(bf16[32,32,128]{2,1,0:T(8,128)(2,1)} %bitcast.38), calls=%async_computation.6 | async-start | bytes 524288 | tf_op jit(solution)/shard_map/all_to_all | solution.py:357
  309.2 11.1 %collective-permute-start.6 = (f32[3,32,128]{2,1,0:T(8,128)S(1)}, f32[3,32,128]{2,1,0:T(8,128)S(1)}, u32[]{:S(2)}, u32[]{:S(2)}) collective-permute-start(f32[3,32,128]{2,1,0:T(8,128)S(1)} %pad_maximum_fusion), channel_id=1, source_target_pairs={{0,496},{1,497},{2,498},{3,499},{4,500},{5,501},{6,502},{7,503},{8... | collective-permute-start | bytes 147464 | tf_op jit(solution)/shard_map/ppermute | solution.py:373
  321.1 19.6 %all-to-all-start.7 = ((bf16[32,32,128]{2,1,0:T(8,128)(2,1)}), bf16[32,32,128]{2,1,0:T(8,128)(2,1)S(1)}, u32[]{:S(2)}, u32[]{:S(2)}) async-start(bf16[32,32,128]{2,1,0:T(8,128)(2,1)} %bitcast.20), calls=%async_computation.7 | async-start | bytes 524288 | tf_op jit(solution)/shard_map/all_to_all | solution.py:357
  330.5 10.2 %copy-start.16 = (f32[15,32,128]{2,1,0:T(8,128)}, f32[15,32,128]{2,1,0:T(8,128)S(1)}, u32[]{:S(2)}) copy-start(f32[15,32,128]{2,1,0:T(8,128)S(1)} %constant_dynamic-update-slice_fusion.1) | copy-start | bytes 737284
  (2 other events, 1.3 us)
Sparse Core Ops, SparseCore 0:
  9.5 88.4 all-gather.6
  135.3 82.3 all-gather.8
  219.9 46.6 all-gather.10

commit v8 on v7

--- a/solution.py
+++ b/solution.py
@@ -44,28 +44,22 @@
 
 
 MIRRORED_UPPER = [(9, 12), (9, 14), (11, 13), (11, 14), (13, 14)]
-MIRRORED_LEAF = [(2, 9), (3, 9), (6, 11), (7, 11), (4, 13), (5, 13), (6, 13), (7, 13)]
 
 
 def mirrored_weights(meta, inverse, panels):
-    def kernel(meta_ref, d_ref, p_ref, upper_ref, leaf_ref):
+    def kernel(meta_ref, d_ref, p_ref, o_ref):
         for i in range(3):
-            upper_ref[i] = d_ref[9 + 2 * i]
+            o_ref[i] = d_ref[9 + 2 * i]
         for i, (source, target) in enumerate(MIRRORED_UPPER):
             block = selected(meta_ref, p_ref, source, target)
-            upper_ref[3 + i, :, :128] = block[:128]
-            upper_ref[3 + i, :, 128:] = block[128:]
-        for i, (source, target) in enumerate(MIRRORED_LEAF):
-            leaf_ref[i] = selected(meta_ref, p_ref, source, target)
+            o_ref[3 + i, :, :128] = block[:128]
+            o_ref[3 + i, :, 128:] = block[128:]
 
     return pl.pallas_call(
         kernel,
         in_specs=[SMEM, VMEM, VMEM],
-        out_specs=[VMEM, VMEM],
-        out_shape=[
-            jax.ShapeDtypeStruct((8, 128, 256), BF16),
-            jax.ShapeDtypeStruct((8, 256, 128), BF16),
-        ],
+        out_specs=VMEM,
+        out_shape=jax.ShapeDtypeStruct((8, 128, 256), BF16),
         compiler_params=params(0),
         name="mirrored_weights",
     )(meta, inverse, panels)
@@ -141,8 +135,8 @@
     )(spread, inverse)
 
 
-def update_from_leaves(meta, own, other, panels, leaf_got, right, right_got):
-    def kernel(meta_ref, a_ref, b_ref, p_ref, g_ref, r_ref, rg_ref, o_ref):
+def update_from_leaves(meta, own, other, panels, right):
+    def kernel(meta_ref, a_ref, b_ref, p_ref, r_ref, o_ref):
         core, row = meta_ref[1], meta_ref[2]
         for t in range(7):
             target = 8 + t
@@ -152,28 +146,25 @@
                 sources = range(4 * (t - 4), 4 * (t - 4) + 4)
             else:
                 sources = range(8)
-            if t in (1, 3, 5):
-                blocks = [g_ref[MIRRORED_LEAF.index((s, target))] for s in sources]
-            else:
-                blocks = [selected(meta_ref, p_ref, s, target) for s in sources]
+            blocks = []
+            for s in sources:
+                slot, found = slot_of(meta_ref, s, target)
+                block = p_ref[s, slot]
+                blocks.append(jnp.where(found, block, jnp.zeros_like(block)))
             for parity, x_ref in ((core, a_ref), (1 - core, b_ref)):
                 acc = jnp.zeros((256, 256), F32)
                 for s, block in zip(sources, blocks, strict=True):
                     acc = acc + dot_t(x_ref[:, s].reshape(256, 128), block)
                 for half in range(2):
-                    side = 1 - half if t in (1, 3, 5) else half
-                    value = acc[:, 128 * side : 128 * side + 128].astype(BF16)
+                    value = acc[:, 128 * half : 128 * half + 128].astype(BF16)
                     o_ref[:, pl.ds(parity, 1), half, t] = value.reshape(8, 1, 32, 128)
         z, parity = row // 4, (row // 2) % 2
         start = pl.multiple_of(16 * (row % 2), 16)
         for half in range(2):
             for t in range(7):
                 part = o_ref[z, parity, half, t, pl.ds(start, 16), :].astype(F32)
-                if t in (1, 3, 5):
-                    held = rg_ref[t // 2, :, 128 * (1 - half) : 128 * (1 - half) + 128]
-                else:
-                    held = r_ref[8 + t, :, 128 * half : 128 * half + 128]
-                o_ref[z, parity, half, t, pl.ds(start, 16), :] = (part - held).astype(BF16)
+                part = part - r_ref[8 + t, :, 128 * half : 128 * half + 128]
+                o_ref[z, parity, half, t, pl.ds(start, 16), :] = part.astype(BF16)
 
     return pl.pallas_call(
         kernel,
@@ -184,49 +175,53 @@
             VMEM,
             pl.BlockSpec((8, 3, 256, 128), lambda i: (0, 0, 0, 0)),
             VMEM,
-            VMEM,
-            VMEM,
         ],
         out_specs=VMEM,
         out_shape=jax.ShapeDtypeStruct((8, 2, 2, 7, 32, 128), BF16),
         compiler_params=params(),
         name="update_from_leaves",
-    )(meta, own, other, panels, leaf_got, right, right_got)
+    )(meta, own, other, panels, right)
 
 
 def first_residual(parts):
-    def kernel(p_ref, o_ref):
-        o_ref[...] = (-jnp.sum(p_ref[...].astype(F32), axis=0)).astype(BF16)
+    def kernel(p_ref, natural_ref, mirrored_ref):
+        residual = (-jnp.sum(p_ref[...].astype(F32), axis=0)).astype(BF16)
+        for i in range(4):
+            natural_ref[i] = residual[2 * i]
+        for i in range(3):
+            mirrored_ref[i] = residual[2 * i + 1]
 
     return pl.pallas_call(
         kernel,
         in_specs=[VMEM],
-        out_specs=VMEM,
-        out_shape=jax.ShapeDtypeStruct((7, 32, 128), BF16),
+        out_specs=[VMEM, VMEM],
+        out_shape=[
+            jax.ShapeDtypeStruct((4, 32, 128), BF16),
+            jax.ShapeDtypeStruct((3, 32, 128), BF16),
+        ],
         compiler_params=params(0),
         name="first_residual",
     )(parts)
 
 
-def first_payload(meta, residual):
-    def kernel(meta_ref, x_ref, o_ref):
+def first_payload(meta, natural, mirrored):
+    def kernel(meta_ref, n_ref, m_ref, o_ref):
         row = meta_ref[2]
         for r in range(NR):
             for p in range(2):
-                o_ref[r, p] = jnp.where(row <= r, x_ref[2 * p], x_ref[2 * p + 1])
-
-    return pl.pallas_call(
-        kernel,
-        in_specs=[SMEM, VMEM],
+                o_ref[r, p] = jnp.where(row <= r, n_ref[p], m_ref[p])
+
+    return pl.pallas_call(
+        kernel,
+        in_specs=[SMEM, VMEM, VMEM],
         out_specs=VMEM,
         out_shape=jax.ShapeDtypeStruct((NR, 2, 32, 128), BF16),
         compiler_params=params(0),
         name="first_payload",
-    )(meta, residual)
-
-
-def solve_level(meta, spread, local, places, weights, targets):
-    pairs = len(places)
+    )(meta, natural, mirrored)
+
+
+def solve_level(meta, spread, local, pairs, weights, targets):
     used = min(b for terms, _ in targets for _, b in terms)
 
     def kernel(meta_ref, x_ref, y_ref, w_hbm, natural_ref, mirrored_ref, o_ref, w_ref, sem):
@@ -241,7 +236,7 @@
             copy.start()
 
         def mirrored_block(b, p):
-            return jnp.where(row == b, y_ref[places[p]], x_ref[b, p])
+            return jnp.where(row == b, y_ref[p], x_ref[b, p])
 
         for c in range(NC):
             copies[c].wait()
@@ -297,33 +292,35 @@
     return acc
 
 
-def solve_root(residual, inverse):
+def solve_root(residual, weights):
     def kernel(x_ref, d_ref, s_ref):
-        s_ref[0] = solve_node(x_ref, d_ref, 0, 2)
-
-    return pl.pallas_call(
-        kernel,
-        in_specs=[VMEM, VMEM],
+        s_ref[0] = solve_node(x_ref, d_ref, 0, 0)
+
+    return pl.pallas_call(
+        kernel,
+        grid=(1,),
+        in_specs=[VMEM, pl.BlockSpec((NC, 1, 128, 256), lambda i: (0, 2, 0, 0))],
         out_specs=VMEM,
         out_shape=jax.ShapeDtypeStruct((1, 32, 128), F32),
-        compiler_params=params(0),
+        compiler_params=params(1, STREAM_LIMIT),
         name="solve_root",
-    )(residual, inverse)
-
-
-def next_residual(meta, parts, residual):
-    def kernel(meta_ref, p_ref, x_ref, o_ref, local_ref, rest_ref):
+    )(residual, weights)
+
+
+def next_residual(meta, parts, natural, mirrored):
+    def kernel(meta_ref, p_ref, n_ref, m_ref, o_ref, local_ref, rest_ref):
         row = meta_ref[2]
-        total = x_ref[4:].astype(F32) - jnp.sum(p_ref[...].astype(F32), axis=0)
-        natural, mirrored = total[0].astype(BF16), total[1].astype(BF16)
+        total = jnp.sum(p_ref[...].astype(F32), axis=0)
+        first = (n_ref[2].astype(F32) - total[0]).astype(BF16)
+        second = (m_ref[2].astype(F32) - total[1]).astype(BF16)
         for r in range(NR):
-            o_ref[r, 0] = jnp.where(row <= r, natural, mirrored)
-        local_ref[0] = mirrored
-        rest_ref[0] = total[2]
-
-    return pl.pallas_call(
-        kernel,
-        in_specs=[SMEM, VMEM, VMEM],
+            o_ref[r, 0] = jnp.where(row <= r, first, second)
+        local_ref[0] = second
+        rest_ref[0] = n_ref[3].astype(F32) - total[2]
+
+    return pl.pallas_call(
+        kernel,
+        in_specs=[SMEM, VMEM, VMEM, VMEM],
         out_specs=[VMEM, VMEM, VMEM],
         out_shape=[
             jax.ShapeDtypeStruct((NR, 1, 32, 128), BF16),
@@ -332,7 +329,7 @@
         ],
         compiler_params=params(0),
         name="next_residual",
-    )(meta, parts, residual)
+    )(meta, parts, natural, mirrored)
 
 
 def last_residual(parts, rest):
@@ -373,8 +370,10 @@
     return lax.ppermute(values, ALL, pairs)
 
 
-def to_mirrored_column(values):
-    pairs = [(r * NC + c, r * NC + 15 - c) for r in range(NR) for c in range(NC)]
+def to_mirrored_owner(values):
+    pairs = [
+        (r * NC + c, (31 - 2 * c - r % 2) * NC + r // 2) for r in range(NR) for c in range(NC)
+    ]
     return lax.ppermute(values, ALL, pairs)
 
 
@@ -392,34 +391,29 @@
     meta = jnp.concatenate(
         [jnp.stack([col, core, row, zero]).astype(jnp.int32), block_map.reshape(-1)]
     )
-    upper_sent, leaf_sent = mirrored_weights(meta, diag_inverse, panels)
-    leaf_got = to_mirrored_column(leaf_sent)
-    right_got = to_mirrored_column(right_sides[9:14:2])
-    stack_two, stack_one = stack_weights(
-        meta, diag_inverse, panels, to_mirrored_row(upper_sent)
-    )
+    sent = mirrored_weights(meta, diag_inverse, panels)
     spread = spread_over(moved, ROW, NR)
-    spread, stack_two, stack_one, leaf_got, right_got = lax.optimization_barrier(
-        (spread, stack_two, stack_one, leaf_got, right_got)
-    )
+    spread, sent = lax.optimization_barrier((spread, sent))
 
     leaves, copies = solve_leaves(spread, leaf_inverse)
+    copies, sent = lax.optimization_barrier((copies, sent))
     own = exchange(copies, "z")
+    stack_two, stack_one = stack_weights(meta, diag_inverse, panels, to_mirrored_row(sent))
+    stack_two, stack_one, own = lax.optimization_barrier((stack_two, stack_one, own))
     other = lax.ppermute(own, "core", [(0, 1), (1, 0)])
-    stack_two, stack_one, own = lax.optimization_barrier((stack_two, stack_one, own))
     weights_two = lax.all_gather(stack_two, COL, axis=0)
     weights_one = lax.all_gather(stack_one, COL, axis=0)
-    parts = update_from_leaves(meta, own, other, panels, leaf_got, right_sides, right_got)
-    parts = exchange(parts.reshape(NR, 7, 32, 128), ROW)
-    residual = to_owner(first_residual(parts))
-
-    spread = exchange(first_payload(meta, residual), ROW)
+    parts = update_from_leaves(meta, own, other, panels, right_sides)
+    natural, mirrored = first_residual(exchange(parts.reshape(NR, 7, 32, 128), ROW))
+    natural, mirrored = to_owner(natural), to_mirrored_owner(mirrored)
+
+    spread = exchange(first_payload(meta, natural, mirrored), ROW)
     targets = [([(0, 4)], False), ([(1, 6)], True), ([(0, 8), (1, 10)], False)]
-    two, two_mirrored, parts = solve_level(meta, spread, residual, [1, 3], weights_two, targets)
-    spread, local, rest = next_residual(meta, exchange(parts, ROW), residual)
+    two, two_mirrored, parts = solve_level(meta, spread, mirrored, 2, weights_two, targets)
+    spread, local, rest = next_residual(meta, exchange(parts, ROW), natural, mirrored)
     spread = exchange(spread, ROW)
     one, one_mirrored, parts = solve_level(
-        meta, spread, local, [0], weights_one, [([(0, 3)], False)]
+        meta, spread, local, 1, weights_one, [([(0, 3)], False)]
     )
     back = to_mirrored_row(jnp.concatenate([two_mirrored, one_mirrored], axis=0))
     spread = last_residual(exchange(parts, ROW), rest)

time: 352 us -> 348 us (0.989)
  blocking collectives: 150 us -> 123 us
  waiting for transfers between devices: 69.5 us -> 91.7 us
    all_to_all x4 -> x5, waiting for transfers between devices: 21.2 us -> 67.4 us  [exchange(): return lax.all_to_all(flat, axes, 0, 0, tiled=True).reshape(shape)]
    ppermute x2, waiting for transfers between devices: 45.7 us -> 18.8 us  [to_mirrored_row(): return lax.ppermute(values, ALL, pairs)]
    all_to_all x4 -> x3, blocking collectives: 150 us -> 123 us  [exchange(): return lax.all_to_all(flat, axes, 0, 0, tiled=True).reshape(shape)]
    all_to_all x4 -> x5, starting transfers between devices: 44.2 us -> 52.6 us  [exchange(): return lax.all_to_all(flat, axes, 0, 0, tiled=True).reshape(shape)]
    ppermute x2 -> x1, starting transfers between devices: 8.4 us -> 6.4 us  [to_mirrored_owner(): return lax.ppermute(values, ALL, pairs)]
    unnamed x48 -> x44, local copies, waits for them, and re-layouts: 8.57 us -> 7.2 us
  transfers between devices with their start and end apart: 14 -> 14, of which waited for: 5 -> 7; matrix products, arithmetic and copies ran while one was open for 1% -> 1% of each run, Pallas kernels for 4% -> 4%
where the time goes in v8:
time: 348 us; the launch traced here: 347 us
  blocking collectives  123 us (35%)
  waiting for transfers between devices  91.7 us (26%)
  starting transfers between devices  74.6 us (21%)
  Pallas kernels  29.1 us (8%)
  local copies, waits for them, and re-layouts  14.2 us (4%)
  between operations  13.4 us (4%)
    all_to_all x3, blocking collectives, exchange(): return lax.all_to_all(flat, axes, 0, 0, tiled=True).reshape(shape)  123 us
    all_to_all x5, waiting for transfers between devices, exchange(): return lax.all_to_all(flat, axes, 0, 0, tiled=True).reshape(shape)  67.4 us
    all_to_all x5, starting transfers between devices, exchange(): return lax.all_to_all(flat, axes, 0, 0, tiled=True).reshape(shape)  52.6 us
    ppermute x2, waiting for transfers between devices, to_mirrored_row(): return lax.ppermute(values, ALL, pairs)  18.8 us
    pallas_call x2, Pallas kernels, solve_level(): pl.pallas_call(kernel, in_specs=[SMEM, VMEM, VMEM, HBM], out_specs=[VMEM,...  15.7 us
    ppermute x2, starting transfers between devices, to_mirrored_row(): return lax.ppermute(values, ALL, pairs)  12.3 us
    unnamed x44, local copies, waits for them, and re-layouts  7.2 us
  transfers between devices with their start and end apart: 14, of which 7 were waited for; matrix products, arithmetic and copies ran while one was open for 1% of the time, Pallas kernels for 4%

profile of v8, /device:TPU:8, one launch (start us, length us, event | category | flops | bytes accessed | tf_op | source)
XLA Modules:
  0.0 346.7 jit_solution(8663925159535545240)
XLA Ops:
  6.5 0.9 slice.39
  7.5 1.9 slice.23
  10.1 1.7 broadcast_in_dim.9
  11.7 26.2 %all-to-all-start = ((bf16[32,128,256]{2,1,0:T(8,128)(2,1)}), bf16[32,128,256]{2,1,0:T(8,128)(2,1)}, u32[]{:S(2)}, u32[]{:S(2)}) async-start(bf16[32,128,256]{2,1,0:T(8,128)(2,1)} %broadcast_in_dim.9), calls=%async_computation | async-start | bytes 4194304 | tf_op jit(solution)/shard_map/all_to_all | solution.py:354
  38.4 1.2 copy-done.1
  40.3 0.8 copy-done.4
  41.1 46.1 %all-to-all-done = bf16[32,128,256]{2,1,0:T(8,128)(2,1)} async-done(((bf16[32,128,256]{2,1,0:T(8,128)(2,1)}), bf16[32,128,256]{2,1,0:T(8,128)(2,1)}, u32[]{:S(2)}, u32[]{:S(2)}) %all-to-all-start) | async-done | bytes 2097184 | tf_op jit(solution)/shard_map/all_to_all | solution.py:354
  87.2 6.5 %solve_leaves.1 = (f32[8,32,128]{2,1,0:T(8,128)}, bf16[8,8,32,128]{3,2,1,0:T(8,128)(2,1)}) custom-call(bf16[32,8,16,256]{3,2,1,0:T(8,128)(2,1)} %bitcast.1.b_ref, bf16[16,8,128,256]{3,2,1,0:T(8,128)(2,1)} %bitcast.32), custom_call_target="tpu_custom_call" | custom-call | tf_op jit(solution)/shard_map/solve_leaves/pallas_call | solution.py:121
  93.8 8.5 %all-to-all-start.1 = ((bf16[8,256,128]{2,1,0:T(8,128)(2,1)}), bf16[8,256,128]{2,1,0:T(8,128)(2,1)S(1)}, u32[]{:S(2)}, u32[]{:S(2)}) async-start(bf16[8,256,128]{2,1,0:T(8,128)(2,1)} %bitcast.37), calls=%async_computation.1 | async-start | bytes 1048576 | tf_op jit(solution)/shard_map/all_to_all | solution.py:354
  102.3 4.6 %collective-permute-start.1 = (bf16[8,128,256]{2,1,0:T(8,128)(2,1)}, bf16[8,128,256]{2,1,0:T(8,128)(2,1)S(1)}, u32[]{:S(2)}, u32[]{:S(2)}) collective-permute-start(bf16[8,128,256]{2,1,0:T(8,128)(2,1)} %copy-done.4), channel_id=1, source_target_pairs={{0,496},{1,497},{2,498},{3,499},{4,500},{5,501},{6,502},{7,503},{8... | collective-permute-start | bytes 1572872 | tf_op jit(solution)/shard_map/ppermute | solution.py:370
  106.9 15.4 %collective-permute-done.1.g_ref = bf16[8,128,256]{2,1,0:T(8,128)(2,1)S(1)} collective-permute-done((bf16[8,128,256]{2,1,0:T(8,128)(2,1)}, bf16[8,128,256]{2,1,0:T(8,128)(2,1)S(1)}, u32[]{:S(2)}, u32[]{:S(2)}) %collective-permute-start.1) | collective-permute-done | bytes 524320 | tf_op jit(solution)/shard_map/ppermute | solution.py:370
  122.3 1.2 copy-done.2
  124.2 0.9 copy-done.3
  126.6 1.9 collective-permute-start.2
  128.5 1.9 collective-permute-done.2.b_ref
  130.4 2.4 update_from_leaves.1
  132.8 61.8 %all_to_all.40 = bf16[32,224,128]{2,1,0:T(8,128)(2,1)S(1)} all-to-all(bf16[32,224,128]{2,1,0:T(8,128)(2,1)S(1)} %bitcast.23), channel_id=1, replica_groups=mesh['x'=4,'y'=8,'z'=8,'core'=2] {'x','y'}, dimensions={0} | all-to-all | bytes 3670016 | tf_op jit(solution)/shard_map/all_to_all | solution.py:354
  195.5 6.4 %collective-permute-start.4 = (bf16[3,32,128]{2,1,0:T(8,128)(2,1)S(1)}, bf16[3,32,128]{2,1,0:T(8,128)(2,1)S(1)}, u32[]{:S(2)}, u32[]{:S(2)}) collective-permute-start(bf16[3,32,128]{2,1,0:T(8,128)(2,1)S(1)} %get-tuple-element.41), channel_id=1, source_target_pairs={{0,496},{1,464},{2,432},{3,400},{4,368},{5,336},{6,304},{7,272},{8... | collective-permute-start | bytes 73736 | tf_op jit(solution)/shard_map/ppermute | solution.py:377
  201.9 2.9 collective-permute-done.4.m_ref.y_ref
  205.5 35.0 %all_to_all.41 = bf16[32,64,128]{2,1,0:T(8,128)(2,1)} all-to-all(bf16[32,64,128]{2,1,0:T(8,128)(2,1)S(1)} %bitcast.27), channel_id=1, replica_groups=mesh['x'=4,'y'=8,'z'=8,'core'=2] {'x','y'}, dimensions={0} | all-to-all | bytes 1048576 | tf_op jit(solution)/shard_map/all_to_all | solution.py:354
  240.5 9.3 %solve_level.2 = (f32[2,32,128]{2,1,0:T(8,128)}, f32[2,32,128]{2,1,0:T(8,128)}, bf16[32,3,32,128]{3,2,1,0:T(8,128)(2,1)}) custom-call(s32[676]{0:T(1024)} %copy-done.7, bf16[32,2,32,128]{3,2,1,0:T(8,128)(2,1)} %bitcast.33, bf16[3,32,128]{2,1,0:T(8,128)(2,1)} %copy-done.9, bf16[16,12,128,256]{3,2,1,0:T(8,128)(2,1)} %bitcast.31), custom_call_target="tpu_custom_call" | custom-call | tf_op jit(solution)/shard_map/solve_level/pallas_call | solution.py:269
  249.9 26.2 %all_to_all.42 = bf16[32,96,128]{2,1,0:T(8,128)(2,1)S(1)} all-to-all(bf16[32,96,128]{2,1,0:T(8,128)(2,1)} %bitcast.36), channel_id=1, replica_groups=mesh['x'=4,'y'=8,'z'=8,'core'=2] {'x','y'}, dimensions={0} | all-to-all | bytes 1572864 | tf_op jit(solution)/shard_map/all_to_all | solution.py:354
  276.8 1.4 next_residual.1
  278.2 4.9 %all-to-all-start.5 = ((bf16[32,32,128]{2,1,0:T(8,128)(2,1)}), bf16[32,32,128]{2,1,0:T(8,128)(2,1)S(1)}, u32[]{:S(2)}, u32[]{:S(2)}) async-start(bf16[32,32,128]{2,1,0:T(8,128)(2,1)} %bitcast.15), calls=%async_computation.5 | async-start | bytes 524288 | tf_op jit(solution)/shard_map/all_to_all | solution.py:354
  283.2 11.0 %all-to-all-done.5 = bf16[32,32,128]{2,1,0:T(8,128)(2,1)S(1)} async-done(((bf16[32,32,128]{2,1,0:T(8,128)(2,1)}), bf16[32,32,128]{2,1,0:T(8,128)(2,1)S(1)}, u32[]{:S(2)}, u32[]{:S(2)}) %all-to-all-start.5) | async-done | bytes 262176 | tf_op jit(solution)/shard_map/all_to_all | solution.py:354
  294.9 6.3 %solve_level.3 = (f32[1,32,128]{2,1,0:T(8,128)}, f32[1,32,128]{2,1,0:T(8,128)}, bf16[32,1,32,128]{3,2,1,0:T(8,128)(2,1)}) custom-call(s32[676]{0:T(1024)} %copy-done.7, bf16[32,1,32,128]{3,2,1,0:T(8,128)(2,1)} %bitcast.34, bf16[1,32,128]{2,1,0:T(8,128)(2,1)} %copy-done.11, bf16[16,5,128,256]{3,2,1,0:T(8,128)(2,1)} %bitcast.29), custom_call_target="tpu_custom_call" | custom-call | tf_op jit(solution)/shard_map/solve_level/pallas_call | solution.py:269
  301.2 4.4 %all-to-all-start.6 = ((bf16[32,32,128]{2,1,0:T(8,128)(2,1)}), bf16[32,32,128]{2,1,0:T(8,128)(2,1)S(1)}, u32[]{:S(2)}, u32[]{:S(2)}) async-start(bf16[32,32,128]{2,1,0:T(8,128)(2,1)} %bitcast.38), calls=%async_computation.6 | async-start | bytes 524288 | tf_op jit(solution)/shard_map/all_to_all | solution.py:354
  306.4 7.7 %collective-permute-start.5 = (f32[3,32,128]{2,1,0:T(8,128)S(1)}, f32[3,32,128]{2,1,0:T(8,128)S(1)}, u32[]{:S(2)}, u32[]{:S(2)}) collective-permute-start(f32[3,32,128]{2,1,0:T(8,128)S(1)} %pad_maximum_fusion), channel_id=1, source_target_pairs={{0,496},{1,497},{2,498},{3,499},{4,500},{5,501},{6,502},{7,503},{8... | collective-permute-start | bytes 147464 | tf_op jit(solution)/shard_map/ppermute | solution.py:370
  314.1 3.4 collective-permute-done.5
  318.3 8.7 %all-to-all-start.7 = ((bf16[32,32,128]{2,1,0:T(8,128)(2,1)}), bf16[32,32,128]{2,1,0:T(8,128)(2,1)S(1)}, u32[]{:S(2)}, u32[]{:S(2)}) async-start(bf16[32,32,128]{2,1,0:T(8,128)(2,1)} %bitcast.20), calls=%async_computation.7 | async-start | bytes 524288 | tf_op jit(solution)/shard_map/all_to_all | solution.py:354
  327.7 10.2 %all-to-all-done.7 = bf16[32,32,128]{2,1,0:T(8,128)(2,1)S(1)} async-done(((bf16[32,32,128]{2,1,0:T(8,128)(2,1)}), bf16[32,32,128]{2,1,0:T(8,128)(2,1)S(1)}, u32[]{:S(2)}, u32[]{:S(2)}) %all-to-all-start.7) | async-done | bytes 262176 | tf_op jit(solution)/shard_map/all_to_all | solution.py:354
  337.9 2.3 solve_root.1
  (63 shorter events, 9.4 us)
Async XLA Ops:
  6.5 80.7 %all-gather.7.cloned.1.call-start = ((), (), s32[]{:S(2)}) async-start(), calls=%async_computation.8 | async-start | bytes 8912896 | tf_op jit(solution)/shard_map/all_gather | solution.py:388
  9.4 0.7 collective-permute-start
  10.1 27.9 %copy-start.17 = (s32[14,16,3]{1,0,2:T(8,128)S(1)}, s32[14,16,3]{1,0,2:T(8,128)}, u32[]{:S(2)}) copy-start(s32[14,16,3]{1,0,2:T(8,128)} %param.7) | copy-start | bytes 8068
  11.7 26.7 %copy-start = (bf16[14,3,256,128]{3,2,1,0:T(8,128)(2,1)S(1)}, bf16[14,3,256,128]{3,2,1,0:T(8,128)(2,1)}, u32[]{:S(2)}) copy-start(bf16[14,3,256,128]{3,2,1,0:T(8,128)(2,1)} %p_ref.5) | copy-start | bytes 8257540
  11.7 75.5 %all-to-all-start = ((bf16[32,128,256]{2,1,0:T(8,128)(2,1)}), bf16[32,128,256]{2,1,0:T(8,128)(2,1)}, u32[]{:S(2)}, u32[]{:S(2)}) async-start(bf16[32,128,256]{2,1,0:T(8,128)(2,1)} %broadcast_in_dim.9), calls=%async_computation | async-start | bytes 4194304 | tf_op jit(solution)/shard_map/all_to_all | solution.py:354
  38.4 1.2 copy-start.1
  39.6 165.3 %copy-start.7 = (s32[676]{0:T(1024)}, s32[676]{0:T(1024)S(1)}, u32[]{:S(2)}) copy-start(s32[676]{0:T(1024)S(1)} %concatenate.9.meta_ref) | copy-start | bytes 8116
  40.3 0.8 copy-start.4
  93.7 36.7 %copy-start.5 = (f32[15,16,256]{2,1,0:T(8,128)S(1)}, f32[15,16,256]{2,1,0:T(8,128)}, u32[]{:S(2)}) copy-start(f32[15,16,256]{2,1,0:T(8,128)} %r_ref.1) | copy-start | bytes 737284
  93.8 32.1 %all-to-all-start.1 = ((bf16[8,256,128]{2,1,0:T(8,128)(2,1)}), bf16[8,256,128]{2,1,0:T(8,128)(2,1)S(1)}, u32[]{:S(2)}, u32[]{:S(2)}) async-start(bf16[8,256,128]{2,1,0:T(8,128)(2,1)} %bitcast.37), calls=%async_computation.1 | async-start | bytes 1048576 | tf_op jit(solution)/shard_map/all_to_all | solution.py:354
  102.2 138.3 %all-gather.9.cloned.1.call-start = ((), (), s32[]{:S(2)}) async-start(), calls=%async_computation.9 | async-start | bytes 13369344 | tf_op jit(solution)/shard_map/all_gather | solution.py:404
  102.3 20.0 %collective-permute-start.1 = (bf16[8,128,256]{2,1,0:T(8,128)(2,1)}, bf16[8,128,256]{2,1,0:T(8,128)(2,1)S(1)}, u32[]{:S(2)}, u32[]{:S(2)}) collective-permute-start(bf16[8,128,256]{2,1,0:T(8,128)(2,1)} %copy-done.4), channel_id=1, source_target_pairs={{0,496},{1,497},{2,498},{3,499},{4,500},{5,501},{6,502},{7,503},{8... | collective-permute-start | bytes 1572872 | tf_op jit(solution)/shard_map/ppermute | solution.py:370
  122.3 1.2 copy-start.2
  124.2 0.9 copy-start.3
  125.1 0.7 copy-start.6
  125.9 157.3 %all-gather.11.cloned.1.call-start = ((), (), s32[]{:S(2)}) async-start(), calls=%async_computation.10 | async-start | bytes 5570560 | tf_op jit(solution)/shard_map/all_gather | solution.py:405
  126.6 3.8 %collective-permute-start.2 = (bf16[8,8,32,128]{3,2,1,0:T(8,128)(2,1)S(1)}, bf16[8,8,32,128]{3,2,1,0:T(8,128)(2,1)S(1)}, u32[]{:S(2)}, u32[]{:S(2)}) collective-permute-start(bf16[8,8,32,128]{3,2,1,0:T(8,128)(2,1)S(1)} %bitcast.25), channel_id=1, source_target_pairs={{0,1},{1,0},{2,3},{3,2},{4,5},{5,4},{6,7},{7,6},{8,9},{9,8},{10,11... | collective-permute-start | bytes 1572872 | tf_op jit(solution)/shard_map/ppermute | solution.py:403
  194.9 10.0 %collective-permute-start.3 = (bf16[4,32,128]{2,1,0:T(8,128)(2,1)S(1)}, bf16[4,32,128]{2,1,0:T(8,128)(2,1)S(1)}, u32[]{:S(2)}, u32[]{:S(2)}) collective-permute-start(bf16[4,32,128]{2,1,0:T(8,128)(2,1)S(1)} %get-tuple-element.40), channel_id=1, source_target_pairs={{0,0},{1,32},{2,64},{3,96},{4,128},{5,160},{6,192},{7,224},{8,256}... | collective-permute-start | bytes 98312 | tf_op jit(solution)/shard_map/ppermute | solution.py:365
  195.5 9.3 %collective-permute-start.4 = (bf16[3,32,128]{2,1,0:T(8,128)(2,1)S(1)}, bf16[3,32,128]{2,1,0:T(8,128)(2,1)S(1)}, u32[]{:S(2)}, u32[]{:S(2)}) collective-permute-start(bf16[3,32,128]{2,1,0:T(8,128)(2,1)S(1)} %get-tuple-element.41), channel_id=1, source_target_pairs={{0,496},{1,464},{2,432},{3,400},{4,368},{5,336},{6,304},{7,272},{8... | collective-permute-start | bytes 73736 | tf_op jit(solution)/shard_map/ppermute | solution.py:377
  204.8 35.7 %copy-start.9 = (bf16[3,32,128]{2,1,0:T(8,128)(2,1)}, bf16[3,32,128]{2,1,0:T(8,128)(2,1)S(1)}, u32[]{:S(2)}) copy-start(bf16[3,32,128]{2,1,0:T(8,128)(2,1)S(1)} %collective-permute-done.4.m_ref.y_ref) | copy-start | bytes 73732
  240.5 35.5 %copy-start.8 = (s32[676]{0:T(1024)S(1)}, s32[676]{0:T(1024)}, u32[]{:S(2)}) copy-start(s32[676]{0:T(1024)} %copy-done.7) | copy-start | bytes 8116
  249.8 33.3 %copy-start.13 = (f32[8,32,128]{2,1,0:T(8,128)S(1)}, f32[8,32,128]{2,1,0:T(8,128)}, u32[]{:S(2)}) copy-start(f32[8,32,128]{2,1,0:T(8,128)} %get-tuple-element.32) | copy-start | bytes 393220
  276.0 0.7 copy-start.10
  278.2 16.0 %copy-start.11 = (bf16[1,32,128]{2,1,0:T(8,128)(2,1)}, bf16[1,32,128]{2,1,0:T(8,128)(2,1)S(1)}, u32[]{:S(2)}) copy-start(bf16[1,32,128]{2,1,0:T(8,128)(2,1)S(1)} %get-tuple-element.47.y_ref) | copy-start | bytes 24580
  278.2 16.0 %all-to-all-start.5 = ((bf16[32,32,128]{2,1,0:T(8,128)(2,1)}), bf16[32,32,128]{2,1,0:T(8,128)(2,1)S(1)}, u32[]{:S(2)}, u32[]{:S(2)}) async-start(bf16[32,32,128]{2,1,0:T(8,128)(2,1)} %bitcast.15), calls=%async_computation.5 | async-start | bytes 524288 | tf_op jit(solution)/shard_map/all_to_all | solution.py:354
  294.2 0.7 copy-start.12
  294.9 10.8 %copy-start.15 = (f32[2,32,128]{2,1,0:T(8,128)S(1)}, f32[2,32,128]{2,1,0:T(8,128)}, u32[]{:S(2)}) copy-start(f32[2,32,128]{2,1,0:T(8,128)} %get-tuple-element.44) | copy-start | bytes 98308
  294.9 19.2 %copy-start.16 = (f32[2,32,128]{2,1,0:T(8,128)S(1)}, f32[2,32,128]{2,1,0:T(8,128)}, u32[]{:S(2)}) copy-start(f32[2,32,128]{2,1,0:T(8,128)} %get-tuple-element.43) | copy-start | bytes 98308
  301.2 16.3 %all-to-all-start.6 = ((bf16[32,32,128]{2,1,0:T(8,128)(2,1)}), bf16[32,32,128]{2,1,0:T(8,128)(2,1)S(1)}, u32[]{:S(2)}, u32[]{:S(2)}) async-start(bf16[32,32,128]{2,1,0:T(8,128)(2,1)} %bitcast.38), calls=%async_computation.6 | async-start | bytes 524288 | tf_op jit(solution)/shard_map/all_to_all | solution.py:354
  306.4 11.1 %collective-permute-start.5 = (f32[3,32,128]{2,1,0:T(8,128)S(1)}, f32[3,32,128]{2,1,0:T(8,128)S(1)}, u32[]{:S(2)}, u32[]{:S(2)}) collective-permute-start(f32[3,32,128]{2,1,0:T(8,128)S(1)} %pad_maximum_fusion), channel_id=1, source_target_pairs={{0,496},{1,497},{2,498},{3,499},{4,500},{5,501},{6,502},{7,503},{8... | collective-permute-start | bytes 147464 | tf_op jit(solution)/shard_map/ppermute | solution.py:370
  318.3 19.6 %all-to-all-start.7 = ((bf16[32,32,128]{2,1,0:T(8,128)(2,1)}), bf16[32,32,128]{2,1,0:T(8,128)(2,1)S(1)}, u32[]{:S(2)}, u32[]{:S(2)}) async-start(bf16[32,32,128]{2,1,0:T(8,128)(2,1)} %bitcast.20), calls=%async_computation.7 | async-start | bytes 524288 | tf_op jit(solution)/shard_map/all_to_all | solution.py:354
  327.7 10.2 %copy-start.14 = (f32[15,32,128]{2,1,0:T(8,128)}, f32[15,32,128]{2,1,0:T(8,128)S(1)}, u32[]{:S(2)}) copy-start(f32[15,32,128]{2,1,0:T(8,128)S(1)} %constant_dynamic-update-slice_fusion.1) | copy-start | bytes 737284
Sparse Core Ops, SparseCore 0:
  9.5 63.9 all-gather.6
  126.0 89.9 all-gather.8
  218.1 44.3 all-gather.10

commit v9 on v6

--- a/solution.py
+++ b/solution.py
@@ -37,50 +37,39 @@
     return slot, meta[base + slot] == target
 
 
-def gathered_block(b):
-    is_low = b < 8
-    source = jnp.where(is_low, 8 + b // 2, 4 + b)
-    target = jnp.where(is_low & (b % 2 == 0), 12 + b // 4, 14)
-    return source, target
-
-
-def stack_upper(meta, inverse, panels, first_node, nodes, first_block, blocks):
-    def kernel(meta_ref, d_ref, p_ref, o_ref):
-        i = pl.program_id(0)
-
-        @pl.when(i < nodes)
-        def _():
-            o_ref[...] = d_ref[...]
-
-        @pl.when(i >= nodes)
-        def _():
-            _, found = slot_of(meta_ref, *gathered_block(first_block + i - nodes))
-            block = p_ref[0, 0]
-            block = jnp.where(found, block, jnp.zeros_like(block))
-            o_ref[0, :, :128] = block[:128]
-            o_ref[0, :, 128:] = block[128:]
-
-    def index(i, meta_ref):
-        source, target = gathered_block(first_block + jnp.maximum(i - nodes, 0))
-        slot, _ = slot_of(meta_ref, source, target)
-        return source, slot, 0, 0
-
-    return pl.pallas_call(
-        kernel,
-        grid_spec=pltpu.PrefetchScalarGridSpec(
-            num_scalar_prefetch=1,
-            grid=(nodes + blocks,),
-            in_specs=[
-                pl.BlockSpec(
-                    (1, 128, 256), lambda i, m: (first_node + jnp.minimum(i, nodes - 1), 0, 0)
-                ),
-                pl.BlockSpec((1, 1, 256, 128), index),
-            ],
-            out_specs=pl.BlockSpec((1, 128, 256), lambda i, m: (i, 0, 0)),
-        ),
-        out_shape=jax.ShapeDtypeStruct((nodes + blocks, 128, 256), BF16),
-        compiler_params=params(),
-        name="stack_upper",
+def selected(meta_ref, p_ref, source, target):
+    slot, found = slot_of(meta_ref, source, target)
+    block = p_ref[source, slot]
+    return jnp.where(found, block, jnp.zeros_like(block))
+
+
+def stack_weights(meta, inverse, panels):
+    def kernel(meta_ref, d_ref, p_ref, two_ref, one_ref):
+        def join(out_ref, place, source, target):
+            for side in range(2):
+                columns = slice(128 * side, 128 * side + 128)
+                block = selected(meta_ref, p_ref, source + side, target)
+                for half in range(2):
+                    out_ref[place + half, :, columns] = block[128 * half : 128 * half + 128]
+
+        two_ref[:4] = d_ref[8:12]
+        one_ref[:3] = d_ref[12:]
+        join(two_ref, 4, 8, 12)
+        join(two_ref, 6, 10, 13)
+        join(two_ref, 8, 8, 14)
+        join(two_ref, 10, 10, 14)
+        join(one_ref, 3, 12, 14)
+
+    return pl.pallas_call(
+        kernel,
+        in_specs=[SMEM, VMEM, VMEM],
+        out_specs=[VMEM, VMEM],
+        out_shape=[
+            jax.ShapeDtypeStruct((12, 128, 256), BF16),
+            jax.ShapeDtypeStruct((5, 128, 256), BF16),
+        ],
+        compiler_params=params(0),
+        name="stack_weights",
     )(meta, inverse, panels)
 
 
@@ -130,11 +119,7 @@
                 sources = range(4 * (t - 4), 4 * (t - 4) + 4)
             else:
                 sources = range(8)
-            blocks = []
-            for s in sources:
-                slot, found = slot_of(meta_ref, s, target)
-                block = p_ref[s, slot]
-                blocks.append(jnp.where(found, block, jnp.zeros_like(block)))
+            blocks = [selected(meta_ref, p_ref, s, target) for s in sources]
             for parity, x_ref in ((core, a_ref), (1 - core, b_ref)):
                 acc = jnp.zeros((256, 256), F32)
                 for s, block in zip(sources, blocks, strict=True):
@@ -189,59 +174,91 @@
     return acc
 
 
-def update_above(solved, w_ref, c, nodes, targets, o_ref):
-    for t, terms in enumerate(targets):
-        for half in range(2):
-            acc = jnp.zeros((32, 128), F32)
-            for s, b in terms:
-                block = w_ref[c, nodes + b, :, 128 * half : 128 * half + 128]
-                acc = acc + dot_t(solved[s], block)
-            o_ref[2 * c + half, t] = acc.astype(BF16)
-
-
-def solve_level(residual, weights, nodes, targets):
-    used = nodes + min(b for terms in targets for _, b in terms)
-
-    def kernel(x_ref, w_hbm, s_ref, o_ref, w_ref, sem):
-        pieces = [(c, slice(0, nodes)) for c in range(NC)]
-        pieces += [(c, slice(used, None)) for c in range(NC)]
-        copies = [
-            pltpu.make_async_copy(w_hbm.at[piece], w_ref.at[piece], sem.at[i])
-            for i, piece in enumerate(pieces)
-        ]
-        for copy in copies:
-            copy.start()
-        for c in range(NC):
-            copies[c].wait()
-            for n in range(nodes):
-                left = jnp.concatenate([x_ref[2 * c, n], x_ref[2 * c + 1, n]], axis=1)
-                value = dot_t(left, w_ref[c, n])
-                if c:
-                    value = value + s_ref[n]
-                s_ref[n] = value
-        solved = [s_ref[n].astype(BF16) for n in range(nodes)]
-        for c in range(NC):
-            copies[NC + c].wait()
-            update_above(solved, w_ref, c, nodes, targets, o_ref)
+def solve_pairs(x_ref, w_hbm, s_ref, w_ref, sem, nodes, first, update):
+    pieces = [(c, slice(0, nodes)) for c in range(NC)]
+    pieces += [(c, slice(first, None)) for c in range(NC)]
+    copies = [
+        pltpu.make_async_copy(w_hbm.at[piece], w_ref.at[piece], sem.at[i])
+        for i, piece in enumerate(pieces)
+    ]
+    for copy in copies:
+        copy.start()
+    for c in range(NC):
+        copies[c].wait()
+        for n in range(nodes):
+            left = jnp.concatenate([x_ref[2 * c, n], x_ref[2 * c + 1, n]], axis=1)
+            value = dot_t(left, w_ref[c, n])
+            if c:
+                value = value + s_ref[n]
+            s_ref[n] = value
+    joined = [
+        jnp.concatenate([s_ref[n].astype(BF16), s_ref[n + 1].astype(BF16)], axis=1)
+        for n in range(0, nodes, 2)
+    ]
+    for c in range(NC):
+        copies[NC + c].wait()
+        update(c, joined)
+
+
+def solve_two(residual, weights):
+    def kernel(x_ref, w_hbm, s_ref, o_ref, keep_ref, w_ref, sem):
+        def update(c, joined):
+            for half in range(2):
+                r = 2 * c + half
+                o_ref[r, 0] = dot_t(joined[0], w_ref[c, 4 + half]).astype(BF16)
+                o_ref[r, 1] = dot_t(joined[1], w_ref[c, 6 + half]).astype(BF16)
+                keep_ref[r] = dot_t(joined[0], w_ref[c, 8 + half]) + dot_t(
+                    joined[1], w_ref[c, 10 + half]
+                )
+
+        solve_pairs(x_ref, w_hbm, s_ref, w_ref, sem, 4, 4, update)
 
     return pl.pallas_call(
         kernel,
         in_specs=[VMEM, HBM],
-        out_specs=[VMEM, VMEM],
+        out_specs=[VMEM, VMEM, VMEM],
         out_shape=[
-            jax.ShapeDtypeStruct((nodes, 32, 128), F32),
-            jax.ShapeDtypeStruct((NR, len(targets), 32, 128), BF16),
+            jax.ShapeDtypeStruct((4, 32, 128), F32),
+            jax.ShapeDtypeStruct((NR, 2, 32, 128), BF16),
+            jax.ShapeDtypeStruct((NR, 32, 128), F32),
         ],
         scratch_shapes=[
             pltpu.VMEM(weights.shape, BF16),
             pltpu.SemaphoreType.DMA((2 * NC,)),
         ],
         compiler_params=params(0, STREAM_LIMIT),
-        name="solve_level",
+        name="solve_two",
     )(residual, weights)
 
 
-def solve_root(residual, inverse):
+def solve_one(residual, weights, keep):
+    def kernel(x_ref, w_hbm, keep_ref, s_ref, o_ref, w_ref, sem):
+        def update(c, joined):
+            for half in range(2):
+                r = 2 * c + half
+                part = keep_ref[r] + dot_t(joined[0], w_ref[c, 3 + half])
+                o_ref[r, 0] = part.astype(BF16)
+
+        solve_pairs(x_ref, w_hbm, s_ref, w_ref, sem, 2, 3, update)
+
+    return pl.pallas_call(
+        kernel,
+        in_specs=[VMEM, HBM, VMEM],
+        out_specs=[VMEM, VMEM],
+        out_shape=[
+            jax.ShapeDtypeStruct((2, 32, 128), F32),
+            jax.ShapeDtypeStruct((NR, 1, 32, 128), BF16),
+        ],
+        scratch_shapes=[
+            pltpu.VMEM(weights.shape, BF16),
+            pltpu.SemaphoreType.DMA((2 * NC,)),
+        ],
+        compiler_params=params(0, STREAM_LIMIT),
+        name="solve_one",
+    )(residual, weights, keep)
+
+
+def solve_root(residual, weights):
     def kernel(x_ref, d_ref, s_ref):
         s_ref[0] = solve_node(x_ref, d_ref, 0, 2)
 
@@ -252,29 +269,23 @@
         out_shape=jax.ShapeDtypeStruct((1, 32, 128), F32),
         compiler_params=params(0),
         name="solve_root",
-    )(residual, inverse)
-
-
-def next_residual(parts, rest, nodes):
-    count = rest.shape[0]
-    after = count - nodes
-
-    def kernel(p_ref, rest_ref, o_ref, *later):
+    )(residual, weights)
+
+
+def next_residual(parts, rest):
+    nodes = rest.shape[0]
+
+    def kernel(p_ref, rest_ref, o_ref):
         residual = rest_ref[...].astype(F32) - jnp.sum(p_ref[...].astype(F32), axis=0)
-        half = residual[:nodes].astype(BF16)
+        half = residual.astype(BF16)
         for r in range(NR):
             o_ref[r] = half
-        if after:
-            later[0][...] = residual[nodes:]
-
-    out_shape = [jax.ShapeDtypeStruct((NR, nodes, 32, 128), BF16)]
-    if after:
-        out_shape.append(jax.ShapeDtypeStruct((after, 32, 128), F32))
+
     return pl.pallas_call(
         kernel,
         in_specs=[VMEM, VMEM],
-        out_specs=[VMEM] * len(out_shape),
-        out_shape=out_shape,
+        out_specs=VMEM,
+        out_shape=jax.ShapeDtypeStruct((NR, nodes, 32, 128), BF16),
         compiler_params=params(0),
         name="next_residual",
     )(parts, rest)
@@ -311,8 +322,7 @@
     meta = jnp.concatenate(
         [jnp.stack([col, core, row, zero]).astype(jnp.int32), block_map.reshape(-1)]
     )
-    stack_two = stack_upper(meta, diag_inverse, panels, 8, 4, 0, 8)
-    stack_one = stack_upper(meta, diag_inverse, panels, 12, 3, 8, 2)
+    stack_two, stack_one = stack_weights(meta, diag_inverse, panels)
     spread = spread_over(moved, ROW, NR)
     spread, stack_two, stack_one = lax.optimization_barrier((spread, stack_two, stack_one))
 
@@ -326,14 +336,12 @@
     parts = exchange(parts.reshape(NR, 7, 32, 128), ROW)
     residual = to_owner(first_residual(parts))
 
-    targets = [[(0, 0), (1, 2)], [(2, 4), (3, 6)], [(0, 1), (1, 3), (2, 5), (3, 7)]]
     spread = spread_over(residual[:4], ROW, NR)
-    two, parts = solve_level(spread, weights_two, 4, targets)
-    spread, rest = next_residual(exchange(parts, ROW), residual[4:], 2)
-    targets = [[(0, 1), (1, 2)]]
-    one, parts = solve_level(exchange(spread, ROW), weights_one, 2, targets)
-    (spread,) = next_residual(exchange(parts, ROW), rest, 1)
-    root = solve_root(exchange(spread, ROW), weights_one)
+    two, parts, keep = solve_two(spread, weights_two)
+    spread = exchange(next_residual(exchange(parts, ROW), residual[4:6]), ROW)
+    one, parts = solve_one(spread, weights_one, keep)
+    spread = exchange(next_residual(exchange(parts, ROW), residual[6:]), ROW)
+    root = solve_root(spread, weights_one)
     return jnp.concatenate([leaves, two, one, root], axis=0)
 
 

time: 335 us -> 329 us (0.982)
  the two profiles are of different devices: /device:TPU:72 before, /device:TPU:8 now
where the time goes in v9:
time: 329 us; the launch traced here: 328 us
  blocking collectives  141 us (43%)
  waiting for transfers between devices  89.3 us (27%)
  starting transfers between devices  44.3 us (13%)
  Pallas kernels  27.7 us (8%)
  between operations  13.3 us (4%)
  local copies, waits for them, and re-layouts  11.7 us (4%)
    all_to_all x4, blocking collectives, exchange(): return lax.all_to_all(flat, axes, 0, 0, tiled=True).reshape(shape)  141 us
    all_to_all x4, waiting for transfers between devices, exchange(): return lax.all_to_all(flat, axes, 0, 0, tiled=True).reshape(shape)  86.7 us
    all_to_all x4, starting transfers between devices, exchange(): return lax.all_to_all(flat, axes, 0, 0, tiled=True).reshape(shape)  40.9 us
    pallas_call x1, Pallas kernels, solve_two(): pl.pallas_call(kernel, in_specs=[VMEM, HBM], out_specs=[VMEM, VMEM, VMEM]...  9.65 us
    unnamed x23, local copies, waits for them, and re-layouts  6.74 us
    pallas_call x1, Pallas kernels, solve_leaves(): pl.pallas_call(kernel, in_specs=[VMEM, HBM], out_specs=[VMEM, VMEM], out_...  6.59 us
  transfers between devices with their start and end apart: 10, of which 5 were waited for; matrix products, arithmetic and copies ran while one was open for 1% of the time, Pallas kernels for 4%

profile of v9, /device:TPU:8, one launch (start us, length us, event | category | flops | bytes accessed | tf_op | source)
XLA Modules:
  0.0 328.1 jit_solution(6570973447467263238)
XLA Ops:
  6.5 0.9 slice.26
  7.5 1.9 slice.17
  9.4 0.7 collective-permute-start
  10.1 1.6 broadcast_in_dim.17
  11.7 26.2 %all-to-all-start = ((bf16[32,128,256]{2,1,0:T(8,128)(2,1)}), bf16[32,128,256]{2,1,0:T(8,128)(2,1)}, u32[]{:S(2)}, u32[]{:S(2)}) async-start(bf16[32,128,256]{2,1,0:T(8,128)(2,1)} %broadcast_in_dim.17), calls=%async_computation | async-start | bytes 4194304 | tf_op jit(solution)/shard_map/all_to_all | solution.py:297
  38.4 1.2 copy-done.2
  39.6 0.8 stack_weights.1
  40.4 0.9 copy-done.3
  41.3 0.7 copy-done.5
  42.0 45.2 %all-to-all-done = bf16[32,128,256]{2,1,0:T(8,128)(2,1)} async-done(((bf16[32,128,256]{2,1,0:T(8,128)(2,1)}), bf16[32,128,256]{2,1,0:T(8,128)(2,1)}, u32[]{:S(2)}, u32[]{:S(2)}) %all-to-all-start) | async-done | bytes 2097184 | tf_op jit(solution)/shard_map/all_to_all | solution.py:297
  87.2 6.6 %solve_leaves.1 = (f32[8,32,128]{2,1,0:T(8,128)}, bf16[8,8,32,128]{3,2,1,0:T(8,128)(2,1)}) custom-call(bf16[32,8,16,256]{3,2,1,0:T(8,128)(2,1)} %bitcast.1.b_ref, bf16[16,8,128,256]{3,2,1,0:T(8,128)(2,1)} %bitcast.33), custom_call_target="tpu_custom_call" | custom-call | tf_op jit(solution)/shard_map/solve_leaves/pallas_call | solution.py:94
  93.8 25.1 %all_to_all.40 = bf16[8,256,128]{2,1,0:T(8,128)(2,1)S(1)} all-to-all(bf16[8,256,128]{2,1,0:T(8,128)(2,1)} %bitcast.37), channel_id=1, replica_groups=mesh['x'=4,'y'=8,'z'=8,'core'=2] {'z'}, dimensions={0} | all-to-all | bytes 1048576 | tf_op jit(solution)/shard_map/all_to_all | solution.py:297
  119.0 0.7 all-gather.11.cloned.1.call-update
  119.7 1.9 collective-permute-start.1
  121.6 1.9 collective-permute-done.1.b_ref
  123.5 2.4 update_from_leaves.1
  125.9 53.1 %all_to_all.41 = bf16[32,224,128]{2,1,0:T(8,128)(2,1)S(1)} all-to-all(bf16[32,224,128]{2,1,0:T(8,128)(2,1)S(1)} %bitcast.24), channel_id=1, replica_groups=mesh['x'=4,'y'=8,'z'=8,'core'=2] {'x','y'}, dimensions={0} | all-to-all | bytes 3670016 | tf_op jit(solution)/shard_map/all_to_all | solution.py:297
  179.2 0.7 collective-permute-start.2
  180.2 47.8 %all_to_all.42 = bf16[32,128,128]{2,1,0:T(8,128)(2,1)} all-to-all(bf16[32,128,128]{2,1,0:T(8,128)(2,1)S(1)} %broadcast_in_dim.19), channel_id=1, replica_groups=mesh['x'=4,'y'=8,'z'=8,'core'=2] {'x','y'}, dimensions={0} | all-to-all | bytes 2097152 | tf_op jit(solution)/shard_map/all_to_all | solution.py:297
  227.9 9.7 %solve_two.1 = (f32[4,32,128]{2,1,0:T(8,128)}, bf16[32,2,32,128]{3,2,1,0:T(8,128)(2,1)}, f32[32,32,128]{2,1,0:T(8,128)}) custom-call(bf16[32,4,32,128]{3,2,1,0:T(8,128)(2,1)} %bitcast.34, bf16[16,12,128,256]{3,2,1,0:T(8,128)(2,1)} %bitcast.32), custom_call_target="tpu_custom_call" | custom-call | tf_op jit(solution)/shard_map/solve_two/pallas_call | solution.py:216
  237.6 5.1 %all-to-all-start.4 = ((bf16[32,64,128]{2,1,0:T(8,128)(2,1)}), bf16[32,64,128]{2,1,0:T(8,128)(2,1)S(1)}, u32[]{:S(2)}, u32[]{:S(2)}) async-start(bf16[32,64,128]{2,1,0:T(8,128)(2,1)} %bitcast.36), calls=%async_computation.4 | async-start | bytes 1048576 | tf_op jit(solution)/shard_map/all_to_all | solution.py:297
  242.7 15.4 %all-to-all-done.4 = bf16[32,64,128]{2,1,0:T(8,128)(2,1)S(1)} async-done(((bf16[32,64,128]{2,1,0:T(8,128)(2,1)}), bf16[32,64,128]{2,1,0:T(8,128)(2,1)S(1)}, u32[]{:S(2)}, u32[]{:S(2)}) %all-to-all-start.4) | async-done | bytes 524320 | tf_op jit(solution)/shard_map/all_to_all | solution.py:297
  258.1 0.9 next_residual.2
  259.0 4.8 %all-to-all-start.5 = ((bf16[32,64,128]{2,1,0:T(8,128)(2,1)}), bf16[32,64,128]{2,1,0:T(8,128)(2,1)S(1)}, u32[]{:S(2)}, u32[]{:S(2)}) async-start(bf16[32,64,128]{2,1,0:T(8,128)(2,1)} %bitcast.15), calls=%async_computation.5 | async-start | bytes 1048576 | tf_op jit(solution)/shard_map/all_to_all | solution.py:297
  263.9 15.0 %all-to-all-done.5 = bf16[32,64,128]{2,1,0:T(8,128)(2,1)S(1)} async-done(((bf16[32,64,128]{2,1,0:T(8,128)(2,1)}), bf16[32,64,128]{2,1,0:T(8,128)(2,1)S(1)}, u32[]{:S(2)}, u32[]{:S(2)}) %all-to-all-start.5) | async-done | bytes 524320 | tf_op jit(solution)/shard_map/all_to_all | solution.py:297
  278.9 0.8 copy-done.6
  279.7 6.6 %solve_one.1 = (f32[2,32,128]{2,1,0:T(8,128)}, bf16[32,1,32,128]{3,2,1,0:T(8,128)(2,1)}) custom-call(bf16[32,2,32,128]{3,2,1,0:T(8,128)(2,1)} %bitcast.35, bf16[16,5,128,256]{3,2,1,0:T(8,128)(2,1)} %bitcast.22, f32[32,32,128]{2,1,0:T(8,128)} %get-tuple-element.36.keep_ref), custom_call_target="tpu_custom_call" | custom-call | tf_op jit(solution)/shard_map/solve_one/pallas_call | solution.py:244
  286.3 4.9 %all-to-all-start.6 = ((bf16[32,32,128]{2,1,0:T(8,128)(2,1)}), bf16[32,32,128]{2,1,0:T(8,128)(2,1)S(1)}, u32[]{:S(2)}, u32[]{:S(2)}) async-start(bf16[32,32,128]{2,1,0:T(8,128)(2,1)} %bitcast.38), calls=%async_computation.6 | async-start | bytes 524288 | tf_op jit(solution)/shard_map/all_to_all | solution.py:297
  291.2 11.0 %all-to-all-done.6 = bf16[32,32,128]{2,1,0:T(8,128)(2,1)S(1)} async-done(((bf16[32,32,128]{2,1,0:T(8,128)(2,1)}), bf16[32,32,128]{2,1,0:T(8,128)(2,1)S(1)}, u32[]{:S(2)}, u32[]{:S(2)}) %all-to-all-start.6) | async-done | bytes 262176 | tf_op jit(solution)/shard_map/all_to_all | solution.py:297
  302.3 15.2 %all_to_all.43 = bf16[32,32,128]{2,1,0:T(8,128)(2,1)S(1)} all-to-all(bf16[32,32,128]{2,1,0:T(8,128)(2,1)S(1)} %bitcast.30), channel_id=1, replica_groups=mesh['x'=4,'y'=8,'z'=8,'core'=2] {'x','y'}, dimensions={0} | all-to-all | bytes 524288 | tf_op jit(solution)/shard_map/all_to_all | solution.py:297
  317.5 2.5 copy-done
  320.9 0.7 pad_maximum_fusion
  (37 shorter events, 2.1 us)
Async XLA Ops:
  6.5 80.6 %all-gather.7.cloned.1.call-start = ((), (), s32[]{:S(2)}) async-start(), calls=%async_computation.8 | async-start | bytes 8912896 | tf_op jit(solution)/shard_map/all_gather | solution.py:319
  9.4 0.7 collective-permute-start
  10.1 27.8 %copy-start.10 = (s32[14,16,3]{1,0,2:T(8,128)S(1)}, s32[14,16,3]{1,0,2:T(8,128)}, u32[]{:S(2)}) copy-start(s32[14,16,3]{1,0,2:T(8,128)} %param.7) | copy-start | bytes 8068
  11.7 26.7 %copy-start.1 = (bf16[14,3,256,128]{3,2,1,0:T(8,128)(2,1)S(1)}, bf16[14,3,256,128]{3,2,1,0:T(8,128)(2,1)}, u32[]{:S(2)}) copy-start(bf16[14,3,256,128]{3,2,1,0:T(8,128)(2,1)} %p_ref.3) | copy-start | bytes 8257540
  11.7 75.5 %all-to-all-start = ((bf16[32,128,256]{2,1,0:T(8,128)(2,1)}), bf16[32,128,256]{2,1,0:T(8,128)(2,1)}, u32[]{:S(2)}, u32[]{:S(2)}) async-start(bf16[32,128,256]{2,1,0:T(8,128)(2,1)} %broadcast_in_dim.17), calls=%async_computation | async-start | bytes 4194304 | tf_op jit(solution)/shard_map/all_to_all | solution.py:297
  37.9 190.1 %all-gather.9.cloned.1.call-start = ((), (), s32[]{:S(2)}) async-start(), calls=%async_computation.9 | async-start | bytes 13369344 | tf_op jit(solution)/shard_map/all_gather | solution.py:333
  38.4 1.2 copy-start.2
  40.4 0.9 copy-start.3
  41.3 0.7 copy-start.5
  87.2 36.3 %copy-start.4 = (f32[15,16,256]{2,1,0:T(8,128)S(1)}, f32[15,16,256]{2,1,0:T(8,128)}, u32[]{:S(2)}) copy-start(f32[15,16,256]{2,1,0:T(8,128)} %r_ref.1) | copy-start | bytes 737284
  118.9 145.0 %all-gather.11.cloned.1.call-start = ((), (), s32[]{:S(2)}) async-start(), calls=%async_computation.10 | async-start | bytes 5570560 | tf_op jit(solution)/shard_map/all_gather | solution.py:334
  119.7 3.8 %collective-permute-start.1 = (bf16[8,8,32,128]{3,2,1,0:T(8,128)(2,1)S(1)}, bf16[8,8,32,128]{3,2,1,0:T(8,128)(2,1)S(1)}, u32[]{:S(2)}, u32[]{:S(2)}) collective-permute-start(bf16[8,8,32,128]{3,2,1,0:T(8,128)(2,1)S(1)} %bitcast.26), channel_id=1, source_target_pairs={{0,1},{1,0},{2,3},{3,2},{4,5},{5,4},{6,7},{7,6},{8,9},{9,8},{10,11... | collective-permute-start | bytes 1572872 | tf_op jit(solution)/shard_map/ppermute | solution.py:331
  179.2 0.7 collective-permute-start.2
  237.6 20.5 %all-to-all-start.4 = ((bf16[32,64,128]{2,1,0:T(8,128)(2,1)}), bf16[32,64,128]{2,1,0:T(8,128)(2,1)S(1)}, u32[]{:S(2)}, u32[]{:S(2)}) async-start(bf16[32,64,128]{2,1,0:T(8,128)(2,1)} %bitcast.36), calls=%async_computation.4 | async-start | bytes 1048576 | tf_op jit(solution)/shard_map/all_to_all | solution.py:297
  259.0 19.9 %all-to-all-start.5 = ((bf16[32,64,128]{2,1,0:T(8,128)(2,1)}), bf16[32,64,128]{2,1,0:T(8,128)(2,1)S(1)}, u32[]{:S(2)}, u32[]{:S(2)}) async-start(bf16[32,64,128]{2,1,0:T(8,128)(2,1)} %bitcast.15), calls=%async_computation.5 | async-start | bytes 1048576 | tf_op jit(solution)/shard_map/all_to_all | solution.py:297
  278.9 0.8 copy-start.6
  286.3 15.9 %all-to-all-start.6 = ((bf16[32,32,128]{2,1,0:T(8,128)(2,1)}), bf16[32,32,128]{2,1,0:T(8,128)(2,1)S(1)}, u32[]{:S(2)}, u32[]{:S(2)}) async-start(bf16[32,32,128]{2,1,0:T(8,128)(2,1)} %bitcast.38), calls=%async_computation.6 | async-start | bytes 524288 | tf_op jit(solution)/shard_map/all_to_all | solution.py:297
  317.5 2.5 copy-start
  319.9 0.9 copy-start.7
  320.0 0.9 copy-start.8
  320.0 0.9 copy-start.9
Sparse Core Ops, SparseCore 0:
  9.5 63.9 all-gather.6
  119.0 76.2 all-gather.8
  197.5 44.4 all-gather.10

commit v10 on v9

--- a/solution.py
+++ b/solution.py
@@ -75,11 +75,14 @@
 
 def solve_leaves(spread, inverse):
     def kernel(b_ref, d_hbm, x_ref, h_ref, d_ref, sem):
-        copies = [pltpu.make_async_copy(d_hbm.at[c], d_ref.at[c], sem.at[c]) for c in range(NC)]
-        for copy in copies:
-            copy.start()
+        copies = []
+        for g in range(4):
+            part = pl.ds(4 * g, 4)
+            copies.append(pltpu.make_async_copy(d_hbm.at[part], d_ref.at[part], sem.at[g]))
+            copies[g].start()
         for c in range(NC):
-            copies[c].wait()
+            if c % 4 == 0:
+                copies[c // 4].wait()
             for n in range(8):
                 left = b_ref[2 * c : 2 * c + 2, n].reshape(32, 256)
                 value = dot_t(left, d_ref[c, n])
@@ -101,55 +104,79 @@
         ],
         scratch_shapes=[
             pltpu.VMEM((NC, 8, 128, 256), BF16),
-            pltpu.SemaphoreType.DMA((NC,)),
+            pltpu.SemaphoreType.DMA((4,)),
         ],
         compiler_params=params(0, STREAM_LIMIT),
         name="solve_leaves",
     )(spread, inverse)
 
 
-def update_from_leaves(meta, own, other, panels, right):
-    def kernel(meta_ref, a_ref, b_ref, p_ref, r_ref, o_ref):
+LEAF_PAIRS = [[0], [2], [4], [6], [0, 2], [4, 6], [0, 2, 4, 6]]
+
+
+def select_leaves(meta, panels):
+    def kernel(meta_ref, p_ref, o_ref):
+        place = 0
+        for t, firsts in enumerate(LEAF_PAIRS):
+            for s in firsts:
+                o_ref[place, :, :128] = selected(meta_ref, p_ref, s, 8 + t)
+                o_ref[place, :, 128:] = selected(meta_ref, p_ref, s + 1, 8 + t)
+                place += 1
+
+    return pl.pallas_call(
+        kernel,
+        grid=(1,),
+        in_specs=[SMEM, pl.BlockSpec((8, 3, 256, 128), lambda i: (0, 0, 0, 0))],
+        out_specs=VMEM,
+        out_shape=jax.ShapeDtypeStruct((12, 256, 256), BF16),
+        compiler_params=params(),
+        name="select_leaves",
+    )(meta, panels)
+
+
+def update_from_leaves(meta, solved, blocks, blocks_got, right, right_got):
+    def kernel(meta_ref, x_ref, a_ref, b_ref, r_ref, rg_ref, o_ref):
         core, row = meta_ref[1], meta_ref[2]
-        for t in range(7):
-            target = 8 + t
-            if t < 4:
-                sources = range(2 * t, 2 * t + 2)
-            elif t < 6:
-                sources = range(4 * (t - 4), 4 * (t - 4) + 4)
-            else:
-                sources = range(8)
-            blocks = [selected(meta_ref, p_ref, s, target) for s in sources]
-            for parity, x_ref in ((core, a_ref), (1 - core, b_ref)):
+        joined = {}
+        for s in range(0, 8, 2):
+            joined[s] = jnp.concatenate(
+                [x_ref[:, s].reshape(256, 128), x_ref[:, s + 1].reshape(256, 128)], axis=1
+            )
+        place = 0
+        for t, firsts in enumerate(LEAF_PAIRS):
+            for column, block_ref in ((core, a_ref), (1 - core, b_ref)):
                 acc = jnp.zeros((256, 256), F32)
-                for s, block in zip(sources, blocks, strict=True):
-                    acc = acc + dot_t(x_ref[:, s].reshape(256, 128), block)
+                for i, s in enumerate(firsts):
+                    acc = acc + dot_t(joined[s], block_ref[place + i])
                 for half in range(2):
                     value = acc[:, 128 * half : 128 * half + 128].astype(BF16)
-                    o_ref[:, pl.ds(parity, 1), half, t] = value.reshape(8, 1, 32, 128)
-        z, parity = row // 4, (row // 2) % 2
+                    o_ref[:, pl.ds(column, 1), half, t] = value.reshape(8, 1, 32, 128)
+            place += len(firsts)
+        z = row // 4
         start = pl.multiple_of(16 * (row % 2), 16)
-        for half in range(2):
+
+        @pl.when(core == (row // 2) % 2)
+        def _():
             for t in range(7):
-                part = o_ref[z, parity, half, t, pl.ds(start, 16), :].astype(F32)
-                part = part - r_ref[8 + t, :, 128 * half : 128 * half + 128]
-                o_ref[z, parity, half, t, pl.ds(start, 16), :] = part.astype(BF16)
-
-    return pl.pallas_call(
-        kernel,
-        grid=(1,),
-        in_specs=[
-            SMEM,
-            VMEM,
-            VMEM,
-            pl.BlockSpec((8, 3, 256, 128), lambda i: (0, 0, 0, 0)),
-            VMEM,
-        ],
+                for half in range(2):
+                    columns = slice(128 * half, 128 * half + 128)
+                    for column, held in (
+                        (core, r_ref[8 + t, :, columns]),
+                        (1 - core, rg_ref[t, :, columns]),
+                    ):
+                        part = o_ref[z, column, half, t, pl.ds(start, 16), :].astype(F32)
+                        o_ref[z, column, half, t, pl.ds(start, 16), :] = (part - held).astype(
+                            BF16
+                        )
+
+    return pl.pallas_call(
+        kernel,
+        in_specs=[SMEM, VMEM, VMEM, VMEM, VMEM, VMEM],
         out_specs=VMEM,
         out_shape=jax.ShapeDtypeStruct((8, 2, 2, 7, 32, 128), BF16),
-        compiler_params=params(),
+        compiler_params=params(0),
         name="update_from_leaves",
-    )(meta, own, other, panels, right)
+    )(meta, solved, blocks, blocks_got, right, right_got)
 
 
 def first_residual(parts):
@@ -174,9 +201,11 @@
     return acc
 
 
-def solve_pairs(x_ref, w_hbm, s_ref, w_ref, sem, nodes, first, update):
-    pieces = [(c, slice(0, nodes)) for c in range(NC)]
-    pieces += [(c, slice(first, None)) for c in range(NC)]
+def solve_pairs(x_ref, w_hbm, s_ref, w_ref, sem, nodes, first, groups, update):
+    size = NC // groups
+    parts = [pl.ds(g * size, size) for g in range(groups)]
+    pieces = [(part, slice(0, nodes)) for part in parts]
+    pieces += [(part, slice(first, None)) for part in parts]
     copies = [
         pltpu.make_async_copy(w_hbm.at[piece], w_ref.at[piece], sem.at[i])
         for i, piece in enumerate(pieces)
@@ -184,7 +213,8 @@
     for copy in copies:
         copy.start()
     for c in range(NC):
-        copies[c].wait()
+        if c % size == 0:
+            copies[c // size].wait()
         for n in range(nodes):
             left = jnp.concatenate([x_ref[2 * c, n], x_ref[2 * c + 1, n]], axis=1)
             value = dot_t(left, w_ref[c, n])
@@ -196,7 +226,8 @@
         for n in range(0, nodes, 2)
     ]
     for c in range(NC):
-        copies[NC + c].wait()
+        if c % size == 0:
+            copies[groups + c // size].wait()
         update(c, joined)
 
 
@@ -211,7 +242,7 @@
                     joined[1], w_ref[c, 10 + half]
                 )
 
-        solve_pairs(x_ref, w_hbm, s_ref, w_ref, sem, 4, 4, update)
+        solve_pairs(x_ref, w_hbm, s_ref, w_ref, sem, 4, 4, 4, update)
 
     return pl.pallas_call(
         kernel,
@@ -224,7 +255,7 @@
         ],
         scratch_shapes=[
             pltpu.VMEM(weights.shape, BF16),
-            pltpu.SemaphoreType.DMA((2 * NC,)),
+            pltpu.SemaphoreType.DMA((8,)),
         ],
         compiler_params=params(0, STREAM_LIMIT),
         name="solve_two",
@@ -239,7 +270,7 @@
                 part = keep_ref[r] + dot_t(joined[0], w_ref[c, 3 + half])
                 o_ref[r, 0] = part.astype(BF16)
 
-        solve_pairs(x_ref, w_hbm, s_ref, w_ref, sem, 2, 3, update)
+        solve_pairs(x_ref, w_hbm, s_ref, w_ref, sem, 2, 3, 2, update)
 
     return pl.pallas_call(
         kernel,
@@ -251,7 +282,7 @@
         ],
         scratch_shapes=[
             pltpu.VMEM(weights.shape, BF16),
-            pltpu.SemaphoreType.DMA((2 * NC,)),
+            pltpu.SemaphoreType.DMA((4,)),
         ],
         compiler_params=params(0, STREAM_LIMIT),
         name="solve_one",
@@ -260,14 +291,15 @@
 
 def solve_root(residual, weights):
     def kernel(x_ref, d_ref, s_ref):
-        s_ref[0] = solve_node(x_ref, d_ref, 0, 2)
-
-    return pl.pallas_call(
-        kernel,
-        in_specs=[VMEM, VMEM],
+        s_ref[0] = solve_node(x_ref, d_ref, 0, 0)
+
+    return pl.pallas_call(
+        kernel,
+        grid=(1,),
+        in_specs=[VMEM, pl.BlockSpec((NC, 1, 128, 256), lambda i: (0, 2, 0, 0))],
         out_specs=VMEM,
         out_shape=jax.ShapeDtypeStruct((1, 32, 128), F32),
-        compiler_params=params(0),
+        compiler_params=params(1, STREAM_LIMIT),
         name="solve_root",
     )(residual, weights)
 
@@ -306,6 +338,19 @@
         (r * NC + c, (2 * c + r % 2) * NC + r // 2) for r in range(NR) for c in range(NC)
     ]
     return lax.ppermute(values, ALL, pairs)
+
+
+def to_solver(values):
+    pairs = [
+        (r * NC + c, (4 * (c // 2) + r % 4) * NC + 2 * (r // 4) + c % 2)
+        for r in range(NR)
+        for c in range(NC)
+    ]
+    return lax.ppermute(values, ALL, pairs)
+
+
+def to_other_core(values):
+    return lax.ppermute(values, "core", [(0, 1), (1, 0)])
 
 
 def per_device(right_sides, diag_inverse, panels, block_map):
@@ -324,17 +369,20 @@
     )
     stack_two, stack_one = stack_weights(meta, diag_inverse, panels)
     spread = spread_over(moved, ROW, NR)
-    spread, stack_two, stack_one = lax.optimization_barrier((spread, stack_two, stack_one))
+    blocks = select_leaves(meta, panels)
+    blocks_got, right_got = to_other_core(blocks), to_other_core(right_sides[8:])
+    spread, stack_two, stack_one, blocks, blocks_got, right_got = lax.optimization_barrier(
+        (spread, stack_two, stack_one, blocks, blocks_got, right_got)
+    )
 
     leaves, copies = solve_leaves(spread, leaf_inverse)
     own = exchange(copies, "z")
-    other = lax.ppermute(own, "core", [(0, 1), (1, 0)])
     stack_two, stack_one, own = lax.optimization_barrier((stack_two, stack_one, own))
     weights_two = lax.all_gather(stack_two, COL, axis=0)
     weights_one = lax.all_gather(stack_one, COL, axis=0)
-    parts = update_from_leaves(meta, own, other, panels, right_sides)
+    parts = update_from_leaves(meta, own, blocks, blocks_got, right_sides, right_got)
     parts = exchange(parts.reshape(NR, 7, 32, 128), ROW)
-    residual = to_owner(first_residual(parts))
+    residual = to_solver(first_residual(parts))
 
     spread = spread_over(residual[:4], ROW, NR)
     two, parts, keep = solve_two(spread, weights_two)

time: 329 us -> 320 us (0.973)
  waiting for transfers between devices: 89.3 us -> 81.2 us
    all_to_all x4, waiting for transfers between devices: 86.7 us -> 80.5 us  [exchange(): return lax.all_to_all(flat, axes, 0, 0, tiled=True).reshape(shape)]
    unnamed x23 -> x25, local copies, waits for them, and re-layouts: 6.74 us -> 3.53 us
  transfers between devices with their start and end apart: 10 -> 11, of which waited for: 5 -> 4; matrix products, arithmetic and copies ran while one was open for 1% -> 1% of each run, Pallas kernels for 4% -> 4%
where the time goes in v10:
time: 320 us; the launch traced here: 319 us
  blocking collectives  139 us (43%)
  waiting for transfers between devices  81.2 us (25%)
  starting transfers between devices  46.1 us (14%)
  Pallas kernels  28.5 us (9%)
  between operations  13.4 us (4%)
  local copies, waits for them, and re-layouts  8.48 us (3%)
    all_to_all x4, blocking collectives, exchange(): return lax.all_to_all(flat, axes, 0, 0, tiled=True).reshape(shape)  139 us
    all_to_all x4, waiting for transfers between devices, exchange(): return lax.all_to_all(flat, axes, 0, 0, tiled=True).reshape(shape)  80.5 us
    all_to_all x4, starting transfers between devices, exchange(): return lax.all_to_all(flat, axes, 0, 0, tiled=True).reshape(shape)  40.4 us
    pallas_call x1, Pallas kernels, solve_two(): pl.pallas_call(kernel, in_specs=[VMEM, HBM], out_specs=[VMEM, VMEM, VMEM]...  8.62 us
    pallas_call x1, Pallas kernels, solve_leaves(): pl.pallas_call(kernel, in_specs=[VMEM, HBM], out_specs=[VMEM, VMEM], out_...  6.89 us
  transfers between devices with their start and end apart: 11, of which 4 were waited for; matrix products, arithmetic and copies ran while one was open for 1% of the time, Pallas kernels for 4%

profile of v10, /device:TPU:8, one launch (start us, length us, event | category | flops | bytes accessed | tf_op | source)
XLA Modules:
  0.0 318.5 jit_solution(9886486294772337096)
XLA Ops:
  6.5 0.9 slice.30
  7.5 1.9 slice.21
  9.4 0.7 collective-permute-start
  10.1 1.6 broadcast_in_dim.17
  11.7 26.2 %all-to-all-start = ((bf16[32,128,256]{2,1,0:T(8,128)(2,1)}), bf16[32,128,256]{2,1,0:T(8,128)(2,1)}, u32[]{:S(2)}, u32[]{:S(2)}) async-start(bf16[32,128,256]{2,1,0:T(8,128)(2,1)} %broadcast_in_dim.17), calls=%async_computation | async-start | bytes 4194304 | tf_op jit(solution)/shard_map/all_to_all | solution.py:329
  38.4 1.0 select_leaves.1.a_ref
  39.4 1.9 collective-permute-start.1
  41.4 2.4 collective-permute-start.2
  43.8 1.8 stack_weights.1
  45.6 1.1 copy-done.4
  46.8 40.4 %all-to-all-done = bf16[32,128,256]{2,1,0:T(8,128)(2,1)} async-done(((bf16[32,128,256]{2,1,0:T(8,128)(2,1)}), bf16[32,128,256]{2,1,0:T(8,128)(2,1)}, u32[]{:S(2)}, u32[]{:S(2)}) %all-to-all-start) | async-done | bytes 2097184 | tf_op jit(solution)/shard_map/all_to_all | solution.py:329
  87.2 6.9 %solve_leaves.1 = (f32[8,32,128]{2,1,0:T(8,128)}, bf16[8,8,32,128]{3,2,1,0:T(8,128)(2,1)}) custom-call(bf16[32,8,16,256]{3,2,1,0:T(8,128)(2,1)} %bitcast.1.b_ref, bf16[16,8,128,256]{3,2,1,0:T(8,128)(2,1)} %bitcast.31), custom_call_target="tpu_custom_call" | custom-call | tf_op jit(solution)/shard_map/solve_leaves/pallas_call | solution.py:97
  94.1 25.3 %all_to_all.40 = bf16[8,256,128]{2,1,0:T(8,128)(2,1)S(1)} all-to-all(bf16[8,256,128]{2,1,0:T(8,128)(2,1)} %bitcast.36), channel_id=1, replica_groups=mesh['x'=4,'y'=8,'z'=8,'core'=2] {'z'}, dimensions={0} | all-to-all | bytes 1048576 | tf_op jit(solution)/shard_map/all_to_all | solution.py:329
  119.5 0.7 all-gather.11.cloned.1.call-update
  120.2 1.4 copy-done.5
  121.6 1.8 update_from_leaves.1
  123.4 51.7 %all_to_all.41 = bf16[32,224,128]{2,1,0:T(8,128)(2,1)S(1)} all-to-all(bf16[32,224,128]{2,1,0:T(8,128)(2,1)S(1)} %bitcast.22), channel_id=1, replica_groups=mesh['x'=4,'y'=8,'z'=8,'core'=2] {'x','y'}, dimensions={0} | all-to-all | bytes 3670016 | tf_op jit(solution)/shard_map/all_to_all | solution.py:329
  175.3 0.7 collective-permute-start.3
  176.2 47.0 %all_to_all.42 = bf16[32,128,128]{2,1,0:T(8,128)(2,1)} all-to-all(bf16[32,128,128]{2,1,0:T(8,128)(2,1)S(1)} %broadcast_in_dim.19), channel_id=1, replica_groups=mesh['x'=4,'y'=8,'z'=8,'core'=2] {'x','y'}, dimensions={0} | all-to-all | bytes 2097152 | tf_op jit(solution)/shard_map/all_to_all | solution.py:329
  223.2 8.6 %solve_two.1 = (f32[4,32,128]{2,1,0:T(8,128)}, bf16[32,2,32,128]{3,2,1,0:T(8,128)(2,1)}, f32[32,32,128]{2,1,0:T(8,128)}) custom-call(bf16[32,4,32,128]{3,2,1,0:T(8,128)(2,1)} %bitcast.32, bf16[16,12,128,256]{3,2,1,0:T(8,128)(2,1)} %bitcast.30), custom_call_target="tpu_custom_call" | custom-call | tf_op jit(solution)/shard_map/solve_two/pallas_call | solution.py:247
  231.8 5.1 %all-to-all-start.4 = ((bf16[32,64,128]{2,1,0:T(8,128)(2,1)}), bf16[32,64,128]{2,1,0:T(8,128)(2,1)S(1)}, u32[]{:S(2)}, u32[]{:S(2)}) async-start(bf16[32,64,128]{2,1,0:T(8,128)(2,1)} %bitcast.35), calls=%async_computation.4 | async-start | bytes 1048576 | tf_op jit(solution)/shard_map/all_to_all | solution.py:329
  237.0 14.8 %all-to-all-done.4 = bf16[32,64,128]{2,1,0:T(8,128)(2,1)S(1)} async-done(((bf16[32,64,128]{2,1,0:T(8,128)(2,1)}), bf16[32,64,128]{2,1,0:T(8,128)(2,1)S(1)}, u32[]{:S(2)}, u32[]{:S(2)}) %all-to-all-start.4) | async-done | bytes 524320 | tf_op jit(solution)/shard_map/all_to_all | solution.py:329
  251.8 0.9 next_residual.2
  252.7 4.7 %all-to-all-start.5 = ((bf16[32,64,128]{2,1,0:T(8,128)(2,1)}), bf16[32,64,128]{2,1,0:T(8,128)(2,1)S(1)}, u32[]{:S(2)}, u32[]{:S(2)}) async-start(bf16[32,64,128]{2,1,0:T(8,128)(2,1)} %bitcast.15), calls=%async_computation.5 | async-start | bytes 1048576 | tf_op jit(solution)/shard_map/all_to_all | solution.py:329
  257.4 14.3 %all-to-all-done.5 = bf16[32,64,128]{2,1,0:T(8,128)(2,1)S(1)} async-done(((bf16[32,64,128]{2,1,0:T(8,128)(2,1)}), bf16[32,64,128]{2,1,0:T(8,128)(2,1)S(1)}, u32[]{:S(2)}, u32[]{:S(2)}) %all-to-all-start.5) | async-done | bytes 524320 | tf_op jit(solution)/shard_map/all_to_all | solution.py:329
  271.7 0.8 copy-done.7
  272.4 4.9 %solve_one.1 = (f32[2,32,128]{2,1,0:T(8,128)}, bf16[32,1,32,128]{3,2,1,0:T(8,128)(2,1)}) custom-call(bf16[32,2,32,128]{3,2,1,0:T(8,128)(2,1)} %bitcast.33, bf16[16,5,128,256]{3,2,1,0:T(8,128)(2,1)} %bitcast.28, f32[32,32,128]{2,1,0:T(8,128)} %get-tuple-element.42.keep_ref), custom_call_target="tpu_custom_call" | custom-call | tf_op jit(solution)/shard_map/solve_one/pallas_call | solution.py:275
  277.3 4.4 %all-to-all-start.6 = ((bf16[32,32,128]{2,1,0:T(8,128)(2,1)}), bf16[32,32,128]{2,1,0:T(8,128)(2,1)S(1)}, u32[]{:S(2)}, u32[]{:S(2)}) async-start(bf16[32,32,128]{2,1,0:T(8,128)(2,1)} %bitcast.37), calls=%async_computation.6 | async-start | bytes 524288 | tf_op jit(solution)/shard_map/all_to_all | solution.py:329
  281.8 11.0 %all-to-all-done.6 = bf16[32,32,128]{2,1,0:T(8,128)(2,1)S(1)} async-done(((bf16[32,32,128]{2,1,0:T(8,128)(2,1)}), bf16[32,32,128]{2,1,0:T(8,128)(2,1)S(1)}, u32[]{:S(2)}, u32[]{:S(2)}) %all-to-all-start.6) | async-done | bytes 262176 | tf_op jit(solution)/shard_map/all_to_all | solution.py:329
  292.8 15.4 %all_to_all.43 = bf16[32,32,128]{2,1,0:T(8,128)(2,1)} all-to-all(bf16[32,32,128]{2,1,0:T(8,128)(2,1)S(1)} %bitcast.27), channel_id=1, replica_groups=mesh['x'=4,'y'=8,'z'=8,'core'=2] {'x','y'}, dimensions={0} | all-to-all | bytes 524288 | tf_op jit(solution)/shard_map/all_to_all | solution.py:329
  308.2 2.4 solve_root.1
  310.6 1.4 pad_maximum_fusion
  (43 shorter events, 1.2 us)
Async XLA Ops:
  6.5 80.6 %all-gather.7.cloned.1.call-start = ((), (), s32[]{:S(2)}) async-start(), calls=%async_computation.8 | async-start | bytes 8912896 | tf_op jit(solution)/shard_map/all_gather | solution.py:364
  9.4 0.7 collective-permute-start
  11.7 26.2 %copy-start.11 = (s32[14,16,3]{1,0,2:T(8,128)S(1)}, s32[14,16,3]{1,0,2:T(8,128)}, u32[]{:S(2)}) copy-start(s32[14,16,3]{1,0,2:T(8,128)} %param.7) | copy-start | bytes 8068
  11.7 26.7 %copy-start = (bf16[14,3,256,128]{3,2,1,0:T(8,128)(2,1)S(1)}, bf16[14,3,256,128]{3,2,1,0:T(8,128)(2,1)}, u32[]{:S(2)}) copy-start(bf16[14,3,256,128]{3,2,1,0:T(8,128)(2,1)} %p_ref.3) | copy-start | bytes 8257540
  11.7 75.5 %all-to-all-start = ((bf16[32,128,256]{2,1,0:T(8,128)(2,1)}), bf16[32,128,256]{2,1,0:T(8,128)(2,1)}, u32[]{:S(2)}, u32[]{:S(2)}) async-start(bf16[32,128,256]{2,1,0:T(8,128)(2,1)} %broadcast_in_dim.17), calls=%async_computation | async-start | bytes 4194304 | tf_op jit(solution)/shard_map/all_to_all | solution.py:329
  37.9 185.3 %all-gather.9.cloned.1.call-start = ((), (), s32[]{:S(2)}) async-start(), calls=%async_computation.9 | async-start | bytes 13369344 | tf_op jit(solution)/shard_map/all_gather | solution.py:381
  38.4 3.0 copy-start.6
  38.4 5.4 %copy-start.3 = (bf16[15,128,256]{2,1,0:T(8,128)(2,1)S(1)}, bf16[15,128,256]{2,1,0:T(8,128)(2,1)}, u32[]{:S(2)}) copy-start(bf16[15,128,256]{2,1,0:T(8,128)(2,1)} %d_ref) | copy-start | bytes 2949124
  39.4 6.2 %copy-start.1 = (bf16[12,256,256]{2,1,0:T(8,128)(2,1)}, bf16[12,256,256]{2,1,0:T(8,128)(2,1)S(1)}, u32[]{:S(2)}) copy-start(bf16[12,256,256]{2,1,0:T(8,128)(2,1)S(1)} %select_leaves.1.a_ref) | copy-start | bytes 4718596
  39.4 6.2 %collective-permute-start.1 = (bf16[12,256,256]{2,1,0:T(8,128)(2,1)S(1)}, bf16[12,256,256]{2,1,0:T(8,128)(2,1)S(1)}, u32[]{:S(2)}, u32[]{:S(2)}) collective-permute-start(bf16[12,256,256]{2,1,0:T(8,128)(2,1)S(1)} %select_leaves.1.a_ref), channel_id=1, source_target_pairs={{0,1},{1,0},{2,3},{3,2},{4,5},{5,4},{6,7},{7,6},{8,9},{9,8},{10,11... | collective-permute-start | bytes 4718600 | tf_op jit(solution)/shard_map/ppermute | solution.py:353
  41.4 4.2 %collective-permute-start.2 = (f32[7,16,256]{2,1,0:T(8,128)S(1)}, f32[7,16,256]{2,1,0:T(8,128)S(1)}, u32[]{:S(2)}, u32[]{:S(2)}) collective-permute-start(f32[7,16,256]{2,1,0:T(8,128)S(1)} %slice.20), channel_id=1, source_target_pairs={{0,1},{1,0},{2,3},{3,2},{4,5},{5,4},{6,7},{7,6},{8,9},{9,8},{10,11... | collective-permute-start | bytes 344072 | tf_op jit(solution)/shard_map/ppermute | solution.py:353
  45.6 1.1 copy-start.4
  94.1 26.1 %copy-start.2 = (bf16[12,256,256]{2,1,0:T(8,128)(2,1)S(1)}, bf16[12,256,256]{2,1,0:T(8,128)(2,1)}, u32[]{:S(2)}) copy-start(bf16[12,256,256]{2,1,0:T(8,128)(2,1)} %copy-done.1) | copy-start | bytes 4718596
  119.4 137.9 %all-gather.11.cloned.1.call-start = ((), (), s32[]{:S(2)}) async-start(), calls=%async_computation.10 | async-start | bytes 5570560 | tf_op jit(solution)/shard_map/all_gather | solution.py:382
  120.2 1.4 copy-start.5
  175.3 0.7 collective-permute-start.3
  231.8 20.0 %all-to-all-start.4 = ((bf16[32,64,128]{2,1,0:T(8,128)(2,1)}), bf16[32,64,128]{2,1,0:T(8,128)(2,1)S(1)}, u32[]{:S(2)}, u32[]{:S(2)}) async-start(bf16[32,64,128]{2,1,0:T(8,128)(2,1)} %bitcast.35), calls=%async_computation.4 | async-start | bytes 1048576 | tf_op jit(solution)/shard_map/all_to_all | solution.py:329
  252.7 19.0 %all-to-all-start.5 = ((bf16[32,64,128]{2,1,0:T(8,128)(2,1)}), bf16[32,64,128]{2,1,0:T(8,128)(2,1)S(1)}, u32[]{:S(2)}, u32[]{:S(2)}) async-start(bf16[32,64,128]{2,1,0:T(8,128)(2,1)} %bitcast.15), calls=%async_computation.5 | async-start | bytes 1048576 | tf_op jit(solution)/shard_map/all_to_all | solution.py:329
  271.7 0.8 copy-start.7
  277.3 15.4 %all-to-all-start.6 = ((bf16[32,32,128]{2,1,0:T(8,128)(2,1)}), bf16[32,32,128]{2,1,0:T(8,128)(2,1)S(1)}, u32[]{:S(2)}, u32[]{:S(2)}) async-start(bf16[32,32,128]{2,1,0:T(8,128)(2,1)} %bitcast.37), calls=%async_computation.6 | async-start | bytes 524288 | tf_op jit(solution)/shard_map/all_to_all | solution.py:329
  308.1 2.4 copy-start.8
  308.1 2.4 copy-start.9
  308.1 2.4 copy-start.10
Sparse Core Ops, SparseCore 0:
  9.5 63.9 all-gather.6
  119.6 76.0 all-gather.8
  197.8 44.6 all-gather.10

commit v11 on v10

--- a/solution.py
+++ b/solution.py
@@ -74,15 +74,20 @@
 
 
 def solve_leaves(spread, inverse):
-    def kernel(b_ref, d_hbm, x_ref, h_ref, d_ref, sem):
+    def kernel(b_hbm, d_hbm, x_ref, h_ref, b_ref, d_ref, sem):
         copies = []
         for g in range(4):
-            part = pl.ds(4 * g, 4)
-            copies.append(pltpu.make_async_copy(d_hbm.at[part], d_ref.at[part], sem.at[g]))
-            copies[g].start()
+            part = pl.ds(8 * g, 8)
+            copies.append(pltpu.make_async_copy(b_hbm.at[part], b_ref.at[part], sem.at[g]))
+        for c in range(NC):
+            copies.append(pltpu.make_async_copy(d_hbm.at[c], d_ref.at[c], sem.at[4 + c]))
+        for g in range(4):
+            for i in (g, *range(4 + 4 * g, 8 + 4 * g)):
+                copies[i].start()
         for c in range(NC):
             if c % 4 == 0:
                 copies[c // 4].wait()
+            copies[4 + c].wait()
             for n in range(8):
                 left = b_ref[2 * c : 2 * c + 2, n].reshape(32, 256)
                 value = dot_t(left, d_ref[c, n])
@@ -96,15 +101,16 @@
 
     return pl.pallas_call(
         kernel,
-        in_specs=[VMEM, HBM],
+        in_specs=[HBM, HBM],
         out_specs=[VMEM, VMEM],
         out_shape=[
             jax.ShapeDtypeStruct((8, 32, 128), F32),
             jax.ShapeDtypeStruct((8, 8, 32, 128), BF16),
         ],
         scratch_shapes=[
+            pltpu.VMEM((32, 8, 16, 256), BF16),
             pltpu.VMEM((NC, 8, 128, 256), BF16),
-            pltpu.SemaphoreType.DMA((4,)),
+            pltpu.SemaphoreType.DMA((4 + NC,)),
         ],
         compiler_params=params(0, STREAM_LIMIT),
         name="solve_leaves",
@@ -135,23 +141,27 @@
 
 
 def update_from_leaves(meta, solved, blocks, blocks_got, right, right_got):
-    def kernel(meta_ref, x_ref, a_ref, b_ref, r_ref, rg_ref, o_ref):
+    def kernel(meta_ref, x_ref, a_ref, b_hbm, r_ref, rg_ref, o_ref, b_ref, sem):
         core, row = meta_ref[1], meta_ref[2]
+        copy = pltpu.make_async_copy(b_hbm, b_ref, sem.at[0])
+        copy.start()
         joined = {}
         for s in range(0, 8, 2):
             joined[s] = jnp.concatenate(
                 [x_ref[:, s].reshape(256, 128), x_ref[:, s + 1].reshape(256, 128)], axis=1
             )
-        place = 0
-        for t, firsts in enumerate(LEAF_PAIRS):
-            for column, block_ref in ((core, a_ref), (1 - core, b_ref)):
+        for column, block_ref in ((core, a_ref), (1 - core, b_ref)):
+            if block_ref is b_ref:
+                copy.wait()
+            place = 0
+            for t, firsts in enumerate(LEAF_PAIRS):
                 acc = jnp.zeros((256, 256), F32)
-                for i, s in enumerate(firsts):
-                    acc = acc + dot_t(joined[s], block_ref[place + i])
+                for s in firsts:
+                    acc = acc + dot_t(joined[s], block_ref[place])
+                    place += 1
                 for half in range(2):
                     value = acc[:, 128 * half : 128 * half + 128].astype(BF16)
                     o_ref[:, pl.ds(column, 1), half, t] = value.reshape(8, 1, 32, 128)
-            place += len(firsts)
         z = row // 4
         start = pl.multiple_of(16 * (row % 2), 16)
 
@@ -171,10 +181,14 @@
 
     return pl.pallas_call(
         kernel,
-        in_specs=[SMEM, VMEM, VMEM, VMEM, VMEM, VMEM],
+        in_specs=[SMEM, VMEM, VMEM, HBM, VMEM, VMEM],
         out_specs=VMEM,
         out_shape=jax.ShapeDtypeStruct((8, 2, 2, 7, 32, 128), BF16),
-        compiler_params=params(0),
+        scratch_shapes=[
+            pltpu.VMEM((12, 256, 256), BF16),
+            pltpu.SemaphoreType.DMA((1,)),
+        ],
+        compiler_params=params(0, STREAM_LIMIT),
         name="update_from_leaves",
     )(meta, solved, blocks, blocks_got, right, right_got)
 
@@ -201,11 +215,11 @@
     return acc
 
 
-def solve_pairs(x_ref, w_hbm, s_ref, w_ref, sem, nodes, first, groups, update):
+def solve_pairs(x_ref, w_hbm, s_ref, w_ref, sem, nodes, first, last, groups, update):
     size = NC // groups
     parts = [pl.ds(g * size, size) for g in range(groups)]
     pieces = [(part, slice(0, nodes)) for part in parts]
-    pieces += [(part, slice(first, None)) for part in parts]
+    pieces += [(part, slice(first, last)) for part in parts]
     copies = [
         pltpu.make_async_copy(w_hbm.at[piece], w_ref.at[piece], sem.at[i])
         for i, piece in enumerate(pieces)
@@ -232,34 +246,65 @@
 
 
 def solve_two(residual, weights):
-    def kernel(x_ref, w_hbm, s_ref, o_ref, keep_ref, w_ref, sem):
+    def kernel(x_ref, w_hbm, s_ref, o_ref, w_ref, sem):
         def update(c, joined):
             for half in range(2):
                 r = 2 * c + half
                 o_ref[r, 0] = dot_t(joined[0], w_ref[c, 4 + half]).astype(BF16)
                 o_ref[r, 1] = dot_t(joined[1], w_ref[c, 6 + half]).astype(BF16)
-                keep_ref[r] = dot_t(joined[0], w_ref[c, 8 + half]) + dot_t(
-                    joined[1], w_ref[c, 10 + half]
-                )
-
-        solve_pairs(x_ref, w_hbm, s_ref, w_ref, sem, 4, 4, 4, update)
+
+        solve_pairs(x_ref, w_hbm, s_ref, w_ref, sem, 4, 4, 8, 4, update)
 
     return pl.pallas_call(
         kernel,
         in_specs=[VMEM, HBM],
-        out_specs=[VMEM, VMEM, VMEM],
+        out_specs=[VMEM, VMEM],
         out_shape=[
             jax.ShapeDtypeStruct((4, 32, 128), F32),
             jax.ShapeDtypeStruct((NR, 2, 32, 128), BF16),
-            jax.ShapeDtypeStruct((NR, 32, 128), F32),
         ],
         scratch_shapes=[
-            pltpu.VMEM(weights.shape, BF16),
+            pltpu.VMEM((NC, 8, 128, 256), BF16),
             pltpu.SemaphoreType.DMA((8,)),
         ],
         compiler_params=params(0, STREAM_LIMIT),
         name="solve_two",
     )(residual, weights)
+
+
+def root_parts(solved, weights):
+    def kernel(s_ref, w_hbm, o_ref, w_ref, sem):
+        copies = []
+        for g in range(4):
+            part = pl.ds(4 * g, 4)
+            copies.append(
+                pltpu.make_async_copy(w_hbm.at[part, slice(8, 12)], w_ref.at[part], sem.at[g])
+            )
+            copies[g].start()
+        joined = [
+            jnp.concatenate([s_ref[n].astype(BF16), s_ref[n + 1].astype(BF16)], axis=1)
+            for n in (0, 2)
+        ]
+        for c in range(NC):
+            if c % 4 == 0:
+                copies[c // 4].wait()
+            for half in range(2):
+                o_ref[2 * c + half] = dot_t(joined[0], w_ref[c, half]) + dot_t(
+                    joined[1], w_ref[c, 2 + half]
+                )
+
+    return pl.pallas_call(
+        kernel,
+        in_specs=[VMEM, HBM],
+        out_specs=VMEM,
+        out_shape=jax.ShapeDtypeStruct((NR, 32, 128), F32),
+        scratch_shapes=[
+            pltpu.VMEM((NC, 4, 128, 256), BF16),
+            pltpu.SemaphoreType.DMA((4,)),
+        ],
+        compiler_params=params(0, STREAM_LIMIT),
+        name="root_parts",
+    )(solved, weights)
 
 
 def solve_one(residual, weights, keep):
@@ -270,7 +315,7 @@
                 part = keep_ref[r] + dot_t(joined[0], w_ref[c, 3 + half])
                 o_ref[r, 0] = part.astype(BF16)
 
-        solve_pairs(x_ref, w_hbm, s_ref, w_ref, sem, 2, 3, 2, update)
+        solve_pairs(x_ref, w_hbm, s_ref, w_ref, sem, 2, 3, 5, 2, update)
 
     return pl.pallas_call(
         kernel,
@@ -385,8 +430,9 @@
     residual = to_solver(first_residual(parts))
 
     spread = spread_over(residual[:4], ROW, NR)
-    two, parts, keep = solve_two(spread, weights_two)
-    spread = exchange(next_residual(exchange(parts, ROW), residual[4:6]), ROW)
+    two, parts = solve_two(spread, weights_two)
+    parts, keep = lax.optimization_barrier((exchange(parts, ROW), root_parts(two, weights_two)))
+    spread = exchange(next_residual(parts, residual[4:6]), ROW)
     one, parts = solve_one(spread, weights_one, keep)
     spread = exchange(next_residual(exchange(parts, ROW), residual[6:]), ROW)
     root = solve_root(spread, weights_one)

time: 320 us -> 318 us (level)
  Pallas kernels: 28.5 us -> 33 us
  waiting for transfers between devices: 81.2 us -> 76.7 us
    all_to_all x4, waiting for transfers between devices: 80.5 us -> 76 us  [exchange(): return lax.all_to_all(flat, axes, 0, 0, tiled=True).reshape(shape)]
    pallas_call x3 -> x4, Pallas kernels: 17.3 us -> 21.7 us  [the longest x1 6.68 us: solve_two(): pl.pallas_call(kernel, in_specs=[VMEM, HBM], out_specs=[VMEM, VMEM], out_...]
  transfers between devices with their start and end apart: 11 -> 11, of which waited for: 4 -> 4; matrix products, arithmetic and copies ran while one was open for 1% -> 1% of each run, Pallas kernels for 4% -> 6%
where the time goes in v11:
time: 318 us; the launch traced here: 317 us
  blocking collectives  140 us (44%)
  waiting for transfers between devices  76.7 us (24%)
  starting transfers between devices  46.1 us (14%)
  Pallas kernels  33 us (10%)
  between operations  13.4 us (4%)
  local copies, waits for them, and re-layouts  6.84 us (2%)
    all_to_all x4, blocking collectives, exchange(): return lax.all_to_all(flat, axes, 0, 0, tiled=True).reshape(shape)  140 us
    all_to_all x4, waiting for transfers between devices, exchange(): return lax.all_to_all(flat, axes, 0, 0, tiled=True).reshape(shape)  76 us
    all_to_all x4, starting transfers between devices, exchange(): return lax.all_to_all(flat, axes, 0, 0, tiled=True).reshape(shape)  40.4 us
    pallas_call x1, Pallas kernels, solve_two(): pl.pallas_call(kernel, in_specs=[VMEM, HBM], out_specs=[VMEM, VMEM], out_...  6.68 us
  transfers between devices with their start and end apart: 11, of which 4 were waited for; matrix products, arithmetic and copies ran while one was open for 1% of the time, Pallas kernels for 6%

profile of v11, /device:TPU:8, one launch (start us, length us, event | category | flops | bytes accessed | tf_op | source)
XLA Modules:
  0.0 317.1 jit_solution(13598391534021194117)
XLA Ops:
  6.5 0.9 slice.30
  7.5 1.9 slice.21
  9.4 0.7 collective-permute-start
  10.1 1.6 broadcast_in_dim.17
  11.7 26.2 %all-to-all-start = ((bf16[32,128,256]{2,1,0:T(8,128)(2,1)}), bf16[32,128,256]{2,1,0:T(8,128)(2,1)}, u32[]{:S(2)}, u32[]{:S(2)}) async-start(bf16[32,128,256]{2,1,0:T(8,128)(2,1)} %broadcast_in_dim.17), calls=%async_computation | async-start | bytes 4194304 | tf_op jit(solution)/shard_map/all_to_all | solution.py:374
  38.4 1.0 select_leaves.1.a_ref
  39.4 1.9 collective-permute-start.1
  41.4 0.9 slice.20
  42.3 2.4 collective-permute-start.2
  44.7 1.8 stack_weights.1
  46.5 40.6 %all-to-all-done = bf16[32,128,256]{2,1,0:T(8,128)(2,1)} async-done(((bf16[32,128,256]{2,1,0:T(8,128)(2,1)}), bf16[32,128,256]{2,1,0:T(8,128)(2,1)}, u32[]{:S(2)}, u32[]{:S(2)}) %all-to-all-start) | async-done | bytes 2097184 | tf_op jit(solution)/shard_map/all_to_all | solution.py:374
  87.2 5.4 %solve_leaves.1 = (f32[8,32,128]{2,1,0:T(8,128)}, bf16[8,8,32,128]{3,2,1,0:T(8,128)(2,1)}) custom-call(bf16[32,8,16,256]{3,2,1,0:T(8,128)(2,1)} %bitcast.1.b_hbm, bf16[16,8,128,256]{3,2,1,0:T(8,128)(2,1)} %bitcast.30), custom_call_target="tpu_custom_call" | custom-call | tf_op jit(solution)/shard_map/solve_leaves/pallas_call | solution.py:102
  92.5 25.2 %all_to_all.40 = bf16[8,256,128]{2,1,0:T(8,128)(2,1)} all-to-all(bf16[8,256,128]{2,1,0:T(8,128)(2,1)} %bitcast.37), channel_id=1, replica_groups=mesh['x'=4,'y'=8,'z'=8,'core'=2] {'z'}, dimensions={0} | all-to-all | bytes 1048576 | tf_op jit(solution)/shard_map/all_to_all | solution.py:374
  117.8 0.7 all-gather.11.cloned.1.call-update
  118.5 5.0 %update_from_leaves.1 = bf16[8,2,2,7,32,128]{5,4,3,2,1,0:T(8,128)(2,1)} custom-call(s32[676]{0:T(1024)} %copy-done.3, bf16[8,8,32,128]{3,2,1,0:T(8,128)(2,1)} %bitcast.33, bf16[12,256,256]{2,1,0:T(8,128)(2,1)} %copy-done.1, bf16[12,256,256]{2,1,0:T(8,128)(2,1)} %collective-permute-done.1.b_hbm, f32[15,16,256]{2,1,0:T(8,128)} %r_ref.1, f32[7,16,256]{2,1,0:T(8,128)} %copy-done.7), custom_call_target="tpu_custom_call" | custom-call | tf_op jit(solution)/shard_map/update_from_leaves/pallas_call | solution.py:182
  123.5 52.0 %all_to_all.41 = bf16[32,224,128]{2,1,0:T(8,128)(2,1)S(1)} all-to-all(bf16[32,224,128]{2,1,0:T(8,128)(2,1)} %bitcast.31), channel_id=1, replica_groups=mesh['x'=4,'y'=8,'z'=8,'core'=2] {'x','y'}, dimensions={0} | all-to-all | bytes 3670016 | tf_op jit(solution)/shard_map/all_to_all | solution.py:374
  175.8 0.7 collective-permute-start.3
  176.7 47.0 %all_to_all.42 = bf16[32,128,128]{2,1,0:T(8,128)(2,1)} all-to-all(bf16[32,128,128]{2,1,0:T(8,128)(2,1)S(1)} %broadcast_in_dim.19), channel_id=1, replica_groups=mesh['x'=4,'y'=8,'z'=8,'core'=2] {'x','y'}, dimensions={0} | all-to-all | bytes 2097152 | tf_op jit(solution)/shard_map/all_to_all | solution.py:374
  223.7 6.7 %solve_two.1 = (f32[4,32,128]{2,1,0:T(8,128)}, bf16[32,2,32,128]{3,2,1,0:T(8,128)(2,1)}) custom-call(bf16[32,4,32,128]{3,2,1,0:T(8,128)(2,1)} %bitcast.32, bf16[16,12,128,256]{3,2,1,0:T(8,128)(2,1)} %bitcast.26), custom_call_target="tpu_custom_call" | custom-call | tf_op jit(solution)/shard_map/solve_two/pallas_call | solution.py:258
  230.4 5.2 %all-to-all-start.4 = ((bf16[32,64,128]{2,1,0:T(8,128)(2,1)}), bf16[32,64,128]{2,1,0:T(8,128)(2,1)S(1)}, u32[]{:S(2)}, u32[]{:S(2)}) async-start(bf16[32,64,128]{2,1,0:T(8,128)(2,1)} %bitcast.36), calls=%async_computation.4 | async-start | bytes 1048576 | tf_op jit(solution)/shard_map/all_to_all | solution.py:374
  235.6 4.7 %root_parts.1.keep_ref = f32[32,32,128]{2,1,0:T(8,128)} custom-call(f32[4,32,128]{2,1,0:T(8,128)} %get-tuple-element.40.s_ref, bf16[16,12,128,256]{3,2,1,0:T(8,128)(2,1)} %bitcast.27), custom_call_target="tpu_custom_call" | custom-call | tf_op jit(solution)/shard_map/root_parts/pallas_call | solution.py:296
  240.3 10.1 %all-to-all-done.4 = bf16[32,64,128]{2,1,0:T(8,128)(2,1)S(1)} async-done(((bf16[32,64,128]{2,1,0:T(8,128)(2,1)}), bf16[32,64,128]{2,1,0:T(8,128)(2,1)S(1)}, u32[]{:S(2)}, u32[]{:S(2)}) %all-to-all-start.4) | async-done | bytes 524320 | tf_op jit(solution)/shard_map/all_to_all | solution.py:374
  250.4 0.9 next_residual.2
  251.3 4.6 %all-to-all-start.5 = ((bf16[32,64,128]{2,1,0:T(8,128)(2,1)}), bf16[32,64,128]{2,1,0:T(8,128)(2,1)S(1)}, u32[]{:S(2)}, u32[]{:S(2)}) async-start(bf16[32,64,128]{2,1,0:T(8,128)(2,1)} %bitcast.15), calls=%async_computation.5 | async-start | bytes 1048576 | tf_op jit(solution)/shard_map/all_to_all | solution.py:374
  256.0 14.2 %all-to-all-done.5 = bf16[32,64,128]{2,1,0:T(8,128)(2,1)S(1)} async-done(((bf16[32,64,128]{2,1,0:T(8,128)(2,1)}), bf16[32,64,128]{2,1,0:T(8,128)(2,1)S(1)}, u32[]{:S(2)}, u32[]{:S(2)}) %all-to-all-start.5) | async-done | bytes 524320 | tf_op jit(solution)/shard_map/all_to_all | solution.py:374
  270.2 0.8 copy-done.4
  271.0 4.9 %solve_one.1 = (f32[2,32,128]{2,1,0:T(8,128)}, bf16[32,1,32,128]{3,2,1,0:T(8,128)(2,1)}) custom-call(bf16[32,2,32,128]{3,2,1,0:T(8,128)(2,1)} %bitcast.34, bf16[16,5,128,256]{3,2,1,0:T(8,128)(2,1)} %bitcast.28, f32[32,32,128]{2,1,0:T(8,128)} %root_parts.1.keep_ref), custom_call_target="tpu_custom_call" | custom-call | tf_op jit(solution)/shard_map/solve_one/pallas_call | solution.py:320
  275.9 4.4 %all-to-all-start.6 = ((bf16[32,32,128]{2,1,0:T(8,128)(2,1)}), bf16[32,32,128]{2,1,0:T(8,128)(2,1)S(1)}, u32[]{:S(2)}, u32[]{:S(2)}) async-start(bf16[32,32,128]{2,1,0:T(8,128)(2,1)} %bitcast.38), calls=%async_computation.6 | async-start | bytes 524288 | tf_op jit(solution)/shard_map/all_to_all | solution.py:374
  280.3 11.0 %all-to-all-done.6 = bf16[32,32,128]{2,1,0:T(8,128)(2,1)S(1)} async-done(((bf16[32,32,128]{2,1,0:T(8,128)(2,1)}), bf16[32,32,128]{2,1,0:T(8,128)(2,1)S(1)}, u32[]{:S(2)}, u32[]{:S(2)}) %all-to-all-start.6) | async-done | bytes 262176 | tf_op jit(solution)/shard_map/all_to_all | solution.py:374
  291.4 15.4 %all_to_all.43 = bf16[32,32,128]{2,1,0:T(8,128)(2,1)} all-to-all(bf16[32,32,128]{2,1,0:T(8,128)(2,1)S(1)} %bitcast.25), channel_id=1, replica_groups=mesh['x'=4,'y'=8,'z'=8,'core'=2] {'x','y'}, dimensions={0} | all-to-all | bytes 524288 | tf_op jit(solution)/shard_map/all_to_all | solution.py:374
  306.7 2.4 solve_root.1
  309.1 1.4 pad_maximum_fusion
  (40 shorter events, 1.2 us)
Async XLA Ops:
  6.5 80.6 %all-gather.7.cloned.1.call-start = ((), (), s32[]{:S(2)}) async-start(), calls=%async_computation.8 | async-start | bytes 8912896 | tf_op jit(solution)/shard_map/all_gather | solution.py:409
  9.4 0.7 collective-permute-start
  11.7 26.2 %copy-start.9 = (s32[14,16,3]{1,0,2:T(8,128)S(1)}, s32[14,16,3]{1,0,2:T(8,128)}, u32[]{:S(2)}) copy-start(s32[14,16,3]{1,0,2:T(8,128)} %param.7) | copy-start | bytes 8068
  11.7 26.7 %copy-start = (bf16[14,3,256,128]{3,2,1,0:T(8,128)(2,1)S(1)}, bf16[14,3,256,128]{3,2,1,0:T(8,128)(2,1)}, u32[]{:S(2)}) copy-start(bf16[14,3,256,128]{3,2,1,0:T(8,128)(2,1)} %p_ref.3) | copy-start | bytes 8257540
  11.7 75.5 %all-to-all-start = ((bf16[32,128,256]{2,1,0:T(8,128)(2,1)}), bf16[32,128,256]{2,1,0:T(8,128)(2,1)}, u32[]{:S(2)}, u32[]{:S(2)}) async-start(bf16[32,128,256]{2,1,0:T(8,128)(2,1)} %broadcast_in_dim.17), calls=%async_computation | async-start | bytes 4194304 | tf_op jit(solution)/shard_map/all_to_all | solution.py:374
  37.9 185.8 %all-gather.9.cloned.1.call-start = ((), (), s32[]{:S(2)}) async-start(), calls=%async_computation.9 | async-start | bytes 13369344 | tf_op jit(solution)/shard_map/all_gather | solution.py:426
  38.4 6.3 %copy-start.3 = (s32[676]{0:T(1024)}, s32[676]{0:T(1024)S(1)}, u32[]{:S(2)}) copy-start(s32[676]{0:T(1024)S(1)} %concatenate.6.meta_ref) | copy-start | bytes 8116
  38.4 6.3 %copy-start.2 = (bf16[15,128,256]{2,1,0:T(8,128)(2,1)S(1)}, bf16[15,128,256]{2,1,0:T(8,128)(2,1)}, u32[]{:S(2)}) copy-start(bf16[15,128,256]{2,1,0:T(8,128)(2,1)} %d_ref) | copy-start | bytes 2949124
  39.4 7.1 %copy-start.1 = (bf16[12,256,256]{2,1,0:T(8,128)(2,1)}, bf16[12,256,256]{2,1,0:T(8,128)(2,1)S(1)}, u32[]{:S(2)}) copy-start(bf16[12,256,256]{2,1,0:T(8,128)(2,1)S(1)} %select_leaves.1.a_ref) | copy-start | bytes 4718596
  39.4 7.1 %collective-permute-start.1 = (bf16[12,256,256]{2,1,0:T(8,128)(2,1)S(1)}, bf16[12,256,256]{2,1,0:T(8,128)(2,1)}, u32[]{:S(2)}, u32[]{:S(2)}) collective-permute-start(bf16[12,256,256]{2,1,0:T(8,128)(2,1)S(1)} %select_leaves.1.a_ref), channel_id=1, source_target_pairs={{0,1},{1,0},{2,3},{3,2},{4,5},{5,4},{6,7},{7,6},{8,9},{9,8},{10,11... | collective-permute-start | bytes 4718600 | tf_op jit(solution)/shard_map/ppermute | solution.py:398
  42.3 4.2 %collective-permute-start.2 = (f32[7,16,256]{2,1,0:T(8,128)S(1)}, f32[7,16,256]{2,1,0:T(8,128)S(1)}, u32[]{:S(2)}, u32[]{:S(2)}) collective-permute-start(f32[7,16,256]{2,1,0:T(8,128)S(1)} %slice.20), channel_id=1, source_target_pairs={{0,1},{1,0},{2,3},{3,2},{4,5},{5,4},{6,7},{7,6},{8,9},{9,8},{10,11... | collective-permute-start | bytes 344072 | tf_op jit(solution)/shard_map/ppermute | solution.py:398
  46.5 46.0 %copy-start.7 = (f32[7,16,256]{2,1,0:T(8,128)}, f32[7,16,256]{2,1,0:T(8,128)S(1)}, u32[]{:S(2)}) copy-start(f32[7,16,256]{2,1,0:T(8,128)S(1)} %collective-permute-done.2.rg_ref) | copy-start | bytes 344068
  117.8 138.2 %all-gather.11.cloned.1.call-start = ((), (), s32[]{:S(2)}) async-start(), calls=%async_computation.10 | async-start | bytes 5570560 | tf_op jit(solution)/shard_map/all_gather | solution.py:427
  175.8 0.7 collective-permute-start.3
  230.4 20.0 %all-to-all-start.4 = ((bf16[32,64,128]{2,1,0:T(8,128)(2,1)}), bf16[32,64,128]{2,1,0:T(8,128)(2,1)S(1)}, u32[]{:S(2)}, u32[]{:S(2)}) async-start(bf16[32,64,128]{2,1,0:T(8,128)(2,1)} %bitcast.36), calls=%async_computation.4 | async-start | bytes 1048576 | tf_op jit(solution)/shard_map/all_to_all | solution.py:374
  251.3 18.9 %all-to-all-start.5 = ((bf16[32,64,128]{2,1,0:T(8,128)(2,1)}), bf16[32,64,128]{2,1,0:T(8,128)(2,1)S(1)}, u32[]{:S(2)}, u32[]{:S(2)}) async-start(bf16[32,64,128]{2,1,0:T(8,128)(2,1)} %bitcast.15), calls=%async_computation.5 | async-start | bytes 1048576 | tf_op jit(solution)/shard_map/all_to_all | solution.py:374
  270.2 0.8 copy-start.4
  275.9 15.4 %all-to-all-start.6 = ((bf16[32,32,128]{2,1,0:T(8,128)(2,1)}), bf16[32,32,128]{2,1,0:T(8,128)(2,1)S(1)}, u32[]{:S(2)}, u32[]{:S(2)}) async-start(bf16[32,32,128]{2,1,0:T(8,128)(2,1)} %bitcast.38), calls=%async_computation.6 | async-start | bytes 524288 | tf_op jit(solution)/shard_map/all_to_all | solution.py:374
  306.7 2.4 copy-start.5
  306.7 2.4 copy-start.6
  306.7 2.4 copy-start.8
Sparse Core Ops, SparseCore 0:
  9.5 63.9 all-gather.6
  117.9 76.2 all-gather.8
  196.3 44.5 all-gather.10

commit v12 on v11

--- a/solution.py
+++ b/solution.py
@@ -141,27 +141,23 @@
 
 
 def update_from_leaves(meta, solved, blocks, blocks_got, right, right_got):
-    def kernel(meta_ref, x_ref, a_ref, b_hbm, r_ref, rg_ref, o_ref, b_ref, sem):
+    def kernel(meta_ref, x_ref, a_ref, b_ref, r_ref, rg_ref, o_ref):
         core, row = meta_ref[1], meta_ref[2]
-        copy = pltpu.make_async_copy(b_hbm, b_ref, sem.at[0])
-        copy.start()
         joined = {}
         for s in range(0, 8, 2):
             joined[s] = jnp.concatenate(
                 [x_ref[:, s].reshape(256, 128), x_ref[:, s + 1].reshape(256, 128)], axis=1
             )
-        for column, block_ref in ((core, a_ref), (1 - core, b_ref)):
-            if block_ref is b_ref:
-                copy.wait()
-            place = 0
-            for t, firsts in enumerate(LEAF_PAIRS):
+        place = 0
+        for t, firsts in enumerate(LEAF_PAIRS):
+            for column, block_ref in ((core, a_ref), (1 - core, b_ref)):
                 acc = jnp.zeros((256, 256), F32)
-                for s in firsts:
-                    acc = acc + dot_t(joined[s], block_ref[place])
-                    place += 1
+                for i, s in enumerate(firsts):
+                    acc = acc + dot_t(joined[s], block_ref[place + i])
                 for half in range(2):
                     value = acc[:, 128 * half : 128 * half + 128].astype(BF16)
                     o_ref[:, pl.ds(column, 1), half, t] = value.reshape(8, 1, 32, 128)
+            place += len(firsts)
         z = row // 4
         start = pl.multiple_of(16 * (row % 2), 16)
 
@@ -181,14 +177,10 @@
 
     return pl.pallas_call(
         kernel,
-        in_specs=[SMEM, VMEM, VMEM, HBM, VMEM, VMEM],
+        in_specs=[SMEM, VMEM, VMEM, VMEM, VMEM, VMEM],
         out_specs=VMEM,
         out_shape=jax.ShapeDtypeStruct((8, 2, 2, 7, 32, 128), BF16),
-        scratch_shapes=[
-            pltpu.VMEM((12, 256, 256), BF16),
-            pltpu.SemaphoreType.DMA((1,)),
-        ],
-        compiler_params=params(0, STREAM_LIMIT),
+        compiler_params=params(0),
         name="update_from_leaves",
     )(meta, solved, blocks, blocks_got, right, right_got)
 

time: 318 us -> 316 us (level)
  Pallas kernels: 33 us -> 29.8 us
    pallas_call x1, Pallas kernels: 4.98 us -> 1.77 us  [update_from_leaves(): pl.pallas_call(kernel, in_specs=[SMEM, VMEM, VMEM, VMEM, VMEM, VMEM], out...]
  transfers between devices with their start and end apart: 11 -> 11, of which waited for: 4 -> 4; matrix products, arithmetic and copies ran while one was open for 1% -> 1% of each run, Pallas kernels for 6% -> 5%
where the time goes in v12:
time: 316 us; the launch traced here: 315 us
  blocking collectives  139 us (44%)
  waiting for transfers between devices  76.5 us (24%)
  starting transfers between devices  46.1 us (15%)
  Pallas kernels  29.8 us (9%)
  between operations  13.4 us (4%)
  local copies, waits for them, and re-layouts  8.49 us (3%)
    all_to_all x4, blocking collectives, exchange(): return lax.all_to_all(flat, axes, 0, 0, tiled=True).reshape(shape)  139 us
    all_to_all x4, waiting for transfers between devices, exchange(): return lax.all_to_all(flat, axes, 0, 0, tiled=True).reshape(shape)  75.7 us
    all_to_all x4, starting transfers between devices, exchange(): return lax.all_to_all(flat, axes, 0, 0, tiled=True).reshape(shape)  40.4 us
    pallas_call x1, Pallas kernels, solve_two(): pl.pallas_call(kernel, in_specs=[VMEM, HBM], out_specs=[VMEM, VMEM], out_...  6.72 us
  transfers between devices with their start and end apart: 11, of which 4 were waited for; matrix products, arithmetic and copies ran while one was open for 1% of the time, Pallas kernels for 5%

profile of v12, /device:TPU:8, one launch (start us, length us, event | category | flops | bytes accessed | tf_op | source)
XLA Modules:
  0.0 315.1 jit_solution(3864448161193318195)
XLA Ops:
  6.5 0.9 slice.30
  7.5 1.9 slice.21
  9.4 0.7 collective-permute-start
  10.1 1.6 broadcast_in_dim.17
  11.7 26.2 %all-to-all-start = ((bf16[32,128,256]{2,1,0:T(8,128)(2,1)}), bf16[32,128,256]{2,1,0:T(8,128)(2,1)}, u32[]{:S(2)}, u32[]{:S(2)}) async-start(bf16[32,128,256]{2,1,0:T(8,128)(2,1)} %broadcast_in_dim.17), calls=%async_computation | async-start | bytes 4194304 | tf_op jit(solution)/shard_map/all_to_all | solution.py:366
  38.4 1.0 select_leaves.1.a_ref
  39.4 1.9 collective-permute-start.1
  41.4 2.4 collective-permute-start.2
  43.8 1.8 stack_weights.1
  45.6 1.1 copy-done.4
  46.8 40.4 %all-to-all-done = bf16[32,128,256]{2,1,0:T(8,128)(2,1)} async-done(((bf16[32,128,256]{2,1,0:T(8,128)(2,1)}), bf16[32,128,256]{2,1,0:T(8,128)(2,1)}, u32[]{:S(2)}, u32[]{:S(2)}) %all-to-all-start) | async-done | bytes 2097184 | tf_op jit(solution)/shard_map/all_to_all | solution.py:366
  87.2 5.4 %solve_leaves.1 = (f32[8,32,128]{2,1,0:T(8,128)}, bf16[8,8,32,128]{3,2,1,0:T(8,128)(2,1)}) custom-call(bf16[32,8,16,256]{3,2,1,0:T(8,128)(2,1)} %bitcast.1.b_hbm, bf16[16,8,128,256]{3,2,1,0:T(8,128)(2,1)} %bitcast.32), custom_call_target="tpu_custom_call" | custom-call | tf_op jit(solution)/shard_map/solve_leaves/pallas_call | solution.py:102
  92.5 25.3 %all_to_all.40 = bf16[8,256,128]{2,1,0:T(8,128)(2,1)S(1)} all-to-all(bf16[8,256,128]{2,1,0:T(8,128)(2,1)} %bitcast.37), channel_id=1, replica_groups=mesh['x'=4,'y'=8,'z'=8,'core'=2] {'z'}, dimensions={0} | all-to-all | bytes 1048576 | tf_op jit(solution)/shard_map/all_to_all | solution.py:366
  117.9 0.7 all-gather.11.cloned.1.call-update
  118.7 1.4 copy-done.5
  120.1 1.8 update_from_leaves.1
  121.8 51.7 %all_to_all.41 = bf16[32,224,128]{2,1,0:T(8,128)(2,1)S(1)} all-to-all(bf16[32,224,128]{2,1,0:T(8,128)(2,1)S(1)} %bitcast.22), channel_id=1, replica_groups=mesh['x'=4,'y'=8,'z'=8,'core'=2] {'x','y'}, dimensions={0} | all-to-all | bytes 3670016 | tf_op jit(solution)/shard_map/all_to_all | solution.py:366
  174.7 47.0 %all_to_all.42 = bf16[32,128,128]{2,1,0:T(8,128)(2,1)} all-to-all(bf16[32,128,128]{2,1,0:T(8,128)(2,1)S(1)} %broadcast_in_dim.19), channel_id=1, replica_groups=mesh['x'=4,'y'=8,'z'=8,'core'=2] {'x','y'}, dimensions={0} | all-to-all | bytes 2097152 | tf_op jit(solution)/shard_map/all_to_all | solution.py:366
  221.7 6.7 %solve_two.1 = (f32[4,32,128]{2,1,0:T(8,128)}, bf16[32,2,32,128]{3,2,1,0:T(8,128)(2,1)}) custom-call(bf16[32,4,32,128]{3,2,1,0:T(8,128)(2,1)} %bitcast.33, bf16[16,12,128,256]{3,2,1,0:T(8,128)(2,1)} %bitcast.28), custom_call_target="tpu_custom_call" | custom-call | tf_op jit(solution)/shard_map/solve_two/pallas_call | solution.py:250
  228.4 5.1 %all-to-all-start.4 = ((bf16[32,64,128]{2,1,0:T(8,128)(2,1)}), bf16[32,64,128]{2,1,0:T(8,128)(2,1)S(1)}, u32[]{:S(2)}, u32[]{:S(2)}) async-start(bf16[32,64,128]{2,1,0:T(8,128)(2,1)} %bitcast.36), calls=%async_computation.4 | async-start | bytes 1048576 | tf_op jit(solution)/shard_map/all_to_all | solution.py:366
  233.5 4.7 %root_parts.1.keep_ref = f32[32,32,128]{2,1,0:T(8,128)} custom-call(f32[4,32,128]{2,1,0:T(8,128)} %get-tuple-element.40.s_ref, bf16[16,12,128,256]{3,2,1,0:T(8,128)(2,1)} %bitcast.29), custom_call_target="tpu_custom_call" | custom-call | tf_op jit(solution)/shard_map/root_parts/pallas_call | solution.py:288
  238.3 10.1 %all-to-all-done.4 = bf16[32,64,128]{2,1,0:T(8,128)(2,1)S(1)} async-done(((bf16[32,64,128]{2,1,0:T(8,128)(2,1)}), bf16[32,64,128]{2,1,0:T(8,128)(2,1)S(1)}, u32[]{:S(2)}, u32[]{:S(2)}) %all-to-all-start.4) | async-done | bytes 524320 | tf_op jit(solution)/shard_map/all_to_all | solution.py:366
  248.4 0.9 next_residual.2
  249.3 4.7 %all-to-all-start.5 = ((bf16[32,64,128]{2,1,0:T(8,128)(2,1)}), bf16[32,64,128]{2,1,0:T(8,128)(2,1)S(1)}, u32[]{:S(2)}, u32[]{:S(2)}) async-start(bf16[32,64,128]{2,1,0:T(8,128)(2,1)} %bitcast.15), calls=%async_computation.5 | async-start | bytes 1048576 | tf_op jit(solution)/shard_map/all_to_all | solution.py:366
  254.0 14.3 %all-to-all-done.5 = bf16[32,64,128]{2,1,0:T(8,128)(2,1)S(1)} async-done(((bf16[32,64,128]{2,1,0:T(8,128)(2,1)}), bf16[32,64,128]{2,1,0:T(8,128)(2,1)S(1)}, u32[]{:S(2)}, u32[]{:S(2)}) %all-to-all-start.5) | async-done | bytes 524320 | tf_op jit(solution)/shard_map/all_to_all | solution.py:366
  268.2 0.8 copy-done.7
  269.0 4.9 %solve_one.1 = (f32[2,32,128]{2,1,0:T(8,128)}, bf16[32,1,32,128]{3,2,1,0:T(8,128)(2,1)}) custom-call(bf16[32,2,32,128]{3,2,1,0:T(8,128)(2,1)} %bitcast.34, bf16[16,5,128,256]{3,2,1,0:T(8,128)(2,1)} %bitcast.30, f32[32,32,128]{2,1,0:T(8,128)} %root_parts.1.keep_ref), custom_call_target="tpu_custom_call" | custom-call | tf_op jit(solution)/shard_map/solve_one/pallas_call | solution.py:312
  273.9 4.4 %all-to-all-start.6 = ((bf16[32,32,128]{2,1,0:T(8,128)(2,1)}), bf16[32,32,128]{2,1,0:T(8,128)(2,1)S(1)}, u32[]{:S(2)}, u32[]{:S(2)}) async-start(bf16[32,32,128]{2,1,0:T(8,128)(2,1)} %bitcast.38), calls=%async_computation.6 | async-start | bytes 524288 | tf_op jit(solution)/shard_map/all_to_all | solution.py:366
  278.3 11.0 %all-to-all-done.6 = bf16[32,32,128]{2,1,0:T(8,128)(2,1)S(1)} async-done(((bf16[32,32,128]{2,1,0:T(8,128)(2,1)}), bf16[32,32,128]{2,1,0:T(8,128)(2,1)S(1)}, u32[]{:S(2)}, u32[]{:S(2)}) %all-to-all-start.6) | async-done | bytes 262176 | tf_op jit(solution)/shard_map/all_to_all | solution.py:366
  289.4 15.4 %all_to_all.43 = bf16[32,32,128]{2,1,0:T(8,128)(2,1)} all-to-all(bf16[32,32,128]{2,1,0:T(8,128)(2,1)S(1)} %bitcast.27), channel_id=1, replica_groups=mesh['x'=4,'y'=8,'z'=8,'core'=2] {'x','y'}, dimensions={0} | all-to-all | bytes 524288 | tf_op jit(solution)/shard_map/all_to_all | solution.py:366
  304.7 2.4 solve_root.1
  307.1 1.4 pad_maximum_fusion
  (44 shorter events, 1.8 us)
Async XLA Ops:
  6.5 80.6 %all-gather.7.cloned.1.call-start = ((), (), s32[]{:S(2)}) async-start(), calls=%async_computation.8 | async-start | bytes 8912896 | tf_op jit(solution)/shard_map/all_gather | solution.py:401
  9.4 0.7 collective-permute-start
  11.7 26.2 %copy-start.11 = (s32[14,16,3]{1,0,2:T(8,128)S(1)}, s32[14,16,3]{1,0,2:T(8,128)}, u32[]{:S(2)}) copy-start(s32[14,16,3]{1,0,2:T(8,128)} %param.7) | copy-start | bytes 8068
  11.7 26.7 %copy-start = (bf16[14,3,256,128]{3,2,1,0:T(8,128)(2,1)S(1)}, bf16[14,3,256,128]{3,2,1,0:T(8,128)(2,1)}, u32[]{:S(2)}) copy-start(bf16[14,3,256,128]{3,2,1,0:T(8,128)(2,1)} %p_ref.3) | copy-start | bytes 8257540
  11.7 75.5 %all-to-all-start = ((bf16[32,128,256]{2,1,0:T(8,128)(2,1)}), bf16[32,128,256]{2,1,0:T(8,128)(2,1)}, u32[]{:S(2)}, u32[]{:S(2)}) async-start(bf16[32,128,256]{2,1,0:T(8,128)(2,1)} %broadcast_in_dim.17), calls=%async_computation | async-start | bytes 4194304 | tf_op jit(solution)/shard_map/all_to_all | solution.py:366
  37.9 183.8 %all-gather.9.cloned.1.call-start = ((), (), s32[]{:S(2)}) async-start(), calls=%async_computation.9 | async-start | bytes 13369344 | tf_op jit(solution)/shard_map/all_gather | solution.py:418
  38.4 3.0 copy-start.6
  38.4 5.4 %copy-start.3 = (bf16[15,128,256]{2,1,0:T(8,128)(2,1)S(1)}, bf16[15,128,256]{2,1,0:T(8,128)(2,1)}, u32[]{:S(2)}) copy-start(bf16[15,128,256]{2,1,0:T(8,128)(2,1)} %d_ref) | copy-start | bytes 2949124
  39.4 6.2 %copy-start.1 = (bf16[12,256,256]{2,1,0:T(8,128)(2,1)}, bf16[12,256,256]{2,1,0:T(8,128)(2,1)S(1)}, u32[]{:S(2)}) copy-start(bf16[12,256,256]{2,1,0:T(8,128)(2,1)S(1)} %select_leaves.1.a_ref) | copy-start | bytes 4718596
  39.4 6.2 %collective-permute-start.1 = (bf16[12,256,256]{2,1,0:T(8,128)(2,1)S(1)}, bf16[12,256,256]{2,1,0:T(8,128)(2,1)S(1)}, u32[]{:S(2)}, u32[]{:S(2)}) collective-permute-start(bf16[12,256,256]{2,1,0:T(8,128)(2,1)S(1)} %select_leaves.1.a_ref), channel_id=1, source_target_pairs={{0,1},{1,0},{2,3},{3,2},{4,5},{5,4},{6,7},{7,6},{8,9},{9,8},{10,11... | collective-permute-start | bytes 4718600 | tf_op jit(solution)/shard_map/ppermute | solution.py:390
  41.4 4.2 %collective-permute-start.2 = (f32[7,16,256]{2,1,0:T(8,128)S(1)}, f32[7,16,256]{2,1,0:T(8,128)S(1)}, u32[]{:S(2)}, u32[]{:S(2)}) collective-permute-start(f32[7,16,256]{2,1,0:T(8,128)S(1)} %slice.20), channel_id=1, source_target_pairs={{0,1},{1,0},{2,3},{3,2},{4,5},{5,4},{6,7},{7,6},{8,9},{9,8},{10,11... | collective-permute-start | bytes 344072 | tf_op jit(solution)/shard_map/ppermute | solution.py:390
  45.6 1.1 copy-start.4
  92.5 26.1 %copy-start.2 = (bf16[12,256,256]{2,1,0:T(8,128)(2,1)S(1)}, bf16[12,256,256]{2,1,0:T(8,128)(2,1)}, u32[]{:S(2)}) copy-start(bf16[12,256,256]{2,1,0:T(8,128)(2,1)} %copy-done.1) | copy-start | bytes 4718596
  117.9 136.1 %all-gather.11.cloned.1.call-start = ((), (), s32[]{:S(2)}) async-start(), calls=%async_computation.10 | async-start | bytes 5570560 | tf_op jit(solution)/shard_map/all_gather | solution.py:419
  118.6 1.4 copy-start.5
  173.7 0.7 collective-permute-start.3
  228.4 20.0 %all-to-all-start.4 = ((bf16[32,64,128]{2,1,0:T(8,128)(2,1)}), bf16[32,64,128]{2,1,0:T(8,128)(2,1)S(1)}, u32[]{:S(2)}, u32[]{:S(2)}) async-start(bf16[32,64,128]{2,1,0:T(8,128)(2,1)} %bitcast.36), calls=%async_computation.4 | async-start | bytes 1048576 | tf_op jit(solution)/shard_map/all_to_all | solution.py:366
  249.3 18.9 %all-to-all-start.5 = ((bf16[32,64,128]{2,1,0:T(8,128)(2,1)}), bf16[32,64,128]{2,1,0:T(8,128)(2,1)S(1)}, u32[]{:S(2)}, u32[]{:S(2)}) async-start(bf16[32,64,128]{2,1,0:T(8,128)(2,1)} %bitcast.15), calls=%async_computation.5 | async-start | bytes 1048576 | tf_op jit(solution)/shard_map/all_to_all | solution.py:366
  268.2 0.8 copy-start.7
  273.9 15.4 %all-to-all-start.6 = ((bf16[32,32,128]{2,1,0:T(8,128)(2,1)}), bf16[32,32,128]{2,1,0:T(8,128)(2,1)S(1)}, u32[]{:S(2)}, u32[]{:S(2)}) async-start(bf16[32,32,128]{2,1,0:T(8,128)(2,1)} %bitcast.38), calls=%async_computation.6 | async-start | bytes 524288 | tf_op jit(solution)/shard_map/all_to_all | solution.py:366
  304.7 2.4 copy-start.8
  304.7 2.4 copy-start.9
  304.7 2.4 copy-start.10
Sparse Core Ops, SparseCore 0:
  9.5 63.9 all-gather.6
  118.0 76.0 all-gather.8
  196.3 44.5 all-gather.10

commit v13 on v12

--- a/solution.py
+++ b/solution.py
@@ -326,19 +326,28 @@
     )(residual, weights, keep)
 
 
-def solve_root(residual, weights):
-    def kernel(x_ref, d_ref, s_ref):
-        s_ref[0] = solve_node(x_ref, d_ref, 0, 0)
+def solve_root(residual, weights, leaves, two, one):
+    def kernel(x_ref, d_ref, leaves_ref, two_ref, one_ref, s_ref):
+        s_ref[:8] = leaves_ref[...]
+        s_ref[8:12] = two_ref[...]
+        s_ref[12:14] = one_ref[...]
+        s_ref[14] = solve_node(x_ref, d_ref, 0, 0)
 
     return pl.pallas_call(
         kernel,
         grid=(1,),
-        in_specs=[VMEM, pl.BlockSpec((NC, 1, 128, 256), lambda i: (0, 2, 0, 0))],
-        out_specs=VMEM,
-        out_shape=jax.ShapeDtypeStruct((1, 32, 128), F32),
+        in_specs=[
+            VMEM,
+            pl.BlockSpec((NC, 1, 128, 256), lambda i: (0, 2, 0, 0)),
+            VMEM,
+            VMEM,
+            VMEM,
+        ],
+        out_specs=VMEM,
+        out_shape=jax.ShapeDtypeStruct((15, 32, 128), F32),
         compiler_params=params(1, STREAM_LIMIT),
         name="solve_root",
-    )(residual, weights)
+    )(residual, weights, leaves, two, one)
 
 
 def next_residual(parts, rest):
@@ -427,8 +436,7 @@
     spread = exchange(next_residual(parts, residual[4:6]), ROW)
     one, parts = solve_one(spread, weights_one, keep)
     spread = exchange(next_residual(exchange(parts, ROW), residual[6:]), ROW)
-    root = solve_root(spread, weights_one)
-    return jnp.concatenate([leaves, two, one, root], axis=0)
+    return solve_root(spread, weights_one, leaves, two, one)
 
 
 def solution(mesh):

time: 316 us -> 315 us (level)
  no operation moved by 1% of the time
where the time goes in v13:
time: 315 us; the launch traced here: 314 us
  blocking collectives  139 us (44%)
  waiting for transfers between devices  76.4 us (24%)
  starting transfers between devices  46.1 us (15%)
  Pallas kernels  30 us (10%)
  between operations  13.4 us (4%)
  local copies, waits for them, and re-layouts  8.46 us (3%)
    all_to_all x4, blocking collectives, exchange(): return lax.all_to_all(flat, axes, 0, 0, tiled=True).reshape(shape)  139 us
    all_to_all x4, waiting for transfers between devices, exchange(): return lax.all_to_all(flat, axes, 0, 0, tiled=True).reshape(shape)  75.7 us
    all_to_all x4, starting transfers between devices, exchange(): return lax.all_to_all(flat, axes, 0, 0, tiled=True).reshape(shape)  40.3 us
    pallas_call x1, Pallas kernels, solve_two(): pl.pallas_call(kernel, in_specs=[VMEM, HBM], out_specs=[VMEM, VMEM], out_...  6.72 us
  transfers between devices with their start and end apart: 11, of which 4 were waited for; matrix products, arithmetic and copies ran while one was open for 1% of the time, Pallas kernels for 5%

profile of v13, /device:TPU:8, one launch (start us, length us, event | category | flops | bytes accessed | tf_op | source)
XLA Modules:
  0.0 313.7 jit_solution(13148038120211642957)
XLA Ops:
  6.5 0.9 slice.30
  7.5 1.9 slice.21
  9.4 0.7 collective-permute-start
  10.1 1.6 broadcast_in_dim.17
  11.7 26.2 %all-to-all-start = ((bf16[32,128,256]{2,1,0:T(8,128)(2,1)}), bf16[32,128,256]{2,1,0:T(8,128)(2,1)}, u32[]{:S(2)}, u32[]{:S(2)}) async-start(bf16[32,128,256]{2,1,0:T(8,128)(2,1)} %broadcast_in_dim.17), calls=%async_computation | async-start | bytes 4194304 | tf_op jit(solution)/shard_map/all_to_all | solution.py:375
  38.4 1.0 select_leaves.1.a_ref
  39.4 1.9 collective-permute-start.1
  41.4 2.4 collective-permute-start.2
  43.8 1.8 stack_weights.1
  45.6 1.1 copy-done.4
  46.8 40.4 %all-to-all-done = bf16[32,128,256]{2,1,0:T(8,128)(2,1)} async-done(((bf16[32,128,256]{2,1,0:T(8,128)(2,1)}), bf16[32,128,256]{2,1,0:T(8,128)(2,1)}, u32[]{:S(2)}, u32[]{:S(2)}) %all-to-all-start) | async-done | bytes 2097184 | tf_op jit(solution)/shard_map/all_to_all | solution.py:375
  87.2 5.4 %solve_leaves.1 = (f32[8,32,128]{2,1,0:T(8,128)}, bf16[8,8,32,128]{3,2,1,0:T(8,128)(2,1)}) custom-call(bf16[32,8,16,256]{3,2,1,0:T(8,128)(2,1)} %bitcast.4.b_hbm, bf16[16,8,128,256]{3,2,1,0:T(8,128)(2,1)} %bitcast.32), custom_call_target="tpu_custom_call" | custom-call | tf_op jit(solution)/shard_map/solve_leaves/pallas_call | solution.py:102
  92.5 25.3 %all_to_all.40 = bf16[8,256,128]{2,1,0:T(8,128)(2,1)S(1)} all-to-all(bf16[8,256,128]{2,1,0:T(8,128)(2,1)} %bitcast.37), channel_id=1, replica_groups=mesh['x'=4,'y'=8,'z'=8,'core'=2] {'z'}, dimensions={0} | all-to-all | bytes 1048576 | tf_op jit(solution)/shard_map/all_to_all | solution.py:375
  117.9 0.7 all-gather.11.cloned.1.call-update
  118.6 1.4 copy-done.5
  120.0 1.8 update_from_leaves.1
  121.7 51.8 %all_to_all.41 = bf16[32,224,128]{2,1,0:T(8,128)(2,1)S(1)} all-to-all(bf16[32,224,128]{2,1,0:T(8,128)(2,1)S(1)} %bitcast.22), channel_id=1, replica_groups=mesh['x'=4,'y'=8,'z'=8,'core'=2] {'x','y'}, dimensions={0} | all-to-all | bytes 3670016 | tf_op jit(solution)/shard_map/all_to_all | solution.py:375
  173.8 0.7 collective-permute-start.3
  174.7 47.0 %all_to_all.42 = bf16[32,128,128]{2,1,0:T(8,128)(2,1)} all-to-all(bf16[32,128,128]{2,1,0:T(8,128)(2,1)S(1)} %broadcast_in_dim.19), channel_id=1, replica_groups=mesh['x'=4,'y'=8,'z'=8,'core'=2] {'x','y'}, dimensions={0} | all-to-all | bytes 2097152 | tf_op jit(solution)/shard_map/all_to_all | solution.py:375
  221.7 6.7 %solve_two.1 = (f32[4,32,128]{2,1,0:T(8,128)}, bf16[32,2,32,128]{3,2,1,0:T(8,128)(2,1)}) custom-call(bf16[32,4,32,128]{3,2,1,0:T(8,128)(2,1)} %bitcast.33, bf16[16,12,128,256]{3,2,1,0:T(8,128)(2,1)} %bitcast.28), custom_call_target="tpu_custom_call" | custom-call | tf_op jit(solution)/shard_map/solve_two/pallas_call | solution.py:250
  228.4 5.1 %all-to-all-start.4 = ((bf16[32,64,128]{2,1,0:T(8,128)(2,1)}), bf16[32,64,128]{2,1,0:T(8,128)(2,1)S(1)}, u32[]{:S(2)}, u32[]{:S(2)}) async-start(bf16[32,64,128]{2,1,0:T(8,128)(2,1)} %bitcast.36), calls=%async_computation.4 | async-start | bytes 1048576 | tf_op jit(solution)/shard_map/all_to_all | solution.py:375
  233.6 4.8 %root_parts.1.keep_ref = f32[32,32,128]{2,1,0:T(8,128)} custom-call(f32[4,32,128]{2,1,0:T(8,128)} %get-tuple-element.40.s_ref.two_ref, bf16[16,12,128,256]{3,2,1,0:T(8,128)(2,1)} %bitcast.29), custom_call_target="tpu_custom_call" | custom-call | tf_op jit(solution)/shard_map/root_parts/pallas_call | solution.py:288
  238.4 10.1 %all-to-all-done.4 = bf16[32,64,128]{2,1,0:T(8,128)(2,1)S(1)} async-done(((bf16[32,64,128]{2,1,0:T(8,128)(2,1)}), bf16[32,64,128]{2,1,0:T(8,128)(2,1)S(1)}, u32[]{:S(2)}, u32[]{:S(2)}) %all-to-all-start.4) | async-done | bytes 524320 | tf_op jit(solution)/shard_map/all_to_all | solution.py:375
  248.4 0.9 next_residual.2
  249.3 4.6 %all-to-all-start.5 = ((bf16[32,64,128]{2,1,0:T(8,128)(2,1)}), bf16[32,64,128]{2,1,0:T(8,128)(2,1)S(1)}, u32[]{:S(2)}, u32[]{:S(2)}) async-start(bf16[32,64,128]{2,1,0:T(8,128)(2,1)} %bitcast.15), calls=%async_computation.5 | async-start | bytes 1048576 | tf_op jit(solution)/shard_map/all_to_all | solution.py:375
  254.0 14.2 %all-to-all-done.5 = bf16[32,64,128]{2,1,0:T(8,128)(2,1)S(1)} async-done(((bf16[32,64,128]{2,1,0:T(8,128)(2,1)}), bf16[32,64,128]{2,1,0:T(8,128)(2,1)S(1)}, u32[]{:S(2)}, u32[]{:S(2)}) %all-to-all-start.5) | async-done | bytes 524320 | tf_op jit(solution)/shard_map/all_to_all | solution.py:375
  268.2 0.8 copy-done.7
  269.0 4.9 %solve_one.1 = (f32[2,32,128]{2,1,0:T(8,128)}, bf16[32,1,32,128]{3,2,1,0:T(8,128)(2,1)}) custom-call(bf16[32,2,32,128]{3,2,1,0:T(8,128)(2,1)} %bitcast.34, bf16[16,5,128,256]{3,2,1,0:T(8,128)(2,1)} %bitcast.30, f32[32,32,128]{2,1,0:T(8,128)} %root_parts.1.keep_ref), custom_call_target="tpu_custom_call" | custom-call | tf_op jit(solution)/shard_map/solve_one/pallas_call | solution.py:312
  273.9 4.4 %all-to-all-start.6 = ((bf16[32,32,128]{2,1,0:T(8,128)(2,1)}), bf16[32,32,128]{2,1,0:T(8,128)(2,1)S(1)}, u32[]{:S(2)}, u32[]{:S(2)}) async-start(bf16[32,32,128]{2,1,0:T(8,128)(2,1)} %bitcast.38), calls=%async_computation.6 | async-start | bytes 524288 | tf_op jit(solution)/shard_map/all_to_all | solution.py:375
  278.3 11.0 %all-to-all-done.6 = bf16[32,32,128]{2,1,0:T(8,128)(2,1)S(1)} async-done(((bf16[32,32,128]{2,1,0:T(8,128)(2,1)}), bf16[32,32,128]{2,1,0:T(8,128)(2,1)S(1)}, u32[]{:S(2)}, u32[]{:S(2)}) %all-to-all-start.6) | async-done | bytes 262176 | tf_op jit(solution)/shard_map/all_to_all | solution.py:375
  289.4 15.4 %all_to_all.43 = bf16[32,32,128]{2,1,0:T(8,128)(2,1)} all-to-all(bf16[32,32,128]{2,1,0:T(8,128)(2,1)S(1)} %bitcast.27), channel_id=1, replica_groups=mesh['x'=4,'y'=8,'z'=8,'core'=2] {'x','y'}, dimensions={0} | all-to-all | bytes 524288 | tf_op jit(solution)/shard_map/all_to_all | solution.py:375
  304.7 2.5 solve_root.1
  (37 shorter events, 1.2 us)
Async XLA Ops:
  6.5 80.6 %all-gather.7.cloned.1.call-start = ((), (), s32[]{:S(2)}) async-start(), calls=%async_computation.8 | async-start | bytes 8912896 | tf_op jit(solution)/shard_map/all_gather | solution.py:410
  9.4 0.7 collective-permute-start
  11.7 26.2 %copy-start.8 = (s32[14,16,3]{1,0,2:T(8,128)S(1)}, s32[14,16,3]{1,0,2:T(8,128)}, u32[]{:S(2)}) copy-start(s32[14,16,3]{1,0,2:T(8,128)} %param.7) | copy-start | bytes 8068
  11.7 26.7 %copy-start = (bf16[14,3,256,128]{3,2,1,0:T(8,128)(2,1)S(1)}, bf16[14,3,256,128]{3,2,1,0:T(8,128)(2,1)}, u32[]{:S(2)}) copy-start(bf16[14,3,256,128]{3,2,1,0:T(8,128)(2,1)} %p_ref.3) | copy-start | bytes 8257540
  11.7 75.5 %all-to-all-start = ((bf16[32,128,256]{2,1,0:T(8,128)(2,1)}), bf16[32,128,256]{2,1,0:T(8,128)(2,1)}, u32[]{:S(2)}, u32[]{:S(2)}) async-start(bf16[32,128,256]{2,1,0:T(8,128)(2,1)} %broadcast_in_dim.17), calls=%async_computation | async-start | bytes 4194304 | tf_op jit(solution)/shard_map/all_to_all | solution.py:375
  37.9 183.9 %all-gather.9.cloned.1.call-start = ((), (), s32[]{:S(2)}) async-start(), calls=%async_computation.9 | async-start | bytes 13369344 | tf_op jit(solution)/shard_map/all_gather | solution.py:427
  38.4 3.0 copy-start.6
  38.4 5.4 %copy-start.3 = (bf16[15,128,256]{2,1,0:T(8,128)(2,1)S(1)}, bf16[15,128,256]{2,1,0:T(8,128)(2,1)}, u32[]{:S(2)}) copy-start(bf16[15,128,256]{2,1,0:T(8,128)(2,1)} %d_ref) | copy-start | bytes 2949124
  39.4 6.2 %copy-start.1 = (bf16[12,256,256]{2,1,0:T(8,128)(2,1)}, bf16[12,256,256]{2,1,0:T(8,128)(2,1)S(1)}, u32[]{:S(2)}) copy-start(bf16[12,256,256]{2,1,0:T(8,128)(2,1)S(1)} %select_leaves.1.a_ref) | copy-start | bytes 4718596
  39.4 6.2 %collective-permute-start.1 = (bf16[12,256,256]{2,1,0:T(8,128)(2,1)S(1)}, bf16[12,256,256]{2,1,0:T(8,128)(2,1)S(1)}, u32[]{:S(2)}, u32[]{:S(2)}) collective-permute-start(bf16[12,256,256]{2,1,0:T(8,128)(2,1)S(1)} %select_leaves.1.a_ref), channel_id=1, source_target_pairs={{0,1},{1,0},{2,3},{3,2},{4,5},{5,4},{6,7},{7,6},{8,9},{9,8},{10,11... | collective-permute-start | bytes 4718600 | tf_op jit(solution)/shard_map/ppermute | solution.py:399
  41.4 4.2 %collective-permute-start.2 = (f32[7,16,256]{2,1,0:T(8,128)S(1)}, f32[7,16,256]{2,1,0:T(8,128)S(1)}, u32[]{:S(2)}, u32[]{:S(2)}) collective-permute-start(f32[7,16,256]{2,1,0:T(8,128)S(1)} %slice.20), channel_id=1, source_target_pairs={{0,1},{1,0},{2,3},{3,2},{4,5},{5,4},{6,7},{7,6},{8,9},{9,8},{10,11... | collective-permute-start | bytes 344072 | tf_op jit(solution)/shard_map/ppermute | solution.py:399
  45.6 1.1 copy-start.4
  92.5 26.0 %copy-start.2 = (bf16[12,256,256]{2,1,0:T(8,128)(2,1)S(1)}, bf16[12,256,256]{2,1,0:T(8,128)(2,1)}, u32[]{:S(2)}) copy-start(bf16[12,256,256]{2,1,0:T(8,128)(2,1)} %copy-done.1) | copy-start | bytes 4718596
  117.8 136.2 %all-gather.11.cloned.1.call-start = ((), (), s32[]{:S(2)}) async-start(), calls=%async_computation.10 | async-start | bytes 5570560 | tf_op jit(solution)/shard_map/all_gather | solution.py:428
  118.6 1.4 copy-start.5
  173.8 0.7 collective-permute-start.3
  228.4 20.0 %all-to-all-start.4 = ((bf16[32,64,128]{2,1,0:T(8,128)(2,1)}), bf16[32,64,128]{2,1,0:T(8,128)(2,1)S(1)}, u32[]{:S(2)}, u32[]{:S(2)}) async-start(bf16[32,64,128]{2,1,0:T(8,128)(2,1)} %bitcast.36), calls=%async_computation.4 | async-start | bytes 1048576 | tf_op jit(solution)/shard_map/all_to_all | solution.py:375
  249.3 18.9 %all-to-all-start.5 = ((bf16[32,64,128]{2,1,0:T(8,128)(2,1)}), bf16[32,64,128]{2,1,0:T(8,128)(2,1)S(1)}, u32[]{:S(2)}, u32[]{:S(2)}) async-start(bf16[32,64,128]{2,1,0:T(8,128)(2,1)} %bitcast.15), calls=%async_computation.5 | async-start | bytes 1048576 | tf_op jit(solution)/shard_map/all_to_all | solution.py:375
  268.2 0.8 copy-start.7
  273.9 15.4 %all-to-all-start.6 = ((bf16[32,32,128]{2,1,0:T(8,128)(2,1)}), bf16[32,32,128]{2,1,0:T(8,128)(2,1)S(1)}, u32[]{:S(2)}, u32[]{:S(2)}) async-start(bf16[32,32,128]{2,1,0:T(8,128)(2,1)} %bitcast.38), calls=%async_computation.6 | async-start | bytes 524288 | tf_op jit(solution)/shard_map/all_to_all | solution.py:375
Sparse Core Ops, SparseCore 0:
  9.5 63.9 all-gather.6
  117.9 76.2 all-gather.8
  196.3 44.5 all-gather.10

commit v14 on v13

--- a/solution.py
+++ b/solution.py
@@ -407,6 +407,7 @@
         (right_sides[:8].astype(BF16), diag_inverse)
     )
     moved = to_owner(leaf_right)
+    moved, diag_inverse = lax.optimization_barrier((moved, diag_inverse))
     leaf_inverse = lax.all_gather(diag_inverse[:8], COL, axis=0)
 
     zero = jnp.zeros((), jnp.int32)

time: 315 us -> 318 us (level)
  transfers between devices with their start and end apart: 11 -> 11, of which waited for: 4 -> 5; matrix products, arithmetic and copies ran while one was open for 1% -> 1% of each run, Pallas kernels for 5% -> 5%
where the time goes in v14:
time: 318 us; the launch traced here: 317 us
  blocking collectives  140 us (44%)
  waiting for transfers between devices  78.7 us (25%)
  starting transfers between devices  46.6 us (15%)
  Pallas kernels  29.9 us (9%)
  between operations  13.4 us (4%)
  local copies, waits for them, and re-layouts  8.46 us (3%)
    all_to_all x4, blocking collectives, exchange(): return lax.all_to_all(flat, axes, 0, 0, tiled=True).reshape(shape)  140 us
    all_to_all x4, waiting for transfers between devices, exchange(): return lax.all_to_all(flat, axes, 0, 0, tiled=True).reshape(shape)  76.8 us
    all_to_all x4, starting transfers between devices, exchange(): return lax.all_to_all(flat, axes, 0, 0, tiled=True).reshape(shape)  40.8 us
    pallas_call x1, Pallas kernels, solve_two(): pl.pallas_call(kernel, in_specs=[VMEM, HBM], out_specs=[VMEM, VMEM], out_...  6.68 us
  transfers between devices with their start and end apart: 11, of which 5 were waited for; matrix products, arithmetic and copies ran while one was open for 1% of the time, Pallas kernels for 5%

profile of v14, /device:TPU:8, one launch (start us, length us, event | category | flops | bytes accessed | tf_op | source)
XLA Modules:
  0.0 316.8 jit_solution(14255402744056669016)
XLA Ops:
  6.5 0.9 slice.30
  7.5 0.7 collective-permute-start
  8.1 1.9 slice.21
  10.1 1.6 broadcast_in_dim.17
  11.7 26.2 %all-to-all-start = ((bf16[32,128,256]{2,1,0:T(8,128)(2,1)}), bf16[32,128,256]{2,1,0:T(8,128)(2,1)}, u32[]{:S(2)}, u32[]{:S(2)}) async-start(bf16[32,128,256]{2,1,0:T(8,128)(2,1)} %broadcast_in_dim.17), calls=%async_computation | async-start | bytes 4194304 | tf_op jit(solution)/shard_map/all_to_all | solution.py:375
  38.4 1.0 select_leaves.1.a_ref
  39.4 1.9 collective-permute-start.1
  41.4 2.4 collective-permute-start.2
  43.8 1.8 stack_weights.1
  45.6 1.1 copy-done.4
  46.8 40.4 %all-to-all-done = bf16[32,128,256]{2,1,0:T(8,128)(2,1)} async-done(((bf16[32,128,256]{2,1,0:T(8,128)(2,1)}), bf16[32,128,256]{2,1,0:T(8,128)(2,1)}, u32[]{:S(2)}, u32[]{:S(2)}) %all-to-all-start) | async-done | bytes 2097184 | tf_op jit(solution)/shard_map/all_to_all | solution.py:375
  87.2 1.1 all-gather.7.cloned.1.call-done
  88.3 5.4 %solve_leaves.1 = (f32[8,32,128]{2,1,0:T(8,128)}, bf16[8,8,32,128]{3,2,1,0:T(8,128)(2,1)}) custom-call(bf16[32,8,16,256]{3,2,1,0:T(8,128)(2,1)} %bitcast.4.b_hbm, bf16[16,8,128,256]{3,2,1,0:T(8,128)(2,1)} %bitcast.32), custom_call_target="tpu_custom_call" | custom-call | tf_op jit(solution)/shard_map/solve_leaves/pallas_call | solution.py:102
  93.7 24.1 %all_to_all.40 = bf16[8,256,128]{2,1,0:T(8,128)(2,1)S(1)} all-to-all(bf16[8,256,128]{2,1,0:T(8,128)(2,1)} %bitcast.37), channel_id=1, replica_groups=mesh['x'=4,'y'=8,'z'=8,'core'=2] {'z'}, dimensions={0} | all-to-all | bytes 1048576 | tf_op jit(solution)/shard_map/all_to_all | solution.py:375
  117.8 0.7 all-gather.11.cloned.1.call-update
  118.5 1.4 copy-done.5
  119.9 1.8 update_from_leaves.1
  121.7 52.8 %all_to_all.41 = bf16[32,224,128]{2,1,0:T(8,128)(2,1)S(1)} all-to-all(bf16[32,224,128]{2,1,0:T(8,128)(2,1)S(1)} %bitcast.22), channel_id=1, replica_groups=mesh['x'=4,'y'=8,'z'=8,'core'=2] {'x','y'}, dimensions={0} | all-to-all | bytes 3670016 | tf_op jit(solution)/shard_map/all_to_all | solution.py:375
  175.7 47.6 %all_to_all.42 = bf16[32,128,128]{2,1,0:T(8,128)(2,1)} all-to-all(bf16[32,128,128]{2,1,0:T(8,128)(2,1)S(1)} %broadcast_in_dim.19), channel_id=1, replica_groups=mesh['x'=4,'y'=8,'z'=8,'core'=2] {'x','y'}, dimensions={0} | all-to-all | bytes 2097152 | tf_op jit(solution)/shard_map/all_to_all | solution.py:375
  223.3 6.7 %solve_two.1 = (f32[4,32,128]{2,1,0:T(8,128)}, bf16[32,2,32,128]{3,2,1,0:T(8,128)(2,1)}) custom-call(bf16[32,4,32,128]{3,2,1,0:T(8,128)(2,1)} %bitcast.33, bf16[16,12,128,256]{3,2,1,0:T(8,128)(2,1)} %bitcast.28), custom_call_target="tpu_custom_call" | custom-call | tf_op jit(solution)/shard_map/solve_two/pallas_call | solution.py:250
  230.0 5.2 %all-to-all-start.4 = ((bf16[32,64,128]{2,1,0:T(8,128)(2,1)}), bf16[32,64,128]{2,1,0:T(8,128)(2,1)S(1)}, u32[]{:S(2)}, u32[]{:S(2)}) async-start(bf16[32,64,128]{2,1,0:T(8,128)(2,1)} %bitcast.36), calls=%async_computation.4 | async-start | bytes 1048576 | tf_op jit(solution)/shard_map/all_to_all | solution.py:375
  235.1 4.7 %root_parts.1.keep_ref = f32[32,32,128]{2,1,0:T(8,128)} custom-call(f32[4,32,128]{2,1,0:T(8,128)} %get-tuple-element.44.s_ref.two_ref, bf16[16,12,128,256]{3,2,1,0:T(8,128)(2,1)} %bitcast.29), custom_call_target="tpu_custom_call" | custom-call | tf_op jit(solution)/shard_map/root_parts/pallas_call | solution.py:288
  239.9 10.6 %all-to-all-done.4 = bf16[32,64,128]{2,1,0:T(8,128)(2,1)S(1)} async-done(((bf16[32,64,128]{2,1,0:T(8,128)(2,1)}), bf16[32,64,128]{2,1,0:T(8,128)(2,1)S(1)}, u32[]{:S(2)}, u32[]{:S(2)}) %all-to-all-start.4) | async-done | bytes 524320 | tf_op jit(solution)/shard_map/all_to_all | solution.py:375
  250.4 0.9 next_residual.2
  251.3 4.8 %all-to-all-start.5 = ((bf16[32,64,128]{2,1,0:T(8,128)(2,1)}), bf16[32,64,128]{2,1,0:T(8,128)(2,1)S(1)}, u32[]{:S(2)}, u32[]{:S(2)}) async-start(bf16[32,64,128]{2,1,0:T(8,128)(2,1)} %bitcast.15), calls=%async_computation.5 | async-start | bytes 1048576 | tf_op jit(solution)/shard_map/all_to_all | solution.py:375
  256.2 14.8 %all-to-all-done.5 = bf16[32,64,128]{2,1,0:T(8,128)(2,1)S(1)} async-done(((bf16[32,64,128]{2,1,0:T(8,128)(2,1)}), bf16[32,64,128]{2,1,0:T(8,128)(2,1)S(1)}, u32[]{:S(2)}, u32[]{:S(2)}) %all-to-all-start.5) | async-done | bytes 524320 | tf_op jit(solution)/shard_map/all_to_all | solution.py:375
  271.0 0.8 copy-done.7
  271.8 4.9 %solve_one.1 = (f32[2,32,128]{2,1,0:T(8,128)}, bf16[32,1,32,128]{3,2,1,0:T(8,128)(2,1)}) custom-call(bf16[32,2,32,128]{3,2,1,0:T(8,128)(2,1)} %bitcast.34, bf16[16,5,128,256]{3,2,1,0:T(8,128)(2,1)} %bitcast.30, f32[32,32,128]{2,1,0:T(8,128)} %root_parts.1.keep_ref), custom_call_target="tpu_custom_call" | custom-call | tf_op jit(solution)/shard_map/solve_one/pallas_call | solution.py:312
  276.7 4.6 %all-to-all-start.6 = ((bf16[32,32,128]{2,1,0:T(8,128)(2,1)}), bf16[32,32,128]{2,1,0:T(8,128)(2,1)S(1)}, u32[]{:S(2)}, u32[]{:S(2)}) async-start(bf16[32,32,128]{2,1,0:T(8,128)(2,1)} %bitcast.38), calls=%async_computation.6 | async-start | bytes 524288 | tf_op jit(solution)/shard_map/all_to_all | solution.py:375
  281.4 11.0 %all-to-all-done.6 = bf16[32,32,128]{2,1,0:T(8,128)(2,1)S(1)} async-done(((bf16[32,32,128]{2,1,0:T(8,128)(2,1)}), bf16[32,32,128]{2,1,0:T(8,128)(2,1)S(1)}, u32[]{:S(2)}, u32[]{:S(2)}) %all-to-all-start.6) | async-done | bytes 262176 | tf_op jit(solution)/shard_map/all_to_all | solution.py:375
  292.5 15.3 %all_to_all.43 = bf16[32,32,128]{2,1,0:T(8,128)(2,1)} all-to-all(bf16[32,32,128]{2,1,0:T(8,128)(2,1)S(1)} %bitcast.27), channel_id=1, replica_groups=mesh['x'=4,'y'=8,'z'=8,'core'=2] {'x','y'}, dimensions={0} | all-to-all | bytes 524288 | tf_op jit(solution)/shard_map/all_to_all | solution.py:375
  307.8 2.5 solve_root.1
  (37 shorter events, 1.8 us)
Async XLA Ops:
  6.5 81.8 %all-gather.7.cloned.1.call-start = ((), (), s32[]{:S(2)}) async-start(), calls=%async_computation.8 | async-start | bytes 8912896 | tf_op jit(solution)/shard_map/all_gather | solution.py:411
  7.5 0.7 collective-permute-start
  11.7 26.2 %copy-start.8 = (s32[14,16,3]{1,0,2:T(8,128)S(1)}, s32[14,16,3]{1,0,2:T(8,128)}, u32[]{:S(2)}) copy-start(s32[14,16,3]{1,0,2:T(8,128)} %param.7) | copy-start | bytes 8068
  11.7 26.7 %copy-start = (bf16[14,3,256,128]{3,2,1,0:T(8,128)(2,1)S(1)}, bf16[14,3,256,128]{3,2,1,0:T(8,128)(2,1)}, u32[]{:S(2)}) copy-start(bf16[14,3,256,128]{3,2,1,0:T(8,128)(2,1)} %p_ref.3) | copy-start | bytes 8257540
  11.7 75.5 %all-to-all-start = ((bf16[32,128,256]{2,1,0:T(8,128)(2,1)}), bf16[32,128,256]{2,1,0:T(8,128)(2,1)}, u32[]{:S(2)}, u32[]{:S(2)}) async-start(bf16[32,128,256]{2,1,0:T(8,128)(2,1)} %broadcast_in_dim.17), calls=%async_computation | async-start | bytes 4194304 | tf_op jit(solution)/shard_map/all_to_all | solution.py:375
  37.9 185.4 %all-gather.9.cloned.1.call-start = ((), (), s32[]{:S(2)}) async-start(), calls=%async_computation.9 | async-start | bytes 13369344 | tf_op jit(solution)/shard_map/all_gather | solution.py:428
  38.4 3.0 copy-start.6
  38.4 5.4 %copy-start.3 = (bf16[15,128,256]{2,1,0:T(8,128)(2,1)S(1)}, bf16[15,128,256]{2,1,0:T(8,128)(2,1)}, u32[]{:S(2)}) copy-start(bf16[15,128,256]{2,1,0:T(8,128)(2,1)} %d_ref) | copy-start | bytes 2949124
  39.4 6.2 %copy-start.1 = (bf16[12,256,256]{2,1,0:T(8,128)(2,1)}, bf16[12,256,256]{2,1,0:T(8,128)(2,1)S(1)}, u32[]{:S(2)}) copy-start(bf16[12,256,256]{2,1,0:T(8,128)(2,1)S(1)} %select_leaves.1.a_ref) | copy-start | bytes 4718596
  39.4 6.2 %collective-permute-start.1 = (bf16[12,256,256]{2,1,0:T(8,128)(2,1)S(1)}, bf16[12,256,256]{2,1,0:T(8,128)(2,1)S(1)}, u32[]{:S(2)}, u32[]{:S(2)}) collective-permute-start(bf16[12,256,256]{2,1,0:T(8,128)(2,1)S(1)} %select_leaves.1.a_ref), channel_id=1, source_target_pairs={{0,1},{1,0},{2,3},{3,2},{4,5},{5,4},{6,7},{7,6},{8,9},{9,8},{10,11... | collective-permute-start | bytes 4718600 | tf_op jit(solution)/shard_map/ppermute | solution.py:399
  41.4 4.2 %collective-permute-start.2 = (f32[7,16,256]{2,1,0:T(8,128)S(1)}, f32[7,16,256]{2,1,0:T(8,128)S(1)}, u32[]{:S(2)}, u32[]{:S(2)}) collective-permute-start(f32[7,16,256]{2,1,0:T(8,128)S(1)} %slice.20), channel_id=1, source_target_pairs={{0,1},{1,0},{2,3},{3,2},{4,5},{5,4},{6,7},{7,6},{8,9},{9,8},{10,11... | collective-permute-start | bytes 344072 | tf_op jit(solution)/shard_map/ppermute | solution.py:399
  45.6 1.1 copy-start.4
  93.6 24.9 %copy-start.2 = (bf16[12,256,256]{2,1,0:T(8,128)(2,1)S(1)}, bf16[12,256,256]{2,1,0:T(8,128)(2,1)}, u32[]{:S(2)}) copy-start(bf16[12,256,256]{2,1,0:T(8,128)(2,1)} %copy-done.1) | copy-start | bytes 4718596
  117.8 138.4 %all-gather.11.cloned.1.call-start = ((), (), s32[]{:S(2)}) async-start(), calls=%async_computation.10 | async-start | bytes 5570560 | tf_op jit(solution)/shard_map/all_gather | solution.py:429
  118.5 1.4 copy-start.5
  174.8 0.7 collective-permute-start.3
  230.0 20.5 %all-to-all-start.4 = ((bf16[32,64,128]{2,1,0:T(8,128)(2,1)}), bf16[32,64,128]{2,1,0:T(8,128)(2,1)S(1)}, u32[]{:S(2)}, u32[]{:S(2)}) async-start(bf16[32,64,128]{2,1,0:T(8,128)(2,1)} %bitcast.36), calls=%async_computation.4 | async-start | bytes 1048576 | tf_op jit(solution)/shard_map/all_to_all | solution.py:375
  251.3 19.7 %all-to-all-start.5 = ((bf16[32,64,128]{2,1,0:T(8,128)(2,1)}), bf16[32,64,128]{2,1,0:T(8,128)(2,1)S(1)}, u32[]{:S(2)}, u32[]{:S(2)}) async-start(bf16[32,64,128]{2,1,0:T(8,128)(2,1)} %bitcast.15), calls=%async_computation.5 | async-start | bytes 1048576 | tf_op jit(solution)/shard_map/all_to_all | solution.py:375
  271.0 0.8 copy-start.7
  276.7 15.7 %all-to-all-start.6 = ((bf16[32,32,128]{2,1,0:T(8,128)(2,1)}), bf16[32,32,128]{2,1,0:T(8,128)(2,1)S(1)}, u32[]{:S(2)}, u32[]{:S(2)}) async-start(bf16[32,32,128]{2,1,0:T(8,128)(2,1)} %bitcast.38), calls=%async_computation.6 | async-start | bytes 524288 | tf_op jit(solution)/shard_map/all_to_all | solution.py:375
Sparse Core Ops, SparseCore 0:
  10.2 78.0 all-gather.6
  117.9 76.5 all-gather.8
  196.6 44.5 all-gather.10
